TPU v7x, 32 devices: a whole 2x2x4 slice. The times are simulated.
32 devices in a mesh: tm: 2 (over y), pts: 16 (over z, x, core).
Axes of the slice: x: 2, y: 2, z: 4, core: 2. Of those that a mesh axis runs over, the one named last changes fastest.
Arguments:
- precip: float32 [512, 16384], P('tm', 'pts'), may hold values from -150 to 300, as said below
- thresholds: float32 [64], replicated, may hold values from -1 to 5
- bin_index: int32 [16384], P('pts'), may hold values from 0 to 63
- test_matrix: float32 [512, 256], P('tm'), may hold values from -0.25 to 0.25
Outputs:
- basis: float32 [16384, 256], P(('pts', 'tm'))
- factor: float32 [256, 256], replicated
Inputs may be any that keep to these rules, and one draw needn't show every extreme that they name: `precip`: precipitation records.
All inputs are finite; a program needn't handle non-finite values.
Results may differ from a plain program's by a relative error of at most 0.0003.
Values sent between devices are 32-bit elements; how exact they have to be, the bound alone decides.
No kernel may reach another device: no remote copies, remote signals or barrier semaphores. Data moves between devices by JAX's collectives and lax.ppermute only.
A program may use at most 64 MiB of HBM per device.

v0:
```python
import functools
import math

import jax
import jax.numpy as jnp
import numpy as np
from jax import lax
from jax.experimental import pallas as pl
from jax.experimental.pallas import tpu as pltpu
from jax.sharding import PartitionSpec as P


HARM = 8
SUB = 8
AXES = ("tm", "pts")
HI = lax.Precision.HIGHEST

year_days = 365.25


def harmonic_filter(days_total):
    phase_base = np.arange(days_total).astype(np.float32)
    columns = [np.ones_like(phase_base)]
    for order in range(1, HARM + 1):
        phase = np.float32(2.0 * math.pi * order / year_days) * phase_base
        columns.append(np.cos(phase.astype(np.float64)))
        columns.append(np.sin(phase.astype(np.float64)))
    table = np.stack(columns, 0).astype(np.float32).astype(np.float64)
    low = np.linalg.cholesky(table @ table.T)
    rows = np.linalg.solve(low, table)
    padded = -(-rows.shape[0] // SUB) * SUB
    rows = np.concatenate([rows, np.zeros((padded - rows.shape[0], days_total))], 0)
    return rows.astype(np.float32)


def nn(a, b):
    return jnp.dot(a, b, precision=HI, preferred_element_type=jnp.float32)


def nt(a, b):
    return lax.dot_general(
        a, b, (((1,), (1,)), ((), ())), precision=HI, preferred_element_type=jnp.float32
    )


def tn(a, b):
    return lax.dot_general(
        a, b, (((0,), (0,)), ((), ())), precision=HI, preferred_element_type=jnp.float32
    )


def swap(value, bit, odd_bit=None):
    total = lax.axis_size("tm") * lax.axis_size("pts")
    odd_bit = bit if odd_bit is None else odd_bit
    return lax.ppermute(
        value, AXES, [(i, i ^ (odd_bit if i % 2 else bit)) for i in range(total)]
    )


def cut_kernel(widths, own_rows, tm_count, days_ref, *refs):
    piece_refs, sem = refs[:-1], refs[-1]
    place = lax.axis_index("tm")
    copies = []
    start = 0
    for width in widths:
        for k in range(1, tm_count):
            at = pl.multiple_of((place ^ k) * own_rows + start, math.gcd(own_rows, start))
            n = len(copies)
            copies.append(
                pltpu.make_async_copy(days_ref.at[:, pl.ds(at, width)], piece_refs[n], sem.at[n])
            )
        start += width
    for copy in copies:
        copy.start()
    for copy in copies:
        copy.wait()


def front_kernel(start, width, own_rows, tm_count, earlier, with_acc, with_cross, last, *refs):
    refs = list(refs)
    take = lambda n: [refs.pop(0) for _ in range(n)]
    days_ref, thr_ref, bin_ref, filt_ref, test_ref = take(5)
    recv_refs = take(tm_count - 1)
    half_refs = take(2 * (tm_count - 1))
    earlier_refs = take(earlier)
    acc_refs = take(1 if with_acc else 0)
    sketch_ref = take(1)[0]
    outs = take(2 if last else int(with_cross))
    table_ref = take(1)[0]
    days_local = days_ref.shape[0]
    place = lax.axis_index("tm")
    low = lax.axis_index("pts") % 2
    at = pl.multiple_of(place * own_rows + start, math.gcd(own_rows, start))
    table_ref[:days_local, :] = test_ref[...]
    half = days_local // 2
    for k in range(tm_count - 1):
        base = days_local * (k + 1)
        table_ref[pl.ds(pl.multiple_of(base + low * half, half), half), :] = half_refs[2 * k][...]
        table_ref[pl.ds(pl.multiple_of(base + (1 - low) * half, half), half), :] = half_refs[2 * k + 1][...]
    bins = bin_ref[:, pl.ds(at, width)]
    count = thr_ref.shape[0]
    entry = lax.broadcasted_iota(jnp.int32, (count, width), 0)
    level = jnp.sum(jnp.where(entry == bins, thr_ref[...], 0.0), axis=0, keepdims=True)
    series = [days_ref[:, pl.ds(at, width)]] + [r[...] for r in recv_refs]
    proj = nn(filt_ref[place], series[0])
    for k in range(1, tm_count):
        proj = proj + nn(filt_ref[place ^ k], series[k])
    excess = [
        jnp.maximum(series[k] - tn(filt_ref[place ^ k], proj) - level, 0.0)
        for k in range(tm_count)
    ]
    sketch = tn(jnp.concatenate(excess, 0), table_ref[...])
    sketch_ref[...] = sketch
    if not with_cross:
        return
    whole = jnp.concatenate([r[...] for r in earlier_refs] + [sketch], 0)
    cross = tn(whole, whole)
    for ref in acc_refs:
        cross = cross + ref[...]
    if not last:
        outs[0][...] = cross
        return
    kept_ref, sent_ref = outs
    tile = cross.shape[0] // 2
    row = lax.broadcasted_iota(jnp.int32, (tile, tile), 0)
    col = lax.broadcasted_iota(jnp.int32, (tile, tile), 1)
    second = cross[tile:, tile:]
    ends = jnp.where(row >= col, cross[:tile, :tile], second)
    side = cross[tile:, :tile]
    diag = jnp.broadcast_to(
        jnp.sum(jnp.where(row == col, second, 0.0), axis=0, keepdims=True), (SUB, tile)
    )
    kept_ref[:tile, :] = jnp.where(low == 0, ends, side)
    sent_ref[:tile, :] = jnp.where(low == 0, side, ends)
    kept_ref[tile:, :] = diag
    sent_ref[tile:, :] = diag


def over_lanes(value, col, tile):
    return jnp.broadcast_to(value[:, col:col + 1], (SUB, tile))


def over_rows(value, row, tile):
    return jnp.broadcast_to(value[row:row + 1, :], (SUB, tile))


def panel(blocks):
    count = len(blocks)
    blocks = list(blocks)
    tile = count * SUB
    lane = lax.broadcasted_iota(jnp.int32, (SUB, tile), 1)
    row = lax.broadcasted_iota(jnp.int32, (SUB, tile), 0)
    upper, inverse = [], []
    for i in range(count):
        first = SUB * i
        own = blocks[i]
        cols = [over_lanes(own, first + k, tile) for k in range(SUB)]
        e = {(j, k): over_rows(cols[k], j, tile) for k in range(SUB) for j in range(k + 1)}
        inside = (lane >= first) & (lane < first + SUB)
        later = {
            t: [over_lanes(blocks[t], first + k, tile) for k in range(SUB)]
            for t in range(i + 1, count)
        }
        rows = [
            jnp.where(inside, jnp.where(lane == first + j, 1.0, 0.0), over_rows(own, j, tile))
            for j in range(SUB)
        ]
        for j in range(SUB):
            s = lax.rsqrt(e[j, j])
            fac = {k: e[j, k] * s for k in range(j + 1, SUB)}
            e[j, j] = e[j, j] * s
            rows[j] = rows[j] * s
            for t in later:
                later[t][j] = later[t][j] * s
            for k in range(j + 1, SUB):
                e[j, k] = fac[k]
                for m in range(k, SUB):
                    e[k, m] = e[k, m] - fac[k] * fac[m]
                rows[k] = rows[k] - fac[k] * rows[j]
                for t in later:
                    later[t][k] = later[t][k] - fac[k] * later[t][j]
        for t in later:
            terms = [later[t][j] * rows[j] for j in range(SUB)]
            while len(terms) > 1:
                terms = [terms[q] + terms[q + 1] for q in range(0, len(terms), 2)]
            blocks[t] = jnp.where(inside, 0.0, blocks[t]) - terms[0]
        up = jnp.zeros((SUB, tile), jnp.float32)
        inv = up
        for j in range(SUB):
            line = jnp.where(lane >= first + SUB, rows[j], 0.0)
            for k in range(j, SUB):
                line = jnp.where(lane == first + k, e[j, k], line)
            up = jnp.where(row == j, line, up)
            inv = jnp.where(row == j, rows[j], inv)
        upper.append(up)
        inverse.append(jnp.where(lane < first + SUB, inv, 0.0))
    return jnp.concatenate(upper, 0), jnp.concatenate(inverse, 0)


def back_kernel(points_total, chunks, part_ref, other_ref, *refs):
    sketch_refs = refs[:chunks]
    basis_ref, factor_ref = refs[chunks:]
    tile = part_ref.shape[1]
    low = lax.axis_index("pts") % 2
    part = part_ref[...] / points_total
    other = other_ref[...] / points_total
    ends = jnp.where(low == 0, part[:tile], other[:tile])
    side = jnp.where(low == 0, other[:tile], part[:tile])
    diag = jnp.where(low == 0, other[tile:tile + 1], part[tile:tile + 1])
    row = lax.broadcasted_iota(jnp.int32, (tile, tile), 0)
    col = lax.broadcasted_iota(jnp.int32, (tile, tile), 1)
    ends_t = ends.T
    side_t = side.T
    split = lambda a: [a[SUB * t:SUB * (t + 1), :] for t in range(tile // SUB)]
    up, inv1 = panel(split(jnp.where(row >= col, ends, ends_t)))
    factor_ref[:tile, :tile] = up
    factor_ref[tile:, :tile] = jnp.zeros((tile, tile), jnp.float32)
    right = nn(inv1, side_t)
    right_t = nt(side, inv1)
    factor_ref[:tile, tile:] = right
    rest = jnp.where(row < col, ends, jnp.where(row == col, diag, ends_t)) - nn(right_t, right)
    up, inv2 = panel(split(rest))
    factor_ref[tile:, tile:] = up
    at = 0
    for ref in sketch_refs:
        size = ref.shape[0]
        left = nt(ref[:, :tile], inv1)
        basis_ref[at:at + size, :tile] = left
        basis_ref[at:at + size, tile:] = nt(ref[:, tile:] - nn(left, right), inv2)
        at += size


def chunk_widths(own_rows):
    step = own_rows // 4
    if step % 128:
        return [own_rows]
    return [2 * step, step, step]


def on_device(precip, thresholds, bin_index, test_matrix):
    tm_count = lax.axis_size("tm")
    pts_count = lax.axis_size("pts")
    low = lax.axis_index("pts") % 2
    days_local, points_local = precip.shape
    columns = test_matrix.shape[1]
    tile = columns // 2
    own_rows = points_local // tm_count
    days_total = days_local * tm_count
    points_total = points_local * pts_count
    f32 = jnp.float32

    rows = harmonic_filter(days_total)
    filt = rows.reshape(rows.shape[0], tm_count, days_local).transpose(1, 0, 2)
    filt = jnp.asarray(filt)
    thr = thresholds[:, None]
    bins = bin_index[None, :]

    vmem = pl.BlockSpec(memory_space=pltpu.VMEM)
    widths = chunk_widths(own_rows)
    half = days_local // 2
    mine = lax.dynamic_slice_in_dim(test_matrix, low * half, half, 0)
    shapes = [
        jax.ShapeDtypeStruct((days_local, width), f32)
        for width in widths
        for _ in range(tm_count - 1)
    ]
    pieces = pl.pallas_call(
        functools.partial(cut_kernel, widths, own_rows, tm_count),
        out_shape=shapes,
        in_specs=[pl.BlockSpec(memory_space=pl.ANY)],
        out_specs=[vmem] * len(shapes),
        scratch_shapes=[pltpu.SemaphoreType.DMA((len(shapes),))],
        compiler_params=pltpu.CompilerParams(vmem_limit_bytes=4 << 20),
        name="cut",
    )(precip)
    sends = [("rows", mine, k) for k in range(1, tm_count)]
    for n in range(len(widths)):
        sends += [("points", pieces[n * (tm_count - 1) + k - 1], k) for k in range(1, tm_count)]
    came = []
    for _, value, k in sends:
        came.append(swap(value, k * pts_count))
    halves, came = came[:tm_count - 1], came[tm_count - 1:]
    received = [came[n * (tm_count - 1):(n + 1) * (tm_count - 1)] for n in range(len(widths))]
    halves = [h for got in halves for h in (got, swap(got, 1))]

    sketches, waiting = [], []
    cross = None
    start = 0
    for index, width in enumerate(widths):
        last = index == len(widths) - 1
        with_cross = last or index == 0
        if sketches:
            received[index], sketches[-1] = lax.optimization_barrier((received[index], sketches[-1]))
        operands = [precip, thr, bins, filt, test_matrix] + received[index] + halves
        operands += waiting if with_cross else []
        operands += [cross] if with_cross and cross is not None else []
        shapes = [jax.ShapeDtypeStruct((width, columns), f32)]
        if last:
            shapes += [jax.ShapeDtypeStruct((tile + SUB, tile), f32)] * 2
        elif with_cross:
            shapes += [jax.ShapeDtypeStruct((columns, columns), f32)]
        out = pl.pallas_call(
            functools.partial(
                front_kernel,
                start,
                width,
                own_rows,
                tm_count,
                len(waiting) if with_cross else 0,
                with_cross and cross is not None,
                with_cross,
                last,
            ),
            out_shape=shapes,
            in_specs=[vmem] * len(operands),
            out_specs=[vmem] * len(shapes),
            scratch_shapes=[pltpu.VMEM((days_total, columns), f32)],
            cost_estimate=pl.CostEstimate(
                flops=12 * width * columns * (days_total + columns),
                bytes_accessed=4 * days_total * (width + columns),
                transcendentals=0,
            ),
            compiler_params=pltpu.CompilerParams(vmem_limit_bytes=16 << 20),
        )(*operands)
        sketches.append(out[0])
        if with_cross:
            waiting = []
            cross = out[1]
        else:
            waiting.append(out[0])
        start += width
    kept, sent = out[1], out[2]

    part = kept + swap(sent, 1)
    bits = [1 << n for n in range(1, (tm_count * pts_count).bit_length() - 1)]
    shift = (len(bits) + 1) // 2
    for n in range(len(bits)):
        part = part + swap(part, bits[n], bits[(n + shift) % len(bits)])
    other = swap(part, 1)

    basis, factor = pl.pallas_call(
        functools.partial(back_kernel, points_total, len(sketches)),
        out_shape=(
            jax.ShapeDtypeStruct((own_rows, columns), f32),
            jax.ShapeDtypeStruct((columns, columns), f32),
        ),
        in_specs=[vmem] * (2 + len(sketches)),
        out_specs=(vmem, vmem),
        compiler_params=pltpu.CompilerParams(vmem_limit_bytes=16 << 20),
        name="back",
    )(part, other, *sketches)
    return basis, factor


def solution(mesh):
    in_specs = (P("tm", "pts"), P(), P("pts"), P("tm", None))
    out_specs = (P(("pts", "tm"), None), P())

    return jax.shard_map(
        on_device, mesh=mesh, in_specs=in_specs, out_specs=out_specs, check_vma=False
    )
```

profile of v0, /device:TPU:0, one launch (start us, length us, event | category | flops | bytes accessed | tf_op | source)
XLA Modules:
  0.0 54.6 jit_solution(4672160074489815184)
XLA Ops:
  0.6 0.0 copy-start.2
  0.7 1.0 %constant_dynamic-slice_fusion = f32[128,256]{1,0:T(8,128)S(1)} fusion(f32[256,256]{1,0:T(8,128)} %refs_4_.5, s32[]{:T(128)S(6)} %select_n.11), kind=kLoop, calls=%fused_computation | loop fusion | bytes 262148 | tf_op jit(solution)/shard_map/dynamic_slice | solution.py:261
  1.6 3.1 %collective-permute-start.3 = (f32[128,256]{1,0:T(8,128)S(1)}, f32[128,256]{1,0:T(8,128)S(1)}, u32[]{:S(2)}, u32[]{:S(2)}) collective-permute-start(f32[128,256]{1,0:T(8,128)S(1)} %constant_dynamic-slice_fusion), channel_id=1, source_target_pairs={{0,16},{1,17},{2,18},{3,19},{4,20},{5,21},{6,22},{7,23},{8,24},{9,... | collective-permute-start | bytes 393224 | tf_op jit(solution)/shard_map/ppermute | solution.py:55
  4.7 0.0 copy-start
  4.7 1.2 %copy-done = f32[256,1024]{1,0:T(8,128)S(1)} copy-done((f32[256,1024]{1,0:T(8,128)S(1)}, f32[256,1024]{1,0:T(8,128)}, u32[]{:S(2)}) %copy-start) | copy-done | bytes 1048600
  5.9 0.0 copy-start.1
  5.9 0.1 cut.1
  6.0 0.1 collective-permute-start.2
  6.1 2.5 %collective-permute-done.3.refs_6_ = f32[128,256]{1,0:T(8,128)S(1)} collective-permute-done((f32[128,256]{1,0:T(8,128)S(1)}, f32[128,256]{1,0:T(8,128)S(1)}, u32[]{:S(2)}, u32[]{:S(2)}) %collective-permute-start.3) | collective-permute-done | bytes 131104 | tf_op jit(solution)/shard_map/ppermute | solution.py:55
  8.6 0.0 collective-permute-start.4
  8.6 2.5 %collective-permute-start.1 = (f32[256,128]{1,0:T(8,128)S(1)}, f32[256,128]{1,0:T(8,128)S(1)}, u32[]{:S(2)}, u32[]{:S(2)}) collective-permute-start(f32[256,128]{1,0:T(8,128)S(1)} %get-tuple-element.15), channel_id=1, source_target_pairs={{0,16},{1,17},{2,18},{3,19},{4,20},{5,21},{6,22},{7,23},{8,24},{9,... | collective-permute-start | bytes 393224 | tf_op jit(solution)/shard_map/ppermute | solution.py:55
  11.1 0.0 copy-start.5
  11.1 0.1 collective-permute-start
  11.1 0.6 %copy-done.5 = f32[64]{0:T(128)S(1)} copy-done((f32[64]{0:T(128)S(1)}, f32[64]{0:T(128)}, u32[]{:S(2)}) %copy-start.5) | copy-done | bytes 280
  11.7 0.0 copy-start.4
  11.7 0.1 copy.9.refs_1_
  11.8 0.0 collective-permute-done.4.refs_7_
  11.8 3.4 %collective-permute-done.2.refs_5_ = f32[256,256]{1,0:T(8,128)S(1)} collective-permute-done((f32[256,256]{1,0:T(8,128)S(1)}, f32[256,256]{1,0:T(8,128)S(1)}, u32[]{:S(2)}, u32[]{:S(2)}) %collective-permute-start.2) | collective-permute-done | bytes 262176 | tf_op jit(solution)/shard_map/ppermute | solution.py:55
  15.3 0.0 copy-done.2
  15.3 0.0 copy-done.1
  15.3 0.0 copy-done.4
  15.3 0.0 copy-start.3
  15.3 0.8 %copy-done.3 = f32[2,24,256]{2,1,0:T(8,128)S(1)} copy-done((f32[2,24,256]{2,1,0:T(8,128)S(1)}, f32[2,24,256]{2,1,0:T(8,128)}, u32[]{:S(2)}) %copy-start.3) | copy-done | bytes 49176
  16.1 2.7 %shard_map.68 = (f32[256,256]{1,0:T(8,128)S(1)}, f32[256,256]{1,0:T(8,128)S(1)}) custom-call(f32[256,1024]{1,0:T(8,128)S(1)} %copy-done.1, f32[64,1]{1,0:T(8,128)S(1)} %copy.9.refs_1_, s32[1,1024]{1,0:T(1,128)S(1)} %bitcast.2, f32[2,24,256]{2,1,0:T(8,128)S(1)} %copy-done.3, f32[256,256]{1,0:T(8,128)S(1)} %copy-done.2, ...), custom_call_target="tpu_custom_call" | custom-call | flops 603979776 | bytes 1048576 | tf_op jit(solution)/shard_map/pallas_call | solution.py:302
  18.7 0.0 collective-permute-done.1.refs_5_
  18.7 1.2 %shard_map.69.refs_8_.refs_1_ = f32[128,256]{1,0:T(8,128)S(1)} custom-call(f32[256,1024]{1,0:T(8,128)S(1)} %copy-done.1, f32[64,1]{1,0:T(8,128)S(1)} %copy.9.refs_1_, s32[1,1024]{1,0:T(1,128)S(1)} %bitcast.3, f32[2,24,256]{2,1,0:T(8,128)S(1)} %copy-done.3, f32[256,256]{1,0:T(8,128)S(1)} %copy-done.2, f32[256,128]{1,0:T(8,128)S(1)} %collective-permute-done.1.refs_5_, ...), custom_call_target="tpu_custom_call" | custom-call | flops 301989888 | bytes 786432 | tf_op jit(solution)/shard_map/pallas_call | solution.py:302
  19.9 0.0 collective-permute-done.refs_5_
  19.9 1.8 %shard_map.70 = (f32[128,256]{1,0:T(8,128)S(1)}, f32[136,128]{1,0:T(8,128)S(1)}, f32[136,128]{1,0:T(8,128)S(1)}) custom-call(f32[256,1024]{1,0:T(8,128)S(1)} %copy-done.1, f32[64,1]{1,0:T(8,128)S(1)} %copy.9.refs_1_, s32[1,1024]{1,0:T(1,128)S(1)} %bitcast.4, f32[2,24,256]{2,1,0:T(8,128)S(1)} %copy-done.3, f32[256,256]{1,0:T(8,128)S(1)} %copy-done.2, ...), custom_call_target="tpu_custom_call" | custom-call | flops 301989888 | bytes 786432 | tf_op jit(solution)/shard_map/pallas_call | solution.py:302
  21.7 0.1 collective-permute-start.5
  21.8 1.2 %collective-permute-done.5 = f32[136,128]{1,0:T(8,128)S(1)} collective-permute-done((f32[136,128]{1,0:T(8,128)S(1)}, f32[136,128]{1,0:T(8,128)S(1)}, u32[]{:S(2)}, u32[]{:S(2)}) %collective-permute-start.5) | collective-permute-done | bytes 69664 | tf_op jit(solution)/shard_map/ppermute | solution.py:55
  23.0 1.6 %collective-permute-start.6 = (f32[136,128]{1,0:T(8,128)S(1)}, f32[136,128]{1,0:T(8,128)S(1)}, u32[]{:S(2)}, u32[]{:S(2)}) collective-permute-start(f32[136,128]{1,0:T(8,128)S(1)} %add.24), channel_id=1, source_target_pairs={{0,2},{1,9},{2,0},{3,11},{4,6},{5,13},{6,4},{7,15},{8,10},{9,1},{1... | collective-permute-start | bytes 208904 | tf_op jit(solution)/shard_map/ppermute | solution.py:55
  24.6 2.8 %collective-permute-done.6 = f32[136,128]{1,0:T(8,128)S(1)} collective-permute-done((f32[136,128]{1,0:T(8,128)S(1)}, f32[136,128]{1,0:T(8,128)S(1)}, u32[]{:S(2)}, u32[]{:S(2)}) %collective-permute-start.6) | collective-permute-done | bytes 69664 | tf_op jit(solution)/shard_map/ppermute | solution.py:55
  27.4 1.6 %collective-permute-start.7 = (f32[136,128]{1,0:T(8,128)S(1)}, f32[136,128]{1,0:T(8,128)S(1)}, u32[]{:S(2)}, u32[]{:S(2)}) collective-permute-start(f32[136,128]{1,0:T(8,128)S(1)} %add.25), channel_id=1, source_target_pairs={{0,4},{1,17},{2,6},{3,19},{4,0},{5,21},{6,2},{7,23},{8,12},{9,25},... | collective-permute-start | bytes 208904 | tf_op jit(solution)/shard_map/ppermute | solution.py:55
  29.1 2.7 %collective-permute-done.7 = f32[136,128]{1,0:T(8,128)S(1)} collective-permute-done((f32[136,128]{1,0:T(8,128)S(1)}, f32[136,128]{1,0:T(8,128)S(1)}, u32[]{:S(2)}, u32[]{:S(2)}) %collective-permute-start.7) | collective-permute-done | bytes 69664 | tf_op jit(solution)/shard_map/ppermute | solution.py:55
  31.8 2.7 %collective-permute-start.8 = (f32[136,128]{1,0:T(8,128)S(1)}, f32[136,128]{1,0:T(8,128)S(1)}, u32[]{:S(2)}, u32[]{:S(2)}) collective-permute-start(f32[136,128]{1,0:T(8,128)S(1)} %add.26), channel_id=1, source_target_pairs={{0,8},{1,3},{2,10},{3,1},{4,12},{5,7},{6,14},{7,5},{8,0},{9,11},{1... | collective-permute-start | bytes 208904 | tf_op jit(solution)/shard_map/ppermute | solution.py:55
  34.5 2.7 %collective-permute-done.8 = f32[136,128]{1,0:T(8,128)S(1)} collective-permute-done((f32[136,128]{1,0:T(8,128)S(1)}, f32[136,128]{1,0:T(8,128)S(1)}, u32[]{:S(2)}, u32[]{:S(2)}) %collective-permute-start.8) | collective-permute-done | bytes 69664 | tf_op jit(solution)/shard_map/ppermute | solution.py:55
  37.2 1.5 %collective-permute-start.9 = (f32[136,128]{1,0:T(8,128)S(1)}, f32[136,128]{1,0:T(8,128)S(1)}, u32[]{:S(2)}, u32[]{:S(2)}) collective-permute-start(f32[136,128]{1,0:T(8,128)S(1)} %add.27), channel_id=1, source_target_pairs={{0,16},{1,5},{2,18},{3,7},{4,20},{5,1},{6,22},{7,3},{8,24},{9,13},... | collective-permute-start | bytes 208904 | tf_op jit(solution)/shard_map/ppermute | solution.py:55
  38.7 2.9 %collective-permute-done.9 = f32[136,128]{1,0:T(8,128)S(1)} collective-permute-done((f32[136,128]{1,0:T(8,128)S(1)}, f32[136,128]{1,0:T(8,128)S(1)}, u32[]{:S(2)}, u32[]{:S(2)}) %collective-permute-start.9) | collective-permute-done | bytes 69664 | tf_op jit(solution)/shard_map/ppermute | solution.py:55
  41.6 0.1 collective-permute-start.10
  41.6 1.2 %collective-permute-done.10.other_ref = f32[136,128]{1,0:T(8,128)S(1)} collective-permute-done((f32[136,128]{1,0:T(8,128)S(1)}, f32[136,128]{1,0:T(8,128)S(1)}, u32[]{:S(2)}, u32[]{:S(2)}) %collective-permute-start.10) | collective-permute-done | bytes 69664 | tf_op jit(solution)/shard_map/ppermute | solution.py:55
  42.9 11.7 %back.1 = (f32[512,256]{1,0:T(8,128)}, f32[256,256]{1,0:T(8,128)}) custom-call(f32[136,128]{1,0:T(8,128)S(1)} %add.28.part_ref, f32[136,128]{1,0:T(8,128)S(1)} %collective-permute-done.10.other_ref, f32[256,256]{1,0:T(8,128)S(1)} %get-tuple-element.23.refs_0_, f32[128,256]{1,0:T(8,128)S(1)} %shard_map.69.refs_8_.refs_1_, ...), custom_call_target="tpu_custom_call" | custom-call | tf_op jit(solution)/shard_map/back/pallas_call | solution.py:341
  (5 shorter events, 0.1 us)
Async XLA Ops:
  0.6 14.6 %copy-start.2 = (f32[256,256]{1,0:T(8,128)S(1)}, f32[256,256]{1,0:T(8,128)}, u32[]{:S(2)}) copy-start(f32[256,256]{1,0:T(8,128)} %refs_4_.5) | copy-start | bytes 786436
  1.6 6.9 %collective-permute-start.3 = (f32[128,256]{1,0:T(8,128)S(1)}, f32[128,256]{1,0:T(8,128)S(1)}, u32[]{:S(2)}, u32[]{:S(2)}) collective-permute-start(f32[128,256]{1,0:T(8,128)S(1)} %constant_dynamic-slice_fusion), channel_id=1, source_target_pairs={{0,16},{1,17},{2,18},{3,19},{4,20},{5,21},{6,22},{7,23},{8,24},{9,... | collective-permute-start | bytes 393224 | tf_op jit(solution)/shard_map/ppermute | solution.py:55
  4.7 1.2 %copy-start = (f32[256,1024]{1,0:T(8,128)S(1)}, f32[256,1024]{1,0:T(8,128)}, u32[]{:S(2)}) copy-start(f32[256,1024]{1,0:T(8,128)} %refs_0_.5) | copy-start | bytes 3145732
  5.9 9.3 %copy-start.1 = (f32[256,1024]{1,0:T(8,128)S(1)}, f32[256,1024]{1,0:T(8,128)}, u32[]{:S(2)}) copy-start(f32[256,1024]{1,0:T(8,128)} %refs_0_.5) | copy-start | bytes 3145732
  6.0 9.2 %collective-permute-start.2 = (f32[256,256]{1,0:T(8,128)S(1)}, f32[256,256]{1,0:T(8,128)S(1)}, u32[]{:S(2)}, u32[]{:S(2)}) collective-permute-start(f32[256,256]{1,0:T(8,128)S(1)} %get-tuple-element.16), channel_id=1, source_target_pairs={{0,16},{1,17},{2,18},{3,19},{4,20},{5,21},{6,22},{7,23},{8,24},{9,... | collective-permute-start | bytes 786440 | tf_op jit(solution)/shard_map/ppermute | solution.py:55
  8.6 3.2 %collective-permute-start.4 = (f32[128,256]{1,0:T(8,128)S(1)}, f32[128,256]{1,0:T(8,128)S(1)}, u32[]{:S(2)}, u32[]{:S(2)}) collective-permute-start(f32[128,256]{1,0:T(8,128)S(1)} %collective-permute-done.3.refs_6_), channel_id=1, source_target_pairs={{0,1},{1,0},{2,3},{3,2},{4,5},{5,4},{6,7},{7,6},{8,9},{9,8},{10,11... | collective-permute-start | bytes 393224 | tf_op jit(solution)/shard_map/ppermute | solution.py:55
  8.6 10.2 %collective-permute-start.1 = (f32[256,128]{1,0:T(8,128)S(1)}, f32[256,128]{1,0:T(8,128)S(1)}, u32[]{:S(2)}, u32[]{:S(2)}) collective-permute-start(f32[256,128]{1,0:T(8,128)S(1)} %get-tuple-element.15), channel_id=1, source_target_pairs={{0,16},{1,17},{2,18},{3,19},{4,20},{5,21},{6,22},{7,23},{8,24},{9,... | collective-permute-start | bytes 393224 | tf_op jit(solution)/shard_map/ppermute | solution.py:55
  11.1 0.7 %copy-start.5 = (f32[64]{0:T(128)S(1)}, f32[64]{0:T(128)}, u32[]{:S(2)}) copy-start(f32[64]{0:T(128)} %param.6) | copy-start | bytes 772
  11.1 8.9 %collective-permute-start = (f32[256,128]{1,0:T(8,128)S(1)}, f32[256,128]{1,0:T(8,128)S(1)}, u32[]{:S(2)}, u32[]{:S(2)}) collective-permute-start(f32[256,128]{1,0:T(8,128)S(1)} %get-tuple-element.14), channel_id=1, source_target_pairs={{0,16},{1,17},{2,18},{3,19},{4,20},{5,21},{6,22},{7,23},{8,24},{9,... | collective-permute-start | bytes 393224 | tf_op jit(solution)/shard_map/ppermute | solution.py:55
  11.7 3.5 %copy-start.4 = (s32[1024]{0:T(1024)S(1)}, s32[1024]{0:T(1024)}, u32[]{:S(2)}) copy-start(s32[1024]{0:T(1024)} %param.7) | copy-start | bytes 12292
  15.3 0.8 %copy-start.3 = (f32[2,24,256]{2,1,0:T(8,128)S(1)}, f32[2,24,256]{2,1,0:T(8,128)}, u32[]{:S(2)}) copy-start(f32[2,24,256]{2,1,0:T(8,128)} %constant.24.clone.refs_3_) | copy-start | bytes 147460
  21.7 1.3 %collective-permute-start.5 = (f32[136,128]{1,0:T(8,128)S(1)}, f32[136,128]{1,0:T(8,128)S(1)}, u32[]{:S(2)}, u32[]{:S(2)}) collective-permute-start(f32[136,128]{1,0:T(8,128)S(1)} %get-tuple-element.22), channel_id=1, source_target_pairs={{0,1},{1,0},{2,3},{3,2},{4,5},{5,4},{6,7},{7,6},{8,9},{9,8},{10,11... | collective-permute-start | bytes 208904 | tf_op jit(solution)/shard_map/ppermute | solution.py:55
  23.0 4.4 %collective-permute-start.6 = (f32[136,128]{1,0:T(8,128)S(1)}, f32[136,128]{1,0:T(8,128)S(1)}, u32[]{:S(2)}, u32[]{:S(2)}) collective-permute-start(f32[136,128]{1,0:T(8,128)S(1)} %add.24), channel_id=1, source_target_pairs={{0,2},{1,9},{2,0},{3,11},{4,6},{5,13},{6,4},{7,15},{8,10},{9,1},{1... | collective-permute-start | bytes 208904 | tf_op jit(solution)/shard_map/ppermute | solution.py:55
  27.4 4.4 %collective-permute-start.7 = (f32[136,128]{1,0:T(8,128)S(1)}, f32[136,128]{1,0:T(8,128)S(1)}, u32[]{:S(2)}, u32[]{:S(2)}) collective-permute-start(f32[136,128]{1,0:T(8,128)S(1)} %add.25), channel_id=1, source_target_pairs={{0,4},{1,17},{2,6},{3,19},{4,0},{5,21},{6,2},{7,23},{8,12},{9,25},... | collective-permute-start | bytes 208904 | tf_op jit(solution)/shard_map/ppermute | solution.py:55
  31.8 5.3 %collective-permute-start.8 = (f32[136,128]{1,0:T(8,128)S(1)}, f32[136,128]{1,0:T(8,128)S(1)}, u32[]{:S(2)}, u32[]{:S(2)}) collective-permute-start(f32[136,128]{1,0:T(8,128)S(1)} %add.26), channel_id=1, source_target_pairs={{0,8},{1,3},{2,10},{3,1},{4,12},{5,7},{6,14},{7,5},{8,0},{9,11},{1... | collective-permute-start | bytes 208904 | tf_op jit(solution)/shard_map/ppermute | solution.py:55
  37.2 4.4 %collective-permute-start.9 = (f32[136,128]{1,0:T(8,128)S(1)}, f32[136,128]{1,0:T(8,128)S(1)}, u32[]{:S(2)}, u32[]{:S(2)}) collective-permute-start(f32[136,128]{1,0:T(8,128)S(1)} %add.27), channel_id=1, source_target_pairs={{0,16},{1,5},{2,18},{3,7},{4,20},{5,1},{6,22},{7,3},{8,24},{9,13},... | collective-permute-start | bytes 208904 | tf_op jit(solution)/shard_map/ppermute | solution.py:55
  41.6 1.3 %collective-permute-start.10 = (f32[136,128]{1,0:T(8,128)S(1)}, f32[136,128]{1,0:T(8,128)S(1)}, u32[]{:S(2)}, u32[]{:S(2)}) collective-permute-start(f32[136,128]{1,0:T(8,128)S(1)} %add.28.part_ref), channel_id=1, source_target_pairs={{0,1},{1,0},{2,3},{3,2},{4,5},{5,4},{6,7},{7,6},{8,9},{9,8},{10,11... | collective-permute-start | bytes 208904 | tf_op jit(solution)/shard_map/ppermute | solution.py:55
where the time goes:
time: 54.9 us; the launch traced here: 54.6 us
  waiting for transfers between devices  19.5 us (36%)
  Pallas kernels  17.4 us (32%)
  starting transfers between devices  13.2 us (24%)
  local copies, waits for them, and re-layouts  3.69 us (7%)
  between operations  0.75 us (1%)
    ppermute x11, waiting for transfers between devices, swap(): lax.ppermute(value, AXES, [(i, i ^ (odd_bit if i % 2 else bit)) for i in...  19.5 us
    ppermute x11, starting transfers between devices, swap(): lax.ppermute(value, AXES, [(i, i ^ (odd_bit if i % 2 else bit)) for i in...  13.2 us
    pallas_call x1, Pallas kernels, on_device(): pl.pallas_call(functools.partial(back_kernel, points_total, len(sketches)...  11.7 us
    pallas_call x3, Pallas kernels, on_device(): pl.pallas_call(functools.partial(front_kernel, start, width, own_rows, tm...  5.59 us
    unnamed x12, local copies, waits for them, and re-layouts  2.61 us
  transfers between devices with their start and end apart: 11, of which 8 were waited for; matrix products, arithmetic and copies ran while one was open for 0% of the time, Pallas kernels for 7%

commit v1 on v0

--- a/solution.py
+++ b/solution.py
@@ -55,6 +55,14 @@
     return lax.ppermute(
         value, AXES, [(i, i ^ (odd_bit if i % 2 else bit)) for i in range(total)]
     )
+
+
+def partners(bits):
+    return list(bits) + ([bits[0] ^ bits[1]] if len(bits) == 2 else [])
+
+
+def partners_order(groups):
+    return groups[::-1] if len({len(g) for g in groups}) == 1 else groups
 
 
 def cut_kernel(widths, own_rows, tm_count, days_ref, *refs):
@@ -144,6 +152,12 @@
     return jnp.broadcast_to(value[row:row + 1, :], (SUB, tile))
 
 
+def tree(terms):
+    while len(terms) > 1:
+        terms = [terms[q] + terms[q + 1] for q in range(0, len(terms), 2)]
+    return terms[0]
+
+
 def panel(blocks):
     count = len(blocks)
     blocks = list(blocks)
@@ -154,13 +168,15 @@
     for i in range(count):
         first = SUB * i
         own = blocks[i]
-        cols = [over_lanes(own, first + k, tile) for k in range(SUB)]
+        cols = [over_lanes(own, first + k, tile) for k in range(SUB)] if i == 0 else ahead
         e = {(j, k): over_rows(cols[k], j, tile) for k in range(SUB) for j in range(k + 1)}
         inside = (lane >= first) & (lane < first + SUB)
         later = {
             t: [over_lanes(blocks[t], first + k, tile) for k in range(SUB)]
             for t in range(i + 1, count)
         }
+        if i + 1 < count:
+            ahead = [over_lanes(blocks[i + 1], first + SUB + k, tile) for k in range(SUB)]
         rows = [
             jnp.where(inside, jnp.where(lane == first + j, 1.0, 0.0), over_rows(own, j, tile))
             for j in range(SUB)
@@ -179,11 +195,13 @@
                 rows[k] = rows[k] - fac[k] * rows[j]
                 for t in later:
                     later[t][k] = later[t][k] - fac[k] * later[t][j]
+        if i + 1 < count:
+            nxt = later[i + 1]
+            for k in range(SUB):
+                ahead[k] = ahead[k] - tree([nxt[j] * over_rows(nxt[j], k, tile) for j in range(SUB)])
         for t in later:
-            terms = [later[t][j] * rows[j] for j in range(SUB)]
-            while len(terms) > 1:
-                terms = [terms[q] + terms[q + 1] for q in range(0, len(terms), 2)]
-            blocks[t] = jnp.where(inside, 0.0, blocks[t]) - terms[0]
+            update = tree([later[t][j] * rows[j] for j in range(SUB)])
+            blocks[t] = jnp.where(inside, 0.0, blocks[t]) - update
         up = jnp.zeros((SUB, tile), jnp.float32)
         inv = up
         for j in range(SUB):
@@ -333,9 +351,16 @@
 
     part = kept + swap(sent, 1)
     bits = [1 << n for n in range(1, (tm_count * pts_count).bit_length() - 1)]
-    shift = (len(bits) + 1) // 2
-    for n in range(len(bits)):
-        part = part + swap(part, bits[n], bits[(n + shift) % len(bits)])
+    groups = []
+    while bits:
+        ends = {bits.pop(0), bits.pop() if bits else 0}
+        groups.append(tuple(sorted(ends)) if len(ends) == 2 and 0 not in ends else (max(ends),))
+    for even, odd in zip(groups, partners_order(groups)):
+        steps = list(zip(partners(even), partners(odd)))
+        got = [swap(part, *pair) for pair in steps]
+        while len(got) > 1:
+            got = [sum(got[n:n + 2][1:], got[n]) for n in range(0, len(got), 2)]
+        part = part + got[0]
     other = swap(part, 1)
 
     basis, factor = pl.pallas_call(

time: 54.9 us -> 49.4 us (0.90)
  Pallas kernels: 17.4 us -> 14.2 us
  waiting for transfers between devices: 19.5 us -> 16.6 us
  starting transfers between devices: 13.2 us -> 13.8 us
    pallas_call x1, Pallas kernels: 11.7 us -> 8.54 us  [on_device(): pl.pallas_call(functools.partial(back_kernel, points_total, len(sketches)...]
    ppermute x11 -> x13, waiting for transfers between devices: 19.5 us -> 16.6 us  [swap(): lax.ppermute(value, AXES, [(i, i ^ (odd_bit if i % 2 else bit)) for i in...]
    ppermute x11 -> x13, starting transfers between devices: 13.2 us -> 13.8 us  [swap(): lax.ppermute(value, AXES, [(i, i ^ (odd_bit if i % 2 else bit)) for i in...]
  transfers between devices with their start and end apart: 11 -> 13, of which waited for: 8 -> 9; matrix products, arithmetic and copies ran while one was open for 0% -> 0% of each run, Pallas kernels for 7% -> 8%
where the time goes in v1:
time: 49.4 us; the launch traced here: 49.2 us
  waiting for transfers between devices  16.6 us (34%)
  Pallas kernels  14.2 us (29%)
  starting transfers between devices  13.8 us (28%)
  local copies, waits for them, and re-layouts  3.69 us (7%)
  between operations  0.75 us (2%)
    ppermute x13, waiting for transfers between devices, swap(): lax.ppermute(value, AXES, [(i, i ^ (odd_bit if i % 2 else bit)) for i in...  16.6 us
    ppermute x13, starting transfers between devices, swap(): lax.ppermute(value, AXES, [(i, i ^ (odd_bit if i % 2 else bit)) for i in...  13.8 us
    pallas_call x1, Pallas kernels, on_device(): pl.pallas_call(functools.partial(back_kernel, points_total, len(sketches)...  8.54 us
    pallas_call x3, Pallas kernels, on_device(): pl.pallas_call(functools.partial(front_kernel, start, width, own_rows, tm...  5.59 us
    unnamed x12, local copies, waits for them, and re-layouts  2.61 us
  transfers between devices with their start and end apart: 13, of which 9 were waited for; matrix products, arithmetic and copies ran while one was open for 0% of the time, Pallas kernels for 8%

profile of v1, /device:TPU:0, one launch (start us, length us, event | category | flops | bytes accessed | tf_op | source)
XLA Modules:
  0.0 49.2 jit_solution(10047933359890191883)
XLA Ops:
  0.6 0.0 copy-start.2
  0.7 1.0 %constant_dynamic-slice_fusion = f32[128,256]{1,0:T(8,128)S(1)} fusion(f32[256,256]{1,0:T(8,128)} %refs_4_.5, s32[]{:T(128)S(6)} %select_n.11), kind=kLoop, calls=%fused_computation.2 | loop fusion | bytes 262148 | tf_op jit(solution)/shard_map/dynamic_slice | solution.py:279
  1.6 3.1 %collective-permute-start.3 = (f32[128,256]{1,0:T(8,128)S(1)}, f32[128,256]{1,0:T(8,128)S(1)}, u32[]{:S(2)}, u32[]{:S(2)}) collective-permute-start(f32[128,256]{1,0:T(8,128)S(1)} %constant_dynamic-slice_fusion), channel_id=1, source_target_pairs={{0,16},{1,17},{2,18},{3,19},{4,20},{5,21},{6,22},{7,23},{8,24},{9,... | collective-permute-start | bytes 393224 | tf_op jit(solution)/shard_map/ppermute | solution.py:55
  4.7 0.0 copy-start
  4.7 1.2 %copy-done = f32[256,1024]{1,0:T(8,128)S(1)} copy-done((f32[256,1024]{1,0:T(8,128)S(1)}, f32[256,1024]{1,0:T(8,128)}, u32[]{:S(2)}) %copy-start) | copy-done | bytes 1048600
  5.9 0.0 copy-start.1
  5.9 0.1 cut.1
  6.0 0.1 collective-permute-start.2
  6.1 2.5 %collective-permute-done.3.refs_6_ = f32[128,256]{1,0:T(8,128)S(1)} collective-permute-done((f32[128,256]{1,0:T(8,128)S(1)}, f32[128,256]{1,0:T(8,128)S(1)}, u32[]{:S(2)}, u32[]{:S(2)}) %collective-permute-start.3) | collective-permute-done | bytes 131104 | tf_op jit(solution)/shard_map/ppermute | solution.py:55
  8.6 0.0 collective-permute-start.4
  8.6 2.5 %collective-permute-start.1 = (f32[256,128]{1,0:T(8,128)S(1)}, f32[256,128]{1,0:T(8,128)S(1)}, u32[]{:S(2)}, u32[]{:S(2)}) collective-permute-start(f32[256,128]{1,0:T(8,128)S(1)} %get-tuple-element.15), channel_id=1, source_target_pairs={{0,16},{1,17},{2,18},{3,19},{4,20},{5,21},{6,22},{7,23},{8,24},{9,... | collective-permute-start | bytes 393224 | tf_op jit(solution)/shard_map/ppermute | solution.py:55
  11.1 0.0 copy-start.5
  11.1 0.1 collective-permute-start
  11.1 0.6 %copy-done.5 = f32[64]{0:T(128)S(1)} copy-done((f32[64]{0:T(128)S(1)}, f32[64]{0:T(128)}, u32[]{:S(2)}) %copy-start.5) | copy-done | bytes 280
  11.7 0.0 copy-start.4
  11.7 0.1 copy.9.refs_1_
  11.8 0.0 collective-permute-done.4.refs_7_
  11.8 3.4 %collective-permute-done.2.refs_5_ = f32[256,256]{1,0:T(8,128)S(1)} collective-permute-done((f32[256,256]{1,0:T(8,128)S(1)}, f32[256,256]{1,0:T(8,128)S(1)}, u32[]{:S(2)}, u32[]{:S(2)}) %collective-permute-start.2) | collective-permute-done | bytes 262176 | tf_op jit(solution)/shard_map/ppermute | solution.py:55
  15.3 0.0 copy-done.2
  15.3 0.0 copy-done.1
  15.3 0.0 copy-done.4
  15.3 0.0 copy-start.3
  15.3 0.8 %copy-done.3 = f32[2,24,256]{2,1,0:T(8,128)S(1)} copy-done((f32[2,24,256]{2,1,0:T(8,128)S(1)}, f32[2,24,256]{2,1,0:T(8,128)}, u32[]{:S(2)}) %copy-start.3) | copy-done | bytes 49176
  16.1 2.7 %shard_map.68 = (f32[256,256]{1,0:T(8,128)S(1)}, f32[256,256]{1,0:T(8,128)S(1)}) custom-call(f32[256,1024]{1,0:T(8,128)S(1)} %copy-done.1, f32[64,1]{1,0:T(8,128)S(1)} %copy.9.refs_1_, s32[1,1024]{1,0:T(1,128)S(1)} %bitcast.2, f32[2,24,256]{2,1,0:T(8,128)S(1)} %copy-done.3, f32[256,256]{1,0:T(8,128)S(1)} %copy-done.2, ...), custom_call_target="tpu_custom_call" | custom-call | flops 603979776 | bytes 1048576 | tf_op jit(solution)/shard_map/pallas_call | solution.py:320
  18.7 0.0 collective-permute-done.1.refs_5_
  18.7 1.2 %shard_map.69.refs_8_.refs_1_ = f32[128,256]{1,0:T(8,128)S(1)} custom-call(f32[256,1024]{1,0:T(8,128)S(1)} %copy-done.1, f32[64,1]{1,0:T(8,128)S(1)} %copy.9.refs_1_, s32[1,1024]{1,0:T(1,128)S(1)} %bitcast.3, f32[2,24,256]{2,1,0:T(8,128)S(1)} %copy-done.3, f32[256,256]{1,0:T(8,128)S(1)} %copy-done.2, f32[256,128]{1,0:T(8,128)S(1)} %collective-permute-done.1.refs_5_, ...), custom_call_target="tpu_custom_call" | custom-call | flops 301989888 | bytes 786432 | tf_op jit(solution)/shard_map/pallas_call | solution.py:320
  19.9 0.0 collective-permute-done.refs_5_
  19.9 1.8 %shard_map.70 = (f32[128,256]{1,0:T(8,128)S(1)}, f32[136,128]{1,0:T(8,128)S(1)}, f32[136,128]{1,0:T(8,128)S(1)}) custom-call(f32[256,1024]{1,0:T(8,128)S(1)} %copy-done.1, f32[64,1]{1,0:T(8,128)S(1)} %copy.9.refs_1_, s32[1,1024]{1,0:T(1,128)S(1)} %bitcast.4, f32[2,24,256]{2,1,0:T(8,128)S(1)} %copy-done.3, f32[256,256]{1,0:T(8,128)S(1)} %copy-done.2, ...), custom_call_target="tpu_custom_call" | custom-call | flops 301989888 | bytes 786432 | tf_op jit(solution)/shard_map/pallas_call | solution.py:320
  21.7 0.1 collective-permute-start.5
  21.8 1.2 %collective-permute-done.5 = f32[136,128]{1,0:T(8,128)S(1)} collective-permute-done((f32[136,128]{1,0:T(8,128)S(1)}, f32[136,128]{1,0:T(8,128)S(1)}, u32[]{:S(2)}, u32[]{:S(2)}) %collective-permute-start.5) | collective-permute-done | bytes 69664 | tf_op jit(solution)/shard_map/ppermute | solution.py:55
  23.0 2.4 %collective-permute-start.8 = (f32[136,128]{1,0:T(8,128)S(1)}, f32[136,128]{1,0:T(8,128)S(1)}, u32[]{:S(2)}, u32[]{:S(2)}) collective-permute-start(f32[136,128]{1,0:T(8,128)S(1)} %add.30), channel_id=1, source_target_pairs={{0,18},{1,13},{2,16},{3,15},{4,22},{5,9},{6,20},{7,11},{8,26},{9,5... | collective-permute-start | bytes 208904 | tf_op jit(solution)/shard_map/ppermute | solution.py:55
  25.5 0.6 %collective-permute-start.7 = (f32[136,128]{1,0:T(8,128)S(1)}, f32[136,128]{1,0:T(8,128)S(1)}, u32[]{:S(2)}, u32[]{:S(2)}) collective-permute-start(f32[136,128]{1,0:T(8,128)S(1)} %add.30), channel_id=1, source_target_pairs={{0,16},{1,9},{2,18},{3,11},{4,20},{5,13},{6,22},{7,15},{8,24},{9,1... | collective-permute-start | bytes 208904 | tf_op jit(solution)/shard_map/ppermute | solution.py:55
  26.1 0.5 %collective-permute-start.6 = (f32[136,128]{1,0:T(8,128)S(1)}, f32[136,128]{1,0:T(8,128)S(1)}, u32[]{:S(2)}, u32[]{:S(2)}) collective-permute-start(f32[136,128]{1,0:T(8,128)S(1)} %add.30), channel_id=1, source_target_pairs={{0,2},{1,5},{2,0},{3,7},{4,6},{5,1},{6,4},{7,3},{8,10},{9,13},{10,... | collective-permute-start | bytes 208904 | tf_op jit(solution)/shard_map/ppermute | solution.py:55
  26.6 1.7 %collective-permute-done.8 = f32[136,128]{1,0:T(8,128)S(1)} collective-permute-done((f32[136,128]{1,0:T(8,128)S(1)}, f32[136,128]{1,0:T(8,128)S(1)}, u32[]{:S(2)}, u32[]{:S(2)}) %collective-permute-start.8) | collective-permute-done | bytes 69664 | tf_op jit(solution)/shard_map/ppermute | solution.py:55
  28.3 1.4 %collective-permute-done.7 = f32[136,128]{1,0:T(8,128)S(1)} collective-permute-done((f32[136,128]{1,0:T(8,128)S(1)}, f32[136,128]{1,0:T(8,128)S(1)}, u32[]{:S(2)}, u32[]{:S(2)}) %collective-permute-start.7) | collective-permute-done | bytes 69664 | tf_op jit(solution)/shard_map/ppermute | solution.py:55
  29.8 0.6 %collective-permute-done.6 = f32[136,128]{1,0:T(8,128)S(1)} collective-permute-done((f32[136,128]{1,0:T(8,128)S(1)}, f32[136,128]{1,0:T(8,128)S(1)}, u32[]{:S(2)}, u32[]{:S(2)}) %collective-permute-start.6) | collective-permute-done | bytes 69664 | tf_op jit(solution)/shard_map/ppermute | solution.py:55
  30.4 3.7 %collective-permute-start.11 = (f32[136,128]{1,0:T(8,128)S(1)}, f32[136,128]{1,0:T(8,128)S(1)}, u32[]{:S(2)}, u32[]{:S(2)}) collective-permute-start(f32[136,128]{1,0:T(8,128)S(1)} %add_add_fusion.1), channel_id=1, source_target_pairs={{0,12},{1,19},{2,14},{3,17},{4,8},{5,23},{6,10},{7,21},{8,4},{9,27... | collective-permute-start | bytes 208904 | tf_op jit(solution)/shard_map/ppermute | solution.py:55
  34.1 0.0 collective-permute-start.10
  34.1 0.8 %collective-permute-start.9 = (f32[136,128]{1,0:T(8,128)S(1)}, f32[136,128]{1,0:T(8,128)S(1)}, u32[]{:S(2)}, u32[]{:S(2)}) collective-permute-start(f32[136,128]{1,0:T(8,128)S(1)} %add_add_fusion.1), channel_id=1, source_target_pairs={{0,4},{1,3},{2,6},{3,1},{4,0},{5,7},{6,2},{7,5},{8,12},{9,11},{10,... | collective-permute-start | bytes 208904 | tf_op jit(solution)/shard_map/ppermute | solution.py:55
  34.8 1.7 %collective-permute-done.11 = f32[136,128]{1,0:T(8,128)S(1)} collective-permute-done((f32[136,128]{1,0:T(8,128)S(1)}, f32[136,128]{1,0:T(8,128)S(1)}, u32[]{:S(2)}, u32[]{:S(2)}) %collective-permute-start.11) | collective-permute-done | bytes 69664 | tf_op jit(solution)/shard_map/ppermute | solution.py:55
  36.6 2.7 %collective-permute-done.10 = f32[136,128]{1,0:T(8,128)S(1)} collective-permute-done((f32[136,128]{1,0:T(8,128)S(1)}, f32[136,128]{1,0:T(8,128)S(1)}, u32[]{:S(2)}, u32[]{:S(2)}) %collective-permute-start.10) | collective-permute-done | bytes 69664 | tf_op jit(solution)/shard_map/ppermute | solution.py:55
  39.3 0.0 collective-permute-done.9
  39.3 0.1 collective-permute-start.12
  39.4 1.2 %collective-permute-done.12.other_ref = f32[136,128]{1,0:T(8,128)S(1)} collective-permute-done((f32[136,128]{1,0:T(8,128)S(1)}, f32[136,128]{1,0:T(8,128)S(1)}, u32[]{:S(2)}, u32[]{:S(2)}) %collective-permute-start.12) | collective-permute-done | bytes 69664 | tf_op jit(solution)/shard_map/ppermute | solution.py:55
  40.6 8.5 %back.1 = (f32[512,256]{1,0:T(8,128)}, f32[256,256]{1,0:T(8,128)}) custom-call(f32[136,128]{1,0:T(8,128)S(1)} %add_add_fusion.part_ref, f32[136,128]{1,0:T(8,128)S(1)} %collective-permute-done.12.other_ref, f32[256,256]{1,0:T(8,128)S(1)} %get-tuple-element.23.refs_0_, f32[128,256]{1,0:T(8,128)S(1)} %shard_map.69.refs_8_.refs_1_, ...), custom_call_target="tpu_custom_call" | custom-call | tf_op jit(solution)/shard_map/back/pallas_call | solution.py:366
  (3 shorter events, 0.1 us)
Async XLA Ops:
  0.6 14.6 %copy-start.2 = (f32[256,256]{1,0:T(8,128)S(1)}, f32[256,256]{1,0:T(8,128)}, u32[]{:S(2)}) copy-start(f32[256,256]{1,0:T(8,128)} %refs_4_.5) | copy-start | bytes 786436
  1.6 6.9 %collective-permute-start.3 = (f32[128,256]{1,0:T(8,128)S(1)}, f32[128,256]{1,0:T(8,128)S(1)}, u32[]{:S(2)}, u32[]{:S(2)}) collective-permute-start(f32[128,256]{1,0:T(8,128)S(1)} %constant_dynamic-slice_fusion), channel_id=1, source_target_pairs={{0,16},{1,17},{2,18},{3,19},{4,20},{5,21},{6,22},{7,23},{8,24},{9,... | collective-permute-start | bytes 393224 | tf_op jit(solution)/shard_map/ppermute | solution.py:55
  4.7 1.2 %copy-start = (f32[256,1024]{1,0:T(8,128)S(1)}, f32[256,1024]{1,0:T(8,128)}, u32[]{:S(2)}) copy-start(f32[256,1024]{1,0:T(8,128)} %refs_0_.5) | copy-start | bytes 3145732
  5.9 9.3 %copy-start.1 = (f32[256,1024]{1,0:T(8,128)S(1)}, f32[256,1024]{1,0:T(8,128)}, u32[]{:S(2)}) copy-start(f32[256,1024]{1,0:T(8,128)} %refs_0_.5) | copy-start | bytes 3145732
  6.0 9.2 %collective-permute-start.2 = (f32[256,256]{1,0:T(8,128)S(1)}, f32[256,256]{1,0:T(8,128)S(1)}, u32[]{:S(2)}, u32[]{:S(2)}) collective-permute-start(f32[256,256]{1,0:T(8,128)S(1)} %get-tuple-element.16), channel_id=1, source_target_pairs={{0,16},{1,17},{2,18},{3,19},{4,20},{5,21},{6,22},{7,23},{8,24},{9,... | collective-permute-start | bytes 786440 | tf_op jit(solution)/shard_map/ppermute | solution.py:55
  8.6 3.2 %collective-permute-start.4 = (f32[128,256]{1,0:T(8,128)S(1)}, f32[128,256]{1,0:T(8,128)S(1)}, u32[]{:S(2)}, u32[]{:S(2)}) collective-permute-start(f32[128,256]{1,0:T(8,128)S(1)} %collective-permute-done.3.refs_6_), channel_id=1, source_target_pairs={{0,1},{1,0},{2,3},{3,2},{4,5},{5,4},{6,7},{7,6},{8,9},{9,8},{10,11... | collective-permute-start | bytes 393224 | tf_op jit(solution)/shard_map/ppermute | solution.py:55
  8.6 10.2 %collective-permute-start.1 = (f32[256,128]{1,0:T(8,128)S(1)}, f32[256,128]{1,0:T(8,128)S(1)}, u32[]{:S(2)}, u32[]{:S(2)}) collective-permute-start(f32[256,128]{1,0:T(8,128)S(1)} %get-tuple-element.15), channel_id=1, source_target_pairs={{0,16},{1,17},{2,18},{3,19},{4,20},{5,21},{6,22},{7,23},{8,24},{9,... | collective-permute-start | bytes 393224 | tf_op jit(solution)/shard_map/ppermute | solution.py:55
  11.1 0.7 %copy-start.5 = (f32[64]{0:T(128)S(1)}, f32[64]{0:T(128)}, u32[]{:S(2)}) copy-start(f32[64]{0:T(128)} %param.6) | copy-start | bytes 772
  11.1 8.9 %collective-permute-start = (f32[256,128]{1,0:T(8,128)S(1)}, f32[256,128]{1,0:T(8,128)S(1)}, u32[]{:S(2)}, u32[]{:S(2)}) collective-permute-start(f32[256,128]{1,0:T(8,128)S(1)} %get-tuple-element.14), channel_id=1, source_target_pairs={{0,16},{1,17},{2,18},{3,19},{4,20},{5,21},{6,22},{7,23},{8,24},{9,... | collective-permute-start | bytes 393224 | tf_op jit(solution)/shard_map/ppermute | solution.py:55
  11.7 3.5 %copy-start.4 = (s32[1024]{0:T(1024)S(1)}, s32[1024]{0:T(1024)}, u32[]{:S(2)}) copy-start(s32[1024]{0:T(1024)} %param.7) | copy-start | bytes 12292
  15.3 0.8 %copy-start.3 = (f32[2,24,256]{2,1,0:T(8,128)S(1)}, f32[2,24,256]{2,1,0:T(8,128)}, u32[]{:S(2)}) copy-start(f32[2,24,256]{2,1,0:T(8,128)} %constant.24.clone.refs_3_) | copy-start | bytes 147460
  21.7 1.3 %collective-permute-start.5 = (f32[136,128]{1,0:T(8,128)S(1)}, f32[136,128]{1,0:T(8,128)S(1)}, u32[]{:S(2)}, u32[]{:S(2)}) collective-permute-start(f32[136,128]{1,0:T(8,128)S(1)} %get-tuple-element.22), channel_id=1, source_target_pairs={{0,1},{1,0},{2,3},{3,2},{4,5},{5,4},{6,7},{7,6},{8,9},{9,8},{10,11... | collective-permute-start | bytes 208904 | tf_op jit(solution)/shard_map/ppermute | solution.py:55
  23.0 5.3 %collective-permute-start.8 = (f32[136,128]{1,0:T(8,128)S(1)}, f32[136,128]{1,0:T(8,128)S(1)}, u32[]{:S(2)}, u32[]{:S(2)}) collective-permute-start(f32[136,128]{1,0:T(8,128)S(1)} %add.30), channel_id=1, source_target_pairs={{0,18},{1,13},{2,16},{3,15},{4,22},{5,9},{6,20},{7,11},{8,26},{9,5... | collective-permute-start | bytes 208904 | tf_op jit(solution)/shard_map/ppermute | solution.py:55
  25.5 4.3 %collective-permute-start.7 = (f32[136,128]{1,0:T(8,128)S(1)}, f32[136,128]{1,0:T(8,128)S(1)}, u32[]{:S(2)}, u32[]{:S(2)}) collective-permute-start(f32[136,128]{1,0:T(8,128)S(1)} %add.30), channel_id=1, source_target_pairs={{0,16},{1,9},{2,18},{3,11},{4,20},{5,13},{6,22},{7,15},{8,24},{9,1... | collective-permute-start | bytes 208904 | tf_op jit(solution)/shard_map/ppermute | solution.py:55
  26.1 4.3 %collective-permute-start.6 = (f32[136,128]{1,0:T(8,128)S(1)}, f32[136,128]{1,0:T(8,128)S(1)}, u32[]{:S(2)}, u32[]{:S(2)}) collective-permute-start(f32[136,128]{1,0:T(8,128)S(1)} %add.30), channel_id=1, source_target_pairs={{0,2},{1,5},{2,0},{3,7},{4,6},{5,1},{6,4},{7,3},{8,10},{9,13},{10,... | collective-permute-start | bytes 208904 | tf_op jit(solution)/shard_map/ppermute | solution.py:55
  30.4 6.2 %collective-permute-start.11 = (f32[136,128]{1,0:T(8,128)S(1)}, f32[136,128]{1,0:T(8,128)S(1)}, u32[]{:S(2)}, u32[]{:S(2)}) collective-permute-start(f32[136,128]{1,0:T(8,128)S(1)} %add_add_fusion.1), channel_id=1, source_target_pairs={{0,12},{1,19},{2,14},{3,17},{4,8},{5,23},{6,10},{7,21},{8,4},{9,27... | collective-permute-start | bytes 208904 | tf_op jit(solution)/shard_map/ppermute | solution.py:55
  34.1 5.2 %collective-permute-start.10 = (f32[136,128]{1,0:T(8,128)S(1)}, f32[136,128]{1,0:T(8,128)S(1)}, u32[]{:S(2)}, u32[]{:S(2)}) collective-permute-start(f32[136,128]{1,0:T(8,128)S(1)} %add_add_fusion.1), channel_id=1, source_target_pairs={{0,8},{1,17},{2,10},{3,19},{4,12},{5,21},{6,14},{7,23},{8,0},{9,25... | collective-permute-start | bytes 208904 | tf_op jit(solution)/shard_map/ppermute | solution.py:55
  34.1 5.2 %collective-permute-start.9 = (f32[136,128]{1,0:T(8,128)S(1)}, f32[136,128]{1,0:T(8,128)S(1)}, u32[]{:S(2)}, u32[]{:S(2)}) collective-permute-start(f32[136,128]{1,0:T(8,128)S(1)} %add_add_fusion.1), channel_id=1, source_target_pairs={{0,4},{1,3},{2,6},{3,1},{4,0},{5,7},{6,2},{7,5},{8,12},{9,11},{10,... | collective-permute-start | bytes 208904 | tf_op jit(solution)/shard_map/ppermute | solution.py:55
  39.3 1.3 %collective-permute-start.12 = (f32[136,128]{1,0:T(8,128)S(1)}, f32[136,128]{1,0:T(8,128)S(1)}, u32[]{:S(2)}, u32[]{:S(2)}) collective-permute-start(f32[136,128]{1,0:T(8,128)S(1)} %add_add_fusion.part_ref), channel_id=1, source_target_pairs={{0,1},{1,0},{2,3},{3,2},{4,5},{5,4},{6,7},{7,6},{8,9},{9,8},{10,11... | collective-permute-start | bytes 208904 | tf_op jit(solution)/shard_map/ppermute | solution.py:55

commit v2 on v1

--- a/solution.py
+++ b/solution.py
@@ -13,6 +13,7 @@
 HARM = 8
 SUB = 8
 AXES = ("tm", "pts")
+QUARTERS = (0, 1, 2, 3)
 HI = lax.Precision.HIGHEST
 
 year_days = 365.25
@@ -89,7 +90,7 @@
     take = lambda n: [refs.pop(0) for _ in range(n)]
     days_ref, thr_ref, bin_ref, filt_ref, test_ref = take(5)
     recv_refs = take(tm_count - 1)
-    half_refs = take(2 * (tm_count - 1))
+    quarter_refs = take(len(QUARTERS) * (tm_count - 1))
     earlier_refs = take(earlier)
     acc_refs = take(1 if with_acc else 0)
     sketch_ref = take(1)[0]
@@ -97,14 +98,15 @@
     table_ref = take(1)[0]
     days_local = days_ref.shape[0]
     place = lax.axis_index("tm")
-    low = lax.axis_index("pts") % 2
+    pts_place = lax.axis_index("pts")
+    low = pts_place % 2
     at = pl.multiple_of(place * own_rows + start, math.gcd(own_rows, start))
     table_ref[:days_local, :] = test_ref[...]
-    half = days_local // 2
-    for k in range(tm_count - 1):
-        base = days_local * (k + 1)
-        table_ref[pl.ds(pl.multiple_of(base + low * half, half), half), :] = half_refs[2 * k][...]
-        table_ref[pl.ds(pl.multiple_of(base + (1 - low) * half, half), half), :] = half_refs[2 * k + 1][...]
+    size = days_local // len(QUARTERS)
+    for n, ref in enumerate(quarter_refs):
+        peer, q = divmod(n, len(QUARTERS))
+        base = days_local * (peer + 1) + ((pts_place % len(QUARTERS)) ^ QUARTERS[q]) * size
+        table_ref[pl.ds(pl.multiple_of(base, size), size), :] = ref[...]
     bins = bin_ref[:, pl.ds(at, width)]
     count = thr_ref.shape[0]
     entry = lax.broadcasted_iota(jnp.int32, (count, width), 0)
@@ -158,44 +160,47 @@
     return terms[0]
 
 
-def panel(blocks):
+def panel(blocks, group):
     count = len(blocks)
     blocks = list(blocks)
     tile = count * SUB
     lane = lax.broadcasted_iota(jnp.int32, (SUB, tile), 1)
     row = lax.broadcasted_iota(jnp.int32, (SUB, tile), 0)
-    upper, inverse = [], []
+    upper, inverse, pending = [], [], []
     for i in range(count):
         first = SUB * i
         own = blocks[i]
-        cols = [over_lanes(own, first + k, tile) for k in range(SUB)] if i == 0 else ahead
-        e = {(j, k): over_rows(cols[k], j, tile) for k in range(SUB) for j in range(k + 1)}
+        end = min(count, (i // group + 1) * group)
+        if i % group == 0:
+            ahead = [over_lanes(own, first + k, tile) for k in range(SUB)]
+        cols, e = ahead, {}
         inside = (lane >= first) & (lane < first + SUB)
         later = {
             t: [over_lanes(blocks[t], first + k, tile) for k in range(SUB)]
-            for t in range(i + 1, count)
+            for t in range(i + 1, end)
         }
-        if i + 1 < count:
+        if i + 1 < end:
             ahead = [over_lanes(blocks[i + 1], first + SUB + k, tile) for k in range(SUB)]
         rows = [
             jnp.where(inside, jnp.where(lane == first + j, 1.0, 0.0), over_rows(own, j, tile))
             for j in range(SUB)
         ]
         for j in range(SUB):
-            s = lax.rsqrt(e[j, j])
-            fac = {k: e[j, k] * s for k in range(j + 1, SUB)}
-            e[j, j] = e[j, j] * s
+            line = [over_rows(cols[k], j, tile) for k in range(j, SUB)]
+            s = lax.rsqrt(line[0])
+            for k in range(j, SUB):
+                e[j, k] = line[k - j] * s
+            down = cols[j] * s
+            for k in range(j + 1, SUB):
+                cols[k] = cols[k] - down * e[j, k]
             rows[j] = rows[j] * s
             for t in later:
                 later[t][j] = later[t][j] * s
             for k in range(j + 1, SUB):
-                e[j, k] = fac[k]
-                for m in range(k, SUB):
-                    e[k, m] = e[k, m] - fac[k] * fac[m]
-                rows[k] = rows[k] - fac[k] * rows[j]
+                rows[k] = rows[k] - e[j, k] * rows[j]
                 for t in later:
-                    later[t][k] = later[t][k] - fac[k] * later[t][j]
-        if i + 1 < count:
+                    later[t][k] = later[t][k] - e[j, k] * later[t][j]
+        if i + 1 < end:
             nxt = later[i + 1]
             for k in range(SUB):
                 ahead[k] = ahead[k] - tree([nxt[j] * over_rows(nxt[j], k, tile) for j in range(SUB)])
@@ -203,21 +208,31 @@
             update = tree([later[t][j] * rows[j] for j in range(SUB)])
             blocks[t] = jnp.where(inside, 0.0, blocks[t]) - update
         up = jnp.zeros((SUB, tile), jnp.float32)
-        inv = up
+        full = up
         for j in range(SUB):
             line = jnp.where(lane >= first + SUB, rows[j], 0.0)
             for k in range(j, SUB):
                 line = jnp.where(lane == first + k, e[j, k], line)
             up = jnp.where(row == j, line, up)
-            inv = jnp.where(row == j, rows[j], inv)
+            full = jnp.where(row == j, rows[j], full)
+        pending.append(jnp.where((lane >= first + SUB) & (lane < SUB * end), 0.0, full))
         upper.append(up)
-        inverse.append(jnp.where(lane < first + SUB, inv, 0.0))
+        inverse.append(jnp.where(lane < first + SUB, full, 0.0))
+        if i + 1 == end < count:
+            done = jnp.concatenate(pending, 0)
+            pending = []
+            rest = SUB * end
+            update = tn(done[:, rest:], done)
+            here = (lane >= rest - group * SUB) & (lane < rest)
+            for t in range(end, count):
+                at = SUB * t - rest
+                blocks[t] = jnp.where(here, 0.0, blocks[t]) - update[at:at + SUB, :]
     return jnp.concatenate(upper, 0), jnp.concatenate(inverse, 0)
 
 
 def back_kernel(points_total, chunks, part_ref, other_ref, *refs):
     sketch_refs = refs[:chunks]
-    basis_ref, factor_ref = refs[chunks:]
+    basis_out, factor_out, basis_ref, factor_ref, sem = refs[chunks:]
     tile = part_ref.shape[1]
     low = lax.axis_index("pts") % 2
     part = part_ref[...] / points_total
@@ -230,35 +245,52 @@
     ends_t = ends.T
     side_t = side.T
     split = lambda a: [a[SUB * t:SUB * (t + 1), :] for t in range(tile // SUB)]
-    up, inv1 = panel(split(jnp.where(row >= col, ends, ends_t)))
+    group = max(1, tile // SUB // 2)
+    copies = []
+
+    def put(src, dst):
+        copies.append(pltpu.make_async_copy(src, dst, sem.at[len(copies)]))
+        copies[-1].start()
+
+    up, inv1 = panel(split(jnp.where(row >= col, ends, ends_t)), group)
     factor_ref[:tile, :tile] = up
     factor_ref[tile:, :tile] = jnp.zeros((tile, tile), jnp.float32)
     right = nn(inv1, side_t)
     right_t = nt(side, inv1)
     factor_ref[:tile, tile:] = right
     rest = jnp.where(row < col, ends, jnp.where(row == col, diag, ends_t)) - nn(right_t, right)
-    up, inv2 = panel(split(rest))
-    factor_ref[tile:, tile:] = up
-    at = 0
+    middle, at = [], 0
     for ref in sketch_refs:
         size = ref.shape[0]
         left = nt(ref[:, :tile], inv1)
         basis_ref[at:at + size, :tile] = left
-        basis_ref[at:at + size, tile:] = nt(ref[:, tile:] - nn(left, right), inv2)
+        middle.append(ref[:, tile:] - nn(left, right))
         at += size
+    put(factor_ref.at[:tile, :], factor_out.at[:tile, :])
+    put(basis_ref.at[:, :tile], basis_out.at[:, :tile])
+    up, inv2 = panel(split(rest), group)
+    factor_ref[tile:, tile:] = up
+    put(factor_ref.at[tile:, :], factor_out.at[tile:, :])
+    at = 0
+    for value in middle:
+        size = value.shape[0]
+        basis_ref[at:at + size, tile:] = nt(value, inv2)
+        put(basis_ref.at[at:at + size, tile:], basis_out.at[at:at + size, tile:])
+        at += size
+    for copy in copies:
+        copy.wait()
 
 
 def chunk_widths(own_rows):
     step = own_rows // 4
     if step % 128:
         return [own_rows]
-    return [2 * step, step, step]
+    return [step] * 4
 
 
 def on_device(precip, thresholds, bin_index, test_matrix):
     tm_count = lax.axis_size("tm")
     pts_count = lax.axis_size("pts")
-    low = lax.axis_index("pts") % 2
     days_local, points_local = precip.shape
     columns = test_matrix.shape[1]
     tile = columns // 2
@@ -275,8 +307,10 @@
 
     vmem = pl.BlockSpec(memory_space=pltpu.VMEM)
     widths = chunk_widths(own_rows)
-    half = days_local // 2
-    mine = lax.dynamic_slice_in_dim(test_matrix, low * half, half, 0)
+    size = days_local // len(QUARTERS)
+    mine = lax.dynamic_slice_in_dim(
+        test_matrix, (lax.axis_index("pts") % len(QUARTERS)) * size, size, 0
+    )
     shapes = [
         jax.ShapeDtypeStruct((days_local, width), f32)
         for width in widths
@@ -297,19 +331,23 @@
     came = []
     for _, value, k in sends:
         came.append(swap(value, k * pts_count))
-    halves, came = came[:tm_count - 1], came[tm_count - 1:]
+    quarters, came = came[:tm_count - 1], came[tm_count - 1:]
     received = [came[n * (tm_count - 1):(n + 1) * (tm_count - 1)] for n in range(len(widths))]
-    halves = [h for got in halves for h in (got, swap(got, 1))]
+    spread = []
+    for got in quarters:
+        beside = swap(got, 2)
+        spread += [got, swap(got, 1)]
+        spread += [beside, swap(beside, 1)]
 
     sketches, waiting = [], []
     cross = None
     start = 0
     for index, width in enumerate(widths):
         last = index == len(widths) - 1
-        with_cross = last or index == 0
+        with_cross = last or sum(v.shape[0] for v in waiting) + width >= columns
         if sketches:
             received[index], sketches[-1] = lax.optimization_barrier((received[index], sketches[-1]))
-        operands = [precip, thr, bins, filt, test_matrix] + received[index] + halves
+        operands = [precip, thr, bins, filt, test_matrix] + received[index] + spread
         operands += waiting if with_cross else []
         operands += [cross] if with_cross and cross is not None else []
         shapes = [jax.ShapeDtypeStruct((width, columns), f32)]
@@ -370,7 +408,12 @@
             jax.ShapeDtypeStruct((columns, columns), f32),
         ),
         in_specs=[vmem] * (2 + len(sketches)),
-        out_specs=(vmem, vmem),
+        out_specs=(pl.BlockSpec(memory_space=pltpu.HBM),) * 2,
+        scratch_shapes=[
+            pltpu.VMEM((own_rows, columns), f32),
+            pltpu.VMEM((columns, columns), f32),
+            pltpu.SemaphoreType.DMA((3 + len(sketches),)),
+        ],
         compiler_params=pltpu.CompilerParams(vmem_limit_bytes=16 << 20),
         name="back",
     )(part, other, *sketches)

time: 49.4 us -> 49.3 us (level)
  starting transfers between devices: 13.8 us -> 17.6 us
  waiting for transfers between devices: 16.6 us -> 14.4 us
  Pallas kernels: 14.2 us -> 13 us
  local copies, waits for them, and re-layouts: 3.69 us -> 3.14 us
    ppermute x13 -> x16, starting transfers between devices: 13.8 us -> 17.6 us  [swap(): lax.ppermute(value, AXES, [(i, i ^ (odd_bit if i % 2 else bit)) for i in...]
    ppermute x13 -> x16, waiting for transfers between devices: 16.6 us -> 14.4 us  [swap(): lax.ppermute(value, AXES, [(i, i ^ (odd_bit if i % 2 else bit)) for i in...]
    pallas_call x1, Pallas kernels: 8.54 us -> 7.17 us  [on_device(): pl.pallas_call(functools.partial(back_kernel, points_total, len(sketches)...]
    pallas_call x3 -> x4, Pallas kernels: 5.59 us -> 5.73 us  [on_device(): pl.pallas_call(functools.partial(front_kernel, start, width, own_rows, tm...]
  transfers between devices with their start and end apart: 13 -> 16, of which waited for: 9 -> 12; matrix products, arithmetic and copies ran while one was open for 0% -> 0% of each run, Pallas kernels for 8% -> 8%
where the time goes in v2:
time: 49.3 us; the launch traced here: 49 us
  starting transfers between devices  17.6 us (36%)
  waiting for transfers between devices  14.4 us (29%)
  Pallas kernels  13 us (26%)
  local copies, waits for them, and re-layouts  3.14 us (6%)
  between operations  0.75 us (2%)
    ppermute x16, starting transfers between devices, swap(): lax.ppermute(value, AXES, [(i, i ^ (odd_bit if i % 2 else bit)) for i in...  17.6 us
    ppermute x16, waiting for transfers between devices, swap(): lax.ppermute(value, AXES, [(i, i ^ (odd_bit if i % 2 else bit)) for i in...  14.4 us
    pallas_call x1, Pallas kernels, on_device(): pl.pallas_call(functools.partial(back_kernel, points_total, len(sketches)...  7.17 us
    pallas_call x4, Pallas kernels, on_device(): pl.pallas_call(functools.partial(front_kernel, start, width, own_rows, tm...  5.73 us
    unnamed x12, local copies, waits for them, and re-layouts  2.19 us
  transfers between devices with their start and end apart: 16, of which 12 were waited for; matrix products, arithmetic and copies ran while one was open for 0% of the time, Pallas kernels for 8%

profile of v2, /device:TPU:0, one launch (start us, length us, event | category | flops | bytes accessed | tf_op | source)
XLA Modules:
  0.0 49.0 jit_solution(1408545601150720265)
XLA Ops:
  0.6 0.0 copy-start.3
  0.7 0.9 %constant_dynamic-slice_fusion = f32[64,256]{1,0:T(8,128)S(1)} fusion(f32[256,256]{1,0:T(8,128)} %refs_4_.7, s32[]{:T(128)S(6)} %select_n.11), kind=kLoop, calls=%fused_computation.2 | loop fusion | bytes 131076 | tf_op jit(solution)/shard_map/dynamic_slice | solution.py:311
  1.5 3.0 %collective-permute-start.4 = (f32[64,256]{1,0:T(8,128)S(1)}, f32[64,256]{1,0:T(8,128)S(1)}, u32[]{:S(2)}, u32[]{:S(2)}) collective-permute-start(f32[64,256]{1,0:T(8,128)S(1)} %constant_dynamic-slice_fusion), channel_id=1, source_target_pairs={{0,16},{1,17},{2,18},{3,19},{4,20},{5,21},{6,22},{7,23},{8,24},{9,... | collective-permute-start | bytes 196616 | tf_op jit(solution)/shard_map/ppermute | solution.py:56
  4.5 1.2 %copy-done = f32[256,1024]{1,0:T(8,128)S(1)} copy-done((f32[256,1024]{1,0:T(8,128)S(1)}, f32[256,1024]{1,0:T(8,128)}, u32[]{:S(2)}) %copy-start) | copy-done | bytes 1048600
  5.7 0.1 cut.1
  5.9 0.9 %collective-permute-done.4.refs_6_ = f32[64,256]{1,0:T(8,128)S(1)} collective-permute-done((f32[64,256]{1,0:T(8,128)S(1)}, f32[64,256]{1,0:T(8,128)S(1)}, u32[]{:S(2)}, u32[]{:S(2)}) %collective-permute-start.4) | collective-permute-done | bytes 65568 | tf_op jit(solution)/shard_map/ppermute | solution.py:56
  6.8 2.0 %collective-permute-start.6 = (f32[64,256]{1,0:T(8,128)S(1)}, f32[64,256]{1,0:T(8,128)S(1)}, u32[]{:S(2)}, u32[]{:S(2)}) collective-permute-start(f32[64,256]{1,0:T(8,128)S(1)} %collective-permute-done.4.refs_6_), channel_id=1, source_target_pairs={{0,2},{1,3},{2,0},{3,1},{4,6},{5,7},{6,4},{7,5},{8,10},{9,11},{10,... | collective-permute-start | bytes 196616 | tf_op jit(solution)/shard_map/ppermute | solution.py:56
  8.7 1.5 %collective-permute-start.3 = (f32[256,128]{1,0:T(8,128)S(1)}, f32[256,128]{1,0:T(8,128)S(1)}, u32[]{:S(2)}, u32[]{:S(2)}) collective-permute-start(f32[256,128]{1,0:T(8,128)S(1)} %get-tuple-element.20), channel_id=1, source_target_pairs={{0,16},{1,17},{2,18},{3,19},{4,20},{5,21},{6,22},{7,23},{8,24},{9,... | collective-permute-start | bytes 393224 | tf_op jit(solution)/shard_map/ppermute | solution.py:56
  10.3 0.0 collective-permute-start.5
  10.3 0.5 %collective-permute-start.2 = (f32[256,128]{1,0:T(8,128)S(1)}, f32[256,128]{1,0:T(8,128)S(1)}, u32[]{:S(2)}, u32[]{:S(2)}) collective-permute-start(f32[256,128]{1,0:T(8,128)S(1)} %get-tuple-element.19), channel_id=1, source_target_pairs={{0,16},{1,17},{2,18},{3,19},{4,20},{5,21},{6,22},{7,23},{8,24},{9,... | collective-permute-start | bytes 393224 | tf_op jit(solution)/shard_map/ppermute | solution.py:56
  10.8 1.5 %collective-permute-start.1 = (f32[256,128]{1,0:T(8,128)S(1)}, f32[256,128]{1,0:T(8,128)S(1)}, u32[]{:S(2)}, u32[]{:S(2)}) collective-permute-start(f32[256,128]{1,0:T(8,128)S(1)} %get-tuple-element.18), channel_id=1, source_target_pairs={{0,16},{1,17},{2,18},{3,19},{4,20},{5,21},{6,22},{7,23},{8,24},{9,... | collective-permute-start | bytes 393224 | tf_op jit(solution)/shard_map/ppermute | solution.py:56
  12.3 0.0 collective-permute-done.6.refs_8_
  12.3 0.0 collective-permute-start.7
  12.3 0.0 collective-permute-done.5.refs_7_
  12.3 0.0 copy-start.5
  12.3 0.8 %collective-permute-start = (f32[256,128]{1,0:T(8,128)S(1)}, f32[256,128]{1,0:T(8,128)S(1)}, u32[]{:S(2)}, u32[]{:S(2)}) collective-permute-start(f32[256,128]{1,0:T(8,128)S(1)} %get-tuple-element.17), channel_id=1, source_target_pairs={{0,16},{1,17},{2,18},{3,19},{4,20},{5,21},{6,22},{7,23},{8,24},{9,... | collective-permute-start | bytes 393224 | tf_op jit(solution)/shard_map/ppermute | solution.py:56
  13.1 0.0 copy-done.5
  13.1 0.1 copy.10.refs_1_
  13.2 0.9 %collective-permute-done.3.refs_5_ = f32[256,128]{1,0:T(8,128)S(1)} collective-permute-done((f32[256,128]{1,0:T(8,128)S(1)}, f32[256,128]{1,0:T(8,128)S(1)}, u32[]{:S(2)}, u32[]{:S(2)}) %collective-permute-start.3) | collective-permute-done | bytes 131104 | tf_op jit(solution)/shard_map/ppermute | solution.py:56
  14.1 0.0 collective-permute-done.7.refs_9_
  14.1 0.0 copy-done.3
  14.1 0.0 copy-done.1
  14.1 0.0 copy-start.2
  14.1 0.9 %copy-done.2 = f32[256,256]{1,0:T(8,128)S(1)} copy-done((f32[256,256]{1,0:T(8,128)S(1)}, f32[256,256]{1,0:T(8,128)}, u32[]{:S(2)}) %copy-start.2) | copy-done | bytes 262168
  15.1 1.1 %shard_map.68.refs_10_.refs_0_ = f32[128,256]{1,0:T(8,128)S(1)} custom-call(f32[256,1024]{1,0:T(8,128)S(1)} %copy-done.1, f32[64,1]{1,0:T(8,128)S(1)} %copy.10.refs_1_, s32[1,1024]{1,0:T(1,128)S(1)} %bitcast.2, f32[2,24,256]{2,1,0:T(8,128)S(1)} %copy-done.3, f32[256,256]{1,0:T(8,128)S(1)} %copy-done.2, f32[256,128]{1,0:T(8,128)S(1)} %collective-permute-done.3.refs_5_, ...), custom_call_target="tpu_custom_call" | custom-call | flops 301989888 | bytes 786432 | tf_op jit(solution)/shard_map/pallas_call | solution.py:358
  16.2 0.7 %collective-permute-done.2.refs_5_ = f32[256,128]{1,0:T(8,128)S(1)} collective-permute-done((f32[256,128]{1,0:T(8,128)S(1)}, f32[256,128]{1,0:T(8,128)S(1)}, u32[]{:S(2)}, u32[]{:S(2)}) %collective-permute-start.2) | collective-permute-done | bytes 131104 | tf_op jit(solution)/shard_map/ppermute | solution.py:56
  16.9 1.7 %shard_map.69 = (f32[128,256]{1,0:T(8,128)S(1)}, f32[256,256]{1,0:T(8,128)S(1)}) custom-call(f32[256,1024]{1,0:T(8,128)S(1)} %copy-done.1, f32[64,1]{1,0:T(8,128)S(1)} %copy.10.refs_1_, s32[1,1024]{1,0:T(1,128)S(1)} %bitcast.3, f32[2,24,256]{2,1,0:T(8,128)S(1)} %copy-done.3, f32[256,256]{1,0:T(8,128)S(1)} %copy-done.2, ...), custom_call_target="tpu_custom_call" | custom-call | flops 301989888 | bytes 786432 | tf_op jit(solution)/shard_map/pallas_call | solution.py:358
  18.7 1.1 %collective-permute-done.1.refs_5_ = f32[256,128]{1,0:T(8,128)S(1)} collective-permute-done((f32[256,128]{1,0:T(8,128)S(1)}, f32[256,128]{1,0:T(8,128)S(1)}, u32[]{:S(2)}, u32[]{:S(2)}) %collective-permute-start.1) | collective-permute-done | bytes 131104 | tf_op jit(solution)/shard_map/ppermute | solution.py:56
  19.7 1.1 %shard_map.70.refs_10_.refs_2_ = f32[128,256]{1,0:T(8,128)S(1)} custom-call(f32[256,1024]{1,0:T(8,128)S(1)} %copy-done.1, f32[64,1]{1,0:T(8,128)S(1)} %copy.10.refs_1_, s32[1,1024]{1,0:T(1,128)S(1)} %bitcast.4, f32[2,24,256]{2,1,0:T(8,128)S(1)} %copy-done.3, f32[256,256]{1,0:T(8,128)S(1)} %copy-done.2, f32[256,128]{1,0:T(8,128)S(1)} %collective-permute-done.1.refs_5_, ...), custom_call_target="tpu_custom_call" | custom-call | flops 301989888 | bytes 786432 | tf_op jit(solution)/shard_map/pallas_call | solution.py:358
  20.9 1.3 %collective-permute-done.refs_5_ = f32[256,128]{1,0:T(8,128)S(1)} collective-permute-done((f32[256,128]{1,0:T(8,128)S(1)}, f32[256,128]{1,0:T(8,128)S(1)}, u32[]{:S(2)}, u32[]{:S(2)}) %collective-permute-start) | collective-permute-done | bytes 131104 | tf_op jit(solution)/shard_map/ppermute | solution.py:56
  22.1 1.7 %shard_map.71 = (f32[128,256]{1,0:T(8,128)S(1)}, f32[136,128]{1,0:T(8,128)S(1)}, f32[136,128]{1,0:T(8,128)S(1)}) custom-call(f32[256,1024]{1,0:T(8,128)S(1)} %copy-done.1, f32[64,1]{1,0:T(8,128)S(1)} %copy.10.refs_1_, s32[1,1024]{1,0:T(1,128)S(1)} %bitcast.5, f32[2,24,256]{2,1,0:T(8,128)S(1)} %copy-done.3, f32[256,256]{1,0:T(8,128)S(1)} %copy-done.2, ...), custom_call_target="tpu_custom_call" | custom-call | flops 301989888 | bytes 786432 | tf_op jit(solution)/shard_map/pallas_call | solution.py:358
  23.9 0.1 collective-permute-start.8
  24.0 1.2 %collective-permute-done.8 = f32[136,128]{1,0:T(8,128)S(1)} collective-permute-done((f32[136,128]{1,0:T(8,128)S(1)}, f32[136,128]{1,0:T(8,128)S(1)}, u32[]{:S(2)}, u32[]{:S(2)}) %collective-permute-start.8) | collective-permute-done | bytes 69664 | tf_op jit(solution)/shard_map/ppermute | solution.py:56
  25.2 1.4 %collective-permute-start.11 = (f32[136,128]{1,0:T(8,128)S(1)}, f32[136,128]{1,0:T(8,128)S(1)}, u32[]{:S(2)}, u32[]{:S(2)}) collective-permute-start(f32[136,128]{1,0:T(8,128)S(1)} %add.30), channel_id=1, source_target_pairs={{0,18},{1,13},{2,16},{3,15},{4,22},{5,9},{6,20},{7,11},{8,26},{9,5... | collective-permute-start | bytes 208904 | tf_op jit(solution)/shard_map/ppermute | solution.py:56
  26.6 0.3 collective-permute-start.10
  27.0 1.8 %collective-permute-start.9 = (f32[136,128]{1,0:T(8,128)S(1)}, f32[136,128]{1,0:T(8,128)S(1)}, u32[]{:S(2)}, u32[]{:S(2)}) collective-permute-start(f32[136,128]{1,0:T(8,128)S(1)} %add.30), channel_id=1, source_target_pairs={{0,2},{1,5},{2,0},{3,7},{4,6},{5,1},{6,4},{7,3},{8,10},{9,13},{10,... | collective-permute-start | bytes 208904 | tf_op jit(solution)/shard_map/ppermute | solution.py:56
  28.8 1.8 %collective-permute-done.11 = f32[136,128]{1,0:T(8,128)S(1)} collective-permute-done((f32[136,128]{1,0:T(8,128)S(1)}, f32[136,128]{1,0:T(8,128)S(1)}, u32[]{:S(2)}, u32[]{:S(2)}) %collective-permute-start.11) | collective-permute-done | bytes 69664 | tf_op jit(solution)/shard_map/ppermute | solution.py:56
  30.5 0.7 %collective-permute-done.10 = f32[136,128]{1,0:T(8,128)S(1)} collective-permute-done((f32[136,128]{1,0:T(8,128)S(1)}, f32[136,128]{1,0:T(8,128)S(1)}, u32[]{:S(2)}, u32[]{:S(2)}) %collective-permute-start.10) | collective-permute-done | bytes 69664 | tf_op jit(solution)/shard_map/ppermute | solution.py:56
  31.3 0.1 collective-permute-done.9
  31.3 4.0 %collective-permute-start.14 = (f32[136,128]{1,0:T(8,128)S(1)}, f32[136,128]{1,0:T(8,128)S(1)}, u32[]{:S(2)}, u32[]{:S(2)}) collective-permute-start(f32[136,128]{1,0:T(8,128)S(1)} %add_add_fusion.1), channel_id=1, source_target_pairs={{0,12},{1,19},{2,14},{3,17},{4,8},{5,23},{6,10},{7,21},{8,4},{9,27... | collective-permute-start | bytes 208904 | tf_op jit(solution)/shard_map/ppermute | solution.py:56
  35.3 0.0 collective-permute-start.13
  35.3 0.6 %collective-permute-start.12 = (f32[136,128]{1,0:T(8,128)S(1)}, f32[136,128]{1,0:T(8,128)S(1)}, u32[]{:S(2)}, u32[]{:S(2)}) collective-permute-start(f32[136,128]{1,0:T(8,128)S(1)} %add_add_fusion.1), channel_id=1, source_target_pairs={{0,4},{1,3},{2,6},{3,1},{4,0},{5,7},{6,2},{7,5},{8,12},{9,11},{10,... | collective-permute-start | bytes 208904 | tf_op jit(solution)/shard_map/ppermute | solution.py:56
  35.9 1.7 %collective-permute-done.14 = f32[136,128]{1,0:T(8,128)S(1)} collective-permute-done((f32[136,128]{1,0:T(8,128)S(1)}, f32[136,128]{1,0:T(8,128)S(1)}, u32[]{:S(2)}, u32[]{:S(2)}) %collective-permute-start.14) | collective-permute-done | bytes 69664 | tf_op jit(solution)/shard_map/ppermute | solution.py:56
  37.7 2.8 %collective-permute-done.13 = f32[136,128]{1,0:T(8,128)S(1)} collective-permute-done((f32[136,128]{1,0:T(8,128)S(1)}, f32[136,128]{1,0:T(8,128)S(1)}, u32[]{:S(2)}, u32[]{:S(2)}) %collective-permute-start.13) | collective-permute-done | bytes 69664 | tf_op jit(solution)/shard_map/ppermute | solution.py:56
  40.5 0.0 collective-permute-done.12
  40.5 0.1 collective-permute-start.15
  40.6 1.2 %collective-permute-done.15.other_ref = f32[136,128]{1,0:T(8,128)S(1)} collective-permute-done((f32[136,128]{1,0:T(8,128)S(1)}, f32[136,128]{1,0:T(8,128)S(1)}, u32[]{:S(2)}, u32[]{:S(2)}) %collective-permute-start.15) | collective-permute-done | bytes 69664 | tf_op jit(solution)/shard_map/ppermute | solution.py:56
  41.9 7.2 %back.1 = (f32[512,256]{1,0:T(8,128)}, f32[256,256]{1,0:T(8,128)}) custom-call(f32[136,128]{1,0:T(8,128)S(1)} %add_add_fusion.part_ref, f32[136,128]{1,0:T(8,128)S(1)} %collective-permute-done.15.other_ref, f32[128,256]{1,0:T(8,128)S(1)} %shard_map.68.refs_10_.refs_0_, f32[128,256]{1,0:T(8,128)S(1)} %get-tuple-element.29.refs_1_, ...), custom_call_target="tpu_custom_call" | custom-call | tf_op jit(solution)/shard_map/back/pallas_call | solution.py:404
  (7 shorter events, 0.1 us)
Async XLA Ops:
  0.6 13.5 %copy-start.3 = (f32[2,24,256]{2,1,0:T(8,128)S(1)}, f32[2,24,256]{2,1,0:T(8,128)}, u32[]{:S(2)}) copy-start(f32[2,24,256]{2,1,0:T(8,128)} %constant.24.clone.refs_3_) | copy-start | bytes 147460
  1.5 5.2 %collective-permute-start.4 = (f32[64,256]{1,0:T(8,128)S(1)}, f32[64,256]{1,0:T(8,128)S(1)}, u32[]{:S(2)}, u32[]{:S(2)}) collective-permute-start(f32[64,256]{1,0:T(8,128)S(1)} %constant_dynamic-slice_fusion), channel_id=1, source_target_pairs={{0,16},{1,17},{2,18},{3,19},{4,20},{5,21},{6,22},{7,23},{8,24},{9,... | collective-permute-start | bytes 196616 | tf_op jit(solution)/shard_map/ppermute | solution.py:56
  4.5 1.2 %copy-start = (f32[256,1024]{1,0:T(8,128)S(1)}, f32[256,1024]{1,0:T(8,128)}, u32[]{:S(2)}) copy-start(f32[256,1024]{1,0:T(8,128)} %refs_0_.7) | copy-start | bytes 3145732
  5.7 8.4 %copy-start.1 = (f32[256,1024]{1,0:T(8,128)S(1)}, f32[256,1024]{1,0:T(8,128)}, u32[]{:S(2)}) copy-start(f32[256,1024]{1,0:T(8,128)} %refs_0_.7) | copy-start | bytes 3145732
  6.8 5.5 %collective-permute-start.6 = (f32[64,256]{1,0:T(8,128)S(1)}, f32[64,256]{1,0:T(8,128)S(1)}, u32[]{:S(2)}, u32[]{:S(2)}) collective-permute-start(f32[64,256]{1,0:T(8,128)S(1)} %collective-permute-done.4.refs_6_), channel_id=1, source_target_pairs={{0,2},{1,3},{2,0},{3,1},{4,6},{5,7},{6,4},{7,5},{8,10},{9,11},{10,... | collective-permute-start | bytes 196616 | tf_op jit(solution)/shard_map/ppermute | solution.py:56
  8.7 5.4 %collective-permute-start.3 = (f32[256,128]{1,0:T(8,128)S(1)}, f32[256,128]{1,0:T(8,128)S(1)}, u32[]{:S(2)}, u32[]{:S(2)}) collective-permute-start(f32[256,128]{1,0:T(8,128)S(1)} %get-tuple-element.20), channel_id=1, source_target_pairs={{0,16},{1,17},{2,18},{3,19},{4,20},{5,21},{6,22},{7,23},{8,24},{9,... | collective-permute-start | bytes 393224 | tf_op jit(solution)/shard_map/ppermute | solution.py:56
  10.3 2.0 %collective-permute-start.5 = (f32[64,256]{1,0:T(8,128)S(1)}, f32[64,256]{1,0:T(8,128)S(1)}, u32[]{:S(2)}, u32[]{:S(2)}) collective-permute-start(f32[64,256]{1,0:T(8,128)S(1)} %collective-permute-done.4.refs_6_), channel_id=1, source_target_pairs={{0,1},{1,0},{2,3},{3,2},{4,5},{5,4},{6,7},{7,6},{8,9},{9,8},{10,11... | collective-permute-start | bytes 196616 | tf_op jit(solution)/shard_map/ppermute | solution.py:56
  10.3 6.6 %collective-permute-start.2 = (f32[256,128]{1,0:T(8,128)S(1)}, f32[256,128]{1,0:T(8,128)S(1)}, u32[]{:S(2)}, u32[]{:S(2)}) collective-permute-start(f32[256,128]{1,0:T(8,128)S(1)} %get-tuple-element.19), channel_id=1, source_target_pairs={{0,16},{1,17},{2,18},{3,19},{4,20},{5,21},{6,22},{7,23},{8,24},{9,... | collective-permute-start | bytes 393224 | tf_op jit(solution)/shard_map/ppermute | solution.py:56
  10.8 8.9 %collective-permute-start.1 = (f32[256,128]{1,0:T(8,128)S(1)}, f32[256,128]{1,0:T(8,128)S(1)}, u32[]{:S(2)}, u32[]{:S(2)}) collective-permute-start(f32[256,128]{1,0:T(8,128)S(1)} %get-tuple-element.18), channel_id=1, source_target_pairs={{0,16},{1,17},{2,18},{3,19},{4,20},{5,21},{6,22},{7,23},{8,24},{9,... | collective-permute-start | bytes 393224 | tf_op jit(solution)/shard_map/ppermute | solution.py:56
  12.3 1.8 %collective-permute-start.7 = (f32[64,256]{1,0:T(8,128)S(1)}, f32[64,256]{1,0:T(8,128)S(1)}, u32[]{:S(2)}, u32[]{:S(2)}) collective-permute-start(f32[64,256]{1,0:T(8,128)S(1)} %collective-permute-done.6.refs_8_), channel_id=1, source_target_pairs={{0,1},{1,0},{2,3},{3,2},{4,5},{5,4},{6,7},{7,6},{8,9},{9,8},{10,11... | collective-permute-start | bytes 196616 | tf_op jit(solution)/shard_map/ppermute | solution.py:56
  12.3 0.8 %copy-start.5 = (f32[64]{0:T(128)S(1)}, f32[64]{0:T(128)}, u32[]{:S(2)}) copy-start(f32[64]{0:T(128)} %param.6) | copy-start | bytes 772
  12.3 9.8 %collective-permute-start = (f32[256,128]{1,0:T(8,128)S(1)}, f32[256,128]{1,0:T(8,128)S(1)}, u32[]{:S(2)}, u32[]{:S(2)}) collective-permute-start(f32[256,128]{1,0:T(8,128)S(1)} %get-tuple-element.17), channel_id=1, source_target_pairs={{0,16},{1,17},{2,18},{3,19},{4,20},{5,21},{6,22},{7,23},{8,24},{9,... | collective-permute-start | bytes 393224 | tf_op jit(solution)/shard_map/ppermute | solution.py:56
  13.1 1.0 %copy-start.4 = (s32[1024]{0:T(1024)S(1)}, s32[1024]{0:T(1024)}, u32[]{:S(2)}) copy-start(s32[1024]{0:T(1024)} %param.7) | copy-start | bytes 12292
  14.1 1.0 %copy-start.2 = (f32[256,256]{1,0:T(8,128)S(1)}, f32[256,256]{1,0:T(8,128)}, u32[]{:S(2)}) copy-start(f32[256,256]{1,0:T(8,128)} %refs_4_.7) | copy-start | bytes 786436
  23.9 1.3 %collective-permute-start.8 = (f32[136,128]{1,0:T(8,128)S(1)}, f32[136,128]{1,0:T(8,128)S(1)}, u32[]{:S(2)}, u32[]{:S(2)}) collective-permute-start(f32[136,128]{1,0:T(8,128)S(1)} %get-tuple-element.27), channel_id=1, source_target_pairs={{0,1},{1,0},{2,3},{3,2},{4,5},{5,4},{6,7},{7,6},{8,9},{9,8},{10,11... | collective-permute-start | bytes 208904 | tf_op jit(solution)/shard_map/ppermute | solution.py:56
  25.2 5.3 %collective-permute-start.11 = (f32[136,128]{1,0:T(8,128)S(1)}, f32[136,128]{1,0:T(8,128)S(1)}, u32[]{:S(2)}, u32[]{:S(2)}) collective-permute-start(f32[136,128]{1,0:T(8,128)S(1)} %add.30), channel_id=1, source_target_pairs={{0,18},{1,13},{2,16},{3,15},{4,22},{5,9},{6,20},{7,11},{8,26},{9,5... | collective-permute-start | bytes 208904 | tf_op jit(solution)/shard_map/ppermute | solution.py:56
  26.6 4.6 %collective-permute-start.10 = (f32[136,128]{1,0:T(8,128)S(1)}, f32[136,128]{1,0:T(8,128)S(1)}, u32[]{:S(2)}, u32[]{:S(2)}) collective-permute-start(f32[136,128]{1,0:T(8,128)S(1)} %add.30), channel_id=1, source_target_pairs={{0,16},{1,9},{2,18},{3,11},{4,20},{5,13},{6,22},{7,15},{8,24},{9,1... | collective-permute-start | bytes 208904 | tf_op jit(solution)/shard_map/ppermute | solution.py:56
  27.0 4.4 %collective-permute-start.9 = (f32[136,128]{1,0:T(8,128)S(1)}, f32[136,128]{1,0:T(8,128)S(1)}, u32[]{:S(2)}, u32[]{:S(2)}) collective-permute-start(f32[136,128]{1,0:T(8,128)S(1)} %add.30), channel_id=1, source_target_pairs={{0,2},{1,5},{2,0},{3,7},{4,6},{5,1},{6,4},{7,3},{8,10},{9,13},{10,... | collective-permute-start | bytes 208904 | tf_op jit(solution)/shard_map/ppermute | solution.py:56
  31.3 6.3 %collective-permute-start.14 = (f32[136,128]{1,0:T(8,128)S(1)}, f32[136,128]{1,0:T(8,128)S(1)}, u32[]{:S(2)}, u32[]{:S(2)}) collective-permute-start(f32[136,128]{1,0:T(8,128)S(1)} %add_add_fusion.1), channel_id=1, source_target_pairs={{0,12},{1,19},{2,14},{3,17},{4,8},{5,23},{6,10},{7,21},{8,4},{9,27... | collective-permute-start | bytes 208904 | tf_op jit(solution)/shard_map/ppermute | solution.py:56
  35.3 5.2 %collective-permute-start.13 = (f32[136,128]{1,0:T(8,128)S(1)}, f32[136,128]{1,0:T(8,128)S(1)}, u32[]{:S(2)}, u32[]{:S(2)}) collective-permute-start(f32[136,128]{1,0:T(8,128)S(1)} %add_add_fusion.1), channel_id=1, source_target_pairs={{0,8},{1,17},{2,10},{3,19},{4,12},{5,21},{6,14},{7,23},{8,0},{9,25... | collective-permute-start | bytes 208904 | tf_op jit(solution)/shard_map/ppermute | solution.py:56
  35.3 5.2 %collective-permute-start.12 = (f32[136,128]{1,0:T(8,128)S(1)}, f32[136,128]{1,0:T(8,128)S(1)}, u32[]{:S(2)}, u32[]{:S(2)}) collective-permute-start(f32[136,128]{1,0:T(8,128)S(1)} %add_add_fusion.1), channel_id=1, source_target_pairs={{0,4},{1,3},{2,6},{3,1},{4,0},{5,7},{6,2},{7,5},{8,12},{9,11},{10,... | collective-permute-start | bytes 208904 | tf_op jit(solution)/shard_map/ppermute | solution.py:56
  40.5 1.3 %collective-permute-start.15 = (f32[136,128]{1,0:T(8,128)S(1)}, f32[136,128]{1,0:T(8,128)S(1)}, u32[]{:S(2)}, u32[]{:S(2)}) collective-permute-start(f32[136,128]{1,0:T(8,128)S(1)} %add_add_fusion.part_ref), channel_id=1, source_target_pairs={{0,1},{1,0},{2,3},{3,2},{4,5},{5,4},{6,7},{7,6},{8,9},{9,8},{10,11... | collective-permute-start | bytes 208904 | tf_op jit(solution)/shard_map/ppermute | solution.py:56

commit v3 on v2

--- a/solution.py
+++ b/solution.py
@@ -83,6 +83,10 @@
         copy.start()
     for copy in copies:
         copy.wait()
+
+
+def hold_kernel(test_ref, held_ref):
+    held_ref[...] = test_ref[...]
 
 
 def front_kernel(start, width, own_rows, tm_count, earlier, with_acc, with_cross, last, *refs):
@@ -325,6 +329,14 @@
         compiler_params=pltpu.CompilerParams(vmem_limit_bytes=4 << 20),
         name="cut",
     )(precip)
+    held = pl.pallas_call(
+        hold_kernel,
+        out_shape=jax.ShapeDtypeStruct(test_matrix.shape, f32),
+        in_specs=[vmem],
+        out_specs=vmem,
+        compiler_params=pltpu.CompilerParams(vmem_limit_bytes=4 << 20),
+        name="hold",
+    )(test_matrix)
     sends = [("rows", mine, k) for k in range(1, tm_count)]
     for n in range(len(widths)):
         sends += [("points", pieces[n * (tm_count - 1) + k - 1], k) for k in range(1, tm_count)]
@@ -347,7 +359,7 @@
         with_cross = last or sum(v.shape[0] for v in waiting) + width >= columns
         if sketches:
             received[index], sketches[-1] = lax.optimization_barrier((received[index], sketches[-1]))
-        operands = [precip, thr, bins, filt, test_matrix] + received[index] + spread
+        operands = [precip, thr, bins, filt, held] + received[index] + spread
         operands += waiting if with_cross else []
         operands += [cross] if with_cross and cross is not None else []
         shapes = [jax.ShapeDtypeStruct((width, columns), f32)]

time: 49.3 us -> 49.3 us (level)
  waiting for transfers between devices: 14.4 us -> 13.2 us
  local copies, waits for them, and re-layouts: 3.14 us -> 4.34 us
    unnamed x12, local copies, waits for them, and re-layouts: 2.19 us -> 3.4 us
    ppermute x16, waiting for transfers between devices: 14.4 us -> 13.2 us  [swap(): lax.ppermute(value, AXES, [(i, i ^ (odd_bit if i % 2 else bit)) for i in...]
  transfers between devices with their start and end apart: 16 -> 16, of which waited for: 12 -> 11; matrix products, arithmetic and copies ran while one was open for 0% -> 0% of each run, Pallas kernels for 8% -> 8%
where the time goes in v3:
time: 49.3 us; the launch traced here: 49 us
  starting transfers between devices  17.6 us (36%)
  waiting for transfers between devices  13.2 us (27%)
  Pallas kernels  13 us (26%)
  local copies, waits for them, and re-layouts  4.34 us (9%)
  between operations  0.76 us (2%)
    ppermute x16, starting transfers between devices, swap(): lax.ppermute(value, AXES, [(i, i ^ (odd_bit if i % 2 else bit)) for i in...  17.6 us
    ppermute x16, waiting for transfers between devices, swap(): lax.ppermute(value, AXES, [(i, i ^ (odd_bit if i % 2 else bit)) for i in...  13.2 us
    pallas_call x1, Pallas kernels, on_device(): pl.pallas_call(functools.partial(back_kernel, points_total, len(sketches)...  7.17 us
    pallas_call x4, Pallas kernels, on_device(): pl.pallas_call(functools.partial(front_kernel, start, width, own_rows, tm...  5.73 us
    unnamed x12, local copies, waits for them, and re-layouts  3.4 us
  transfers between devices with their start and end apart: 16, of which 11 were waited for; matrix products, arithmetic and copies ran while one was open for 0% of the time, Pallas kernels for 8%

profile of v3, /device:TPU:0, one launch (start us, length us, event | category | flops | bytes accessed | tf_op | source)
XLA Modules:
  0.0 49.0 jit_solution(15136006421389545559)
XLA Ops:
  0.6 0.8 %constant_dynamic-slice_fusion = f32[64,256]{1,0:T(8,128)S(1)} fusion(f32[256,256]{1,0:T(8,128)} %test_ref.1, s32[]{:T(128)S(6)} %select_n.11), kind=kLoop, calls=%fused_computation.2 | loop fusion | bytes 131076 | tf_op jit(solution)/shard_map/dynamic_slice | solution.py:315
  1.5 3.0 %collective-permute-start.4 = (f32[64,256]{1,0:T(8,128)S(1)}, f32[64,256]{1,0:T(8,128)S(1)}, u32[]{:S(2)}, u32[]{:S(2)}) collective-permute-start(f32[64,256]{1,0:T(8,128)S(1)} %constant_dynamic-slice_fusion), channel_id=1, source_target_pairs={{0,16},{1,17},{2,18},{3,19},{4,20},{5,21},{6,22},{7,23},{8,24},{9,... | collective-permute-start | bytes 196616 | tf_op jit(solution)/shard_map/ppermute | solution.py:56
  4.5 0.0 copy-start
  4.5 1.2 %copy-done = f32[256,1024]{1,0:T(8,128)S(1)} copy-done((f32[256,1024]{1,0:T(8,128)S(1)}, f32[256,1024]{1,0:T(8,128)}, u32[]{:S(2)}) %copy-start) | copy-done | bytes 1048600
  5.7 0.1 cut.1
  5.8 0.9 %collective-permute-done.4.refs_6_ = f32[64,256]{1,0:T(8,128)S(1)} collective-permute-done((f32[64,256]{1,0:T(8,128)S(1)}, f32[64,256]{1,0:T(8,128)S(1)}, u32[]{:S(2)}, u32[]{:S(2)}) %collective-permute-start.4) | collective-permute-done | bytes 65568 | tf_op jit(solution)/shard_map/ppermute | solution.py:56
  6.7 2.0 %collective-permute-start.6 = (f32[64,256]{1,0:T(8,128)S(1)}, f32[64,256]{1,0:T(8,128)S(1)}, u32[]{:S(2)}, u32[]{:S(2)}) collective-permute-start(f32[64,256]{1,0:T(8,128)S(1)} %collective-permute-done.4.refs_6_), channel_id=1, source_target_pairs={{0,2},{1,3},{2,0},{3,1},{4,6},{5,7},{6,4},{7,5},{8,10},{9,11},{10,... | collective-permute-start | bytes 196616 | tf_op jit(solution)/shard_map/ppermute | solution.py:56
  8.7 1.5 %collective-permute-start.3 = (f32[256,128]{1,0:T(8,128)S(1)}, f32[256,128]{1,0:T(8,128)S(1)}, u32[]{:S(2)}, u32[]{:S(2)}) collective-permute-start(f32[256,128]{1,0:T(8,128)S(1)} %get-tuple-element.20), channel_id=1, source_target_pairs={{0,16},{1,17},{2,18},{3,19},{4,20},{5,21},{6,22},{7,23},{8,24},{9,... | collective-permute-start | bytes 393224 | tf_op jit(solution)/shard_map/ppermute | solution.py:56
  10.2 0.0 collective-permute-start.5
  10.3 0.5 %collective-permute-start.2 = (f32[256,128]{1,0:T(8,128)S(1)}, f32[256,128]{1,0:T(8,128)S(1)}, u32[]{:S(2)}, u32[]{:S(2)}) collective-permute-start(f32[256,128]{1,0:T(8,128)S(1)} %get-tuple-element.19), channel_id=1, source_target_pairs={{0,16},{1,17},{2,18},{3,19},{4,20},{5,21},{6,22},{7,23},{8,24},{9,... | collective-permute-start | bytes 393224 | tf_op jit(solution)/shard_map/ppermute | solution.py:56
  10.8 1.5 %collective-permute-start.1 = (f32[256,128]{1,0:T(8,128)S(1)}, f32[256,128]{1,0:T(8,128)S(1)}, u32[]{:S(2)}, u32[]{:S(2)}) collective-permute-start(f32[256,128]{1,0:T(8,128)S(1)} %get-tuple-element.18), channel_id=1, source_target_pairs={{0,16},{1,17},{2,18},{3,19},{4,20},{5,21},{6,22},{7,23},{8,24},{9,... | collective-permute-start | bytes 393224 | tf_op jit(solution)/shard_map/ppermute | solution.py:56
  12.3 0.0 collective-permute-done.6.refs_8_
  12.3 0.0 collective-permute-start.7
  12.3 0.0 collective-permute-done.5.refs_7_
  12.3 0.7 %collective-permute-start = (f32[256,128]{1,0:T(8,128)S(1)}, f32[256,128]{1,0:T(8,128)S(1)}, u32[]{:S(2)}, u32[]{:S(2)}) collective-permute-start(f32[256,128]{1,0:T(8,128)S(1)} %get-tuple-element.17), channel_id=1, source_target_pairs={{0,16},{1,17},{2,18},{3,19},{4,20},{5,21},{6,22},{7,23},{8,24},{9,... | collective-permute-start | bytes 393224 | tf_op jit(solution)/shard_map/ppermute | solution.py:56
  13.0 0.9 %copy-done.3 = f32[256,256]{1,0:T(8,128)S(1)} copy-done((f32[256,256]{1,0:T(8,128)S(1)}, f32[256,256]{1,0:T(8,128)}, u32[]{:S(2)}) %copy-start.3) | copy-done | bytes 262168
  14.0 0.0 copy-start.5
  14.0 0.6 %copy-done.5 = f32[64]{0:T(128)S(1)} copy-done((f32[64]{0:T(128)S(1)}, f32[64]{0:T(128)}, u32[]{:S(2)}) %copy-start.5) | copy-done | bytes 280
  14.7 0.1 copy.10.refs_1_
  14.8 0.0 collective-permute-done.3.refs_5_
  14.8 0.0 collective-permute-done.7.refs_9_
  14.8 0.0 copy-done.1
  14.8 0.0 copy-done.2
  14.8 0.6 %copy-done.4 = s32[1024]{0:T(1024)S(1)} copy-done((s32[1024]{0:T(1024)S(1)}, s32[1024]{0:T(1024)}, u32[]{:S(2)}) %copy-start.4) | copy-done | bytes 4120
  15.4 1.1 %shard_map.68.refs_10_.refs_0_ = f32[128,256]{1,0:T(8,128)S(1)} custom-call(f32[256,1024]{1,0:T(8,128)S(1)} %copy-done.1, f32[64,1]{1,0:T(8,128)S(1)} %copy.10.refs_1_, s32[1,1024]{1,0:T(1,128)S(1)} %bitcast.2, f32[2,24,256]{2,1,0:T(8,128)S(1)} %copy-done.2, f32[256,256]{1,0:T(8,128)S(1)} %hold.1.refs_4_, f32[256,128]{1,0:T(8,128)S(1)} %collective-permute-done.3.refs_5_, ...), custom_call_target="tpu_custom_call" | custom-call | flops 301989888 | bytes 786432 | tf_op jit(solution)/shard_map/pallas_call | solution.py:370
  16.5 0.4 collective-permute-done.2.refs_5_
  16.9 1.7 %shard_map.69 = (f32[128,256]{1,0:T(8,128)S(1)}, f32[256,256]{1,0:T(8,128)S(1)}) custom-call(f32[256,1024]{1,0:T(8,128)S(1)} %copy-done.1, f32[64,1]{1,0:T(8,128)S(1)} %copy.10.refs_1_, s32[1,1024]{1,0:T(1,128)S(1)} %bitcast.3, f32[2,24,256]{2,1,0:T(8,128)S(1)} %copy-done.2, f32[256,256]{1,0:T(8,128)S(1)} %hold.1.refs_4_, ...), custom_call_target="tpu_custom_call" | custom-call | flops 301989888 | bytes 786432 | tf_op jit(solution)/shard_map/pallas_call | solution.py:370
  18.6 1.1 %collective-permute-done.1.refs_5_ = f32[256,128]{1,0:T(8,128)S(1)} collective-permute-done((f32[256,128]{1,0:T(8,128)S(1)}, f32[256,128]{1,0:T(8,128)S(1)}, u32[]{:S(2)}, u32[]{:S(2)}) %collective-permute-start.1) | collective-permute-done | bytes 131104 | tf_op jit(solution)/shard_map/ppermute | solution.py:56
  19.7 1.1 %shard_map.70.refs_10_.refs_2_ = f32[128,256]{1,0:T(8,128)S(1)} custom-call(f32[256,1024]{1,0:T(8,128)S(1)} %copy-done.1, f32[64,1]{1,0:T(8,128)S(1)} %copy.10.refs_1_, s32[1,1024]{1,0:T(1,128)S(1)} %bitcast.4, f32[2,24,256]{2,1,0:T(8,128)S(1)} %copy-done.2, f32[256,256]{1,0:T(8,128)S(1)} %hold.1.refs_4_, f32[256,128]{1,0:T(8,128)S(1)} %collective-permute-done.1.refs_5_, ...), custom_call_target="tpu_custom_call" | custom-call | flops 301989888 | bytes 786432 | tf_op jit(solution)/shard_map/pallas_call | solution.py:370
  20.8 1.3 %collective-permute-done.refs_5_ = f32[256,128]{1,0:T(8,128)S(1)} collective-permute-done((f32[256,128]{1,0:T(8,128)S(1)}, f32[256,128]{1,0:T(8,128)S(1)}, u32[]{:S(2)}, u32[]{:S(2)}) %collective-permute-start) | collective-permute-done | bytes 131104 | tf_op jit(solution)/shard_map/ppermute | solution.py:56
  22.1 1.7 %shard_map.71 = (f32[128,256]{1,0:T(8,128)S(1)}, f32[136,128]{1,0:T(8,128)S(1)}, f32[136,128]{1,0:T(8,128)S(1)}) custom-call(f32[256,1024]{1,0:T(8,128)S(1)} %copy-done.1, f32[64,1]{1,0:T(8,128)S(1)} %copy.10.refs_1_, s32[1,1024]{1,0:T(1,128)S(1)} %bitcast.5, f32[2,24,256]{2,1,0:T(8,128)S(1)} %copy-done.2, f32[256,256]{1,0:T(8,128)S(1)} %hold.1.refs_4_, ...), custom_call_target="tpu_custom_call" | custom-call | flops 301989888 | bytes 786432 | tf_op jit(solution)/shard_map/pallas_call | solution.py:370
  23.9 0.1 collective-permute-start.8
  23.9 1.2 %collective-permute-done.8 = f32[136,128]{1,0:T(8,128)S(1)} collective-permute-done((f32[136,128]{1,0:T(8,128)S(1)}, f32[136,128]{1,0:T(8,128)S(1)}, u32[]{:S(2)}, u32[]{:S(2)}) %collective-permute-start.8) | collective-permute-done | bytes 69664 | tf_op jit(solution)/shard_map/ppermute | solution.py:56
  25.2 1.4 %collective-permute-start.11 = (f32[136,128]{1,0:T(8,128)S(1)}, f32[136,128]{1,0:T(8,128)S(1)}, u32[]{:S(2)}, u32[]{:S(2)}) collective-permute-start(f32[136,128]{1,0:T(8,128)S(1)} %add.30), channel_id=1, source_target_pairs={{0,18},{1,13},{2,16},{3,15},{4,22},{5,9},{6,20},{7,11},{8,26},{9,5... | collective-permute-start | bytes 208904 | tf_op jit(solution)/shard_map/ppermute | solution.py:56
  26.6 0.3 collective-permute-start.10
  26.9 1.8 %collective-permute-start.9 = (f32[136,128]{1,0:T(8,128)S(1)}, f32[136,128]{1,0:T(8,128)S(1)}, u32[]{:S(2)}, u32[]{:S(2)}) collective-permute-start(f32[136,128]{1,0:T(8,128)S(1)} %add.30), channel_id=1, source_target_pairs={{0,2},{1,5},{2,0},{3,7},{4,6},{5,1},{6,4},{7,3},{8,10},{9,13},{10,... | collective-permute-start | bytes 208904 | tf_op jit(solution)/shard_map/ppermute | solution.py:56
  28.8 1.8 %collective-permute-done.11 = f32[136,128]{1,0:T(8,128)S(1)} collective-permute-done((f32[136,128]{1,0:T(8,128)S(1)}, f32[136,128]{1,0:T(8,128)S(1)}, u32[]{:S(2)}, u32[]{:S(2)}) %collective-permute-start.11) | collective-permute-done | bytes 69664 | tf_op jit(solution)/shard_map/ppermute | solution.py:56
  30.5 0.7 %collective-permute-done.10 = f32[136,128]{1,0:T(8,128)S(1)} collective-permute-done((f32[136,128]{1,0:T(8,128)S(1)}, f32[136,128]{1,0:T(8,128)S(1)}, u32[]{:S(2)}, u32[]{:S(2)}) %collective-permute-start.10) | collective-permute-done | bytes 69664 | tf_op jit(solution)/shard_map/ppermute | solution.py:56
  31.2 0.1 collective-permute-done.9
  31.3 4.0 %collective-permute-start.14 = (f32[136,128]{1,0:T(8,128)S(1)}, f32[136,128]{1,0:T(8,128)S(1)}, u32[]{:S(2)}, u32[]{:S(2)}) collective-permute-start(f32[136,128]{1,0:T(8,128)S(1)} %add_add_fusion.1), channel_id=1, source_target_pairs={{0,12},{1,19},{2,14},{3,17},{4,8},{5,23},{6,10},{7,21},{8,4},{9,27... | collective-permute-start | bytes 208904 | tf_op jit(solution)/shard_map/ppermute | solution.py:56
  35.3 0.0 collective-permute-start.13
  35.3 0.6 %collective-permute-start.12 = (f32[136,128]{1,0:T(8,128)S(1)}, f32[136,128]{1,0:T(8,128)S(1)}, u32[]{:S(2)}, u32[]{:S(2)}) collective-permute-start(f32[136,128]{1,0:T(8,128)S(1)} %add_add_fusion.1), channel_id=1, source_target_pairs={{0,4},{1,3},{2,6},{3,1},{4,0},{5,7},{6,2},{7,5},{8,12},{9,11},{10,... | collective-permute-start | bytes 208904 | tf_op jit(solution)/shard_map/ppermute | solution.py:56
  35.9 1.7 %collective-permute-done.14 = f32[136,128]{1,0:T(8,128)S(1)} collective-permute-done((f32[136,128]{1,0:T(8,128)S(1)}, f32[136,128]{1,0:T(8,128)S(1)}, u32[]{:S(2)}, u32[]{:S(2)}) %collective-permute-start.14) | collective-permute-done | bytes 69664 | tf_op jit(solution)/shard_map/ppermute | solution.py:56
  37.7 2.8 %collective-permute-done.13 = f32[136,128]{1,0:T(8,128)S(1)} collective-permute-done((f32[136,128]{1,0:T(8,128)S(1)}, f32[136,128]{1,0:T(8,128)S(1)}, u32[]{:S(2)}, u32[]{:S(2)}) %collective-permute-start.13) | collective-permute-done | bytes 69664 | tf_op jit(solution)/shard_map/ppermute | solution.py:56
  40.5 0.0 collective-permute-done.12
  40.5 0.1 collective-permute-start.15
  40.6 1.2 %collective-permute-done.15.other_ref = f32[136,128]{1,0:T(8,128)S(1)} collective-permute-done((f32[136,128]{1,0:T(8,128)S(1)}, f32[136,128]{1,0:T(8,128)S(1)}, u32[]{:S(2)}, u32[]{:S(2)}) %collective-permute-start.15) | collective-permute-done | bytes 69664 | tf_op jit(solution)/shard_map/ppermute | solution.py:56
  41.8 7.2 %back.1 = (f32[512,256]{1,0:T(8,128)}, f32[256,256]{1,0:T(8,128)}) custom-call(f32[136,128]{1,0:T(8,128)S(1)} %add_add_fusion.part_ref, f32[136,128]{1,0:T(8,128)S(1)} %collective-permute-done.15.other_ref, f32[128,256]{1,0:T(8,128)S(1)} %shard_map.68.refs_10_.refs_0_, f32[128,256]{1,0:T(8,128)S(1)} %get-tuple-element.29.refs_1_, ...), custom_call_target="tpu_custom_call" | custom-call | tf_op jit(solution)/shard_map/back/pallas_call | solution.py:416
  (8 shorter events, 0.1 us)
Async XLA Ops:
  1.5 5.2 %collective-permute-start.4 = (f32[64,256]{1,0:T(8,128)S(1)}, f32[64,256]{1,0:T(8,128)S(1)}, u32[]{:S(2)}, u32[]{:S(2)}) collective-permute-start(f32[64,256]{1,0:T(8,128)S(1)} %constant_dynamic-slice_fusion), channel_id=1, source_target_pairs={{0,16},{1,17},{2,18},{3,19},{4,20},{5,21},{6,22},{7,23},{8,24},{9,... | collective-permute-start | bytes 196616 | tf_op jit(solution)/shard_map/ppermute | solution.py:56
  4.5 1.2 %copy-start = (f32[256,1024]{1,0:T(8,128)S(1)}, f32[256,1024]{1,0:T(8,128)}, u32[]{:S(2)}) copy-start(f32[256,1024]{1,0:T(8,128)} %refs_0_.7) | copy-start | bytes 3145732
  5.7 9.1 %copy-start.1 = (f32[256,1024]{1,0:T(8,128)S(1)}, f32[256,1024]{1,0:T(8,128)}, u32[]{:S(2)}) copy-start(f32[256,1024]{1,0:T(8,128)} %refs_0_.7) | copy-start | bytes 3145732
  6.7 5.5 %collective-permute-start.6 = (f32[64,256]{1,0:T(8,128)S(1)}, f32[64,256]{1,0:T(8,128)S(1)}, u32[]{:S(2)}, u32[]{:S(2)}) collective-permute-start(f32[64,256]{1,0:T(8,128)S(1)} %collective-permute-done.4.refs_6_), channel_id=1, source_target_pairs={{0,2},{1,3},{2,0},{3,1},{4,6},{5,7},{6,4},{7,5},{8,10},{9,11},{10,... | collective-permute-start | bytes 196616 | tf_op jit(solution)/shard_map/ppermute | solution.py:56
  8.7 6.0 %collective-permute-start.3 = (f32[256,128]{1,0:T(8,128)S(1)}, f32[256,128]{1,0:T(8,128)S(1)}, u32[]{:S(2)}, u32[]{:S(2)}) collective-permute-start(f32[256,128]{1,0:T(8,128)S(1)} %get-tuple-element.20), channel_id=1, source_target_pairs={{0,16},{1,17},{2,18},{3,19},{4,20},{5,21},{6,22},{7,23},{8,24},{9,... | collective-permute-start | bytes 393224 | tf_op jit(solution)/shard_map/ppermute | solution.py:56
  10.2 2.0 %collective-permute-start.5 = (f32[64,256]{1,0:T(8,128)S(1)}, f32[64,256]{1,0:T(8,128)S(1)}, u32[]{:S(2)}, u32[]{:S(2)}) collective-permute-start(f32[64,256]{1,0:T(8,128)S(1)} %collective-permute-done.4.refs_6_), channel_id=1, source_target_pairs={{0,1},{1,0},{2,3},{3,2},{4,5},{5,4},{6,7},{7,6},{8,9},{9,8},{10,11... | collective-permute-start | bytes 196616 | tf_op jit(solution)/shard_map/ppermute | solution.py:56
  10.3 6.6 %collective-permute-start.2 = (f32[256,128]{1,0:T(8,128)S(1)}, f32[256,128]{1,0:T(8,128)S(1)}, u32[]{:S(2)}, u32[]{:S(2)}) collective-permute-start(f32[256,128]{1,0:T(8,128)S(1)} %get-tuple-element.19), channel_id=1, source_target_pairs={{0,16},{1,17},{2,18},{3,19},{4,20},{5,21},{6,22},{7,23},{8,24},{9,... | collective-permute-start | bytes 393224 | tf_op jit(solution)/shard_map/ppermute | solution.py:56
  10.8 8.9 %collective-permute-start.1 = (f32[256,128]{1,0:T(8,128)S(1)}, f32[256,128]{1,0:T(8,128)S(1)}, u32[]{:S(2)}, u32[]{:S(2)}) collective-permute-start(f32[256,128]{1,0:T(8,128)S(1)} %get-tuple-element.18), channel_id=1, source_target_pairs={{0,16},{1,17},{2,18},{3,19},{4,20},{5,21},{6,22},{7,23},{8,24},{9,... | collective-permute-start | bytes 393224 | tf_op jit(solution)/shard_map/ppermute | solution.py:56
  12.3 2.5 %collective-permute-start.7 = (f32[64,256]{1,0:T(8,128)S(1)}, f32[64,256]{1,0:T(8,128)S(1)}, u32[]{:S(2)}, u32[]{:S(2)}) collective-permute-start(f32[64,256]{1,0:T(8,128)S(1)} %collective-permute-done.6.refs_8_), channel_id=1, source_target_pairs={{0,1},{1,0},{2,3},{3,2},{4,5},{5,4},{6,7},{7,6},{8,9},{9,8},{10,11... | collective-permute-start | bytes 196616 | tf_op jit(solution)/shard_map/ppermute | solution.py:56
  12.3 9.8 %collective-permute-start = (f32[256,128]{1,0:T(8,128)S(1)}, f32[256,128]{1,0:T(8,128)S(1)}, u32[]{:S(2)}, u32[]{:S(2)}) collective-permute-start(f32[256,128]{1,0:T(8,128)S(1)} %get-tuple-element.17), channel_id=1, source_target_pairs={{0,16},{1,17},{2,18},{3,19},{4,20},{5,21},{6,22},{7,23},{8,24},{9,... | collective-permute-start | bytes 393224 | tf_op jit(solution)/shard_map/ppermute | solution.py:56
  13.0 0.9 %copy-start.3 = (f32[256,256]{1,0:T(8,128)S(1)}, f32[256,256]{1,0:T(8,128)}, u32[]{:S(2)}) copy-start(f32[256,256]{1,0:T(8,128)} %test_ref.1) | copy-start | bytes 786436
  14.0 0.8 %copy-start.2 = (f32[2,24,256]{2,1,0:T(8,128)S(1)}, f32[2,24,256]{2,1,0:T(8,128)}, u32[]{:S(2)}) copy-start(f32[2,24,256]{2,1,0:T(8,128)} %constant.24.clone.refs_3_) | copy-start | bytes 147460
  14.0 0.7 %copy-start.5 = (f32[64]{0:T(128)S(1)}, f32[64]{0:T(128)}, u32[]{:S(2)}) copy-start(f32[64]{0:T(128)} %param.6) | copy-start | bytes 772
  14.7 0.7 %copy-start.4 = (s32[1024]{0:T(1024)S(1)}, s32[1024]{0:T(1024)}, u32[]{:S(2)}) copy-start(s32[1024]{0:T(1024)} %param.7) | copy-start | bytes 12292
  23.9 1.3 %collective-permute-start.8 = (f32[136,128]{1,0:T(8,128)S(1)}, f32[136,128]{1,0:T(8,128)S(1)}, u32[]{:S(2)}, u32[]{:S(2)}) collective-permute-start(f32[136,128]{1,0:T(8,128)S(1)} %get-tuple-element.27), channel_id=1, source_target_pairs={{0,1},{1,0},{2,3},{3,2},{4,5},{5,4},{6,7},{7,6},{8,9},{9,8},{10,11... | collective-permute-start | bytes 208904 | tf_op jit(solution)/shard_map/ppermute | solution.py:56
  25.2 5.3 %collective-permute-start.11 = (f32[136,128]{1,0:T(8,128)S(1)}, f32[136,128]{1,0:T(8,128)S(1)}, u32[]{:S(2)}, u32[]{:S(2)}) collective-permute-start(f32[136,128]{1,0:T(8,128)S(1)} %add.30), channel_id=1, source_target_pairs={{0,18},{1,13},{2,16},{3,15},{4,22},{5,9},{6,20},{7,11},{8,26},{9,5... | collective-permute-start | bytes 208904 | tf_op jit(solution)/shard_map/ppermute | solution.py:56
  26.6 4.6 %collective-permute-start.10 = (f32[136,128]{1,0:T(8,128)S(1)}, f32[136,128]{1,0:T(8,128)S(1)}, u32[]{:S(2)}, u32[]{:S(2)}) collective-permute-start(f32[136,128]{1,0:T(8,128)S(1)} %add.30), channel_id=1, source_target_pairs={{0,16},{1,9},{2,18},{3,11},{4,20},{5,13},{6,22},{7,15},{8,24},{9,1... | collective-permute-start | bytes 208904 | tf_op jit(solution)/shard_map/ppermute | solution.py:56
  26.9 4.4 %collective-permute-start.9 = (f32[136,128]{1,0:T(8,128)S(1)}, f32[136,128]{1,0:T(8,128)S(1)}, u32[]{:S(2)}, u32[]{:S(2)}) collective-permute-start(f32[136,128]{1,0:T(8,128)S(1)} %add.30), channel_id=1, source_target_pairs={{0,2},{1,5},{2,0},{3,7},{4,6},{5,1},{6,4},{7,3},{8,10},{9,13},{10,... | collective-permute-start | bytes 208904 | tf_op jit(solution)/shard_map/ppermute | solution.py:56
  31.3 6.4 %collective-permute-start.14 = (f32[136,128]{1,0:T(8,128)S(1)}, f32[136,128]{1,0:T(8,128)S(1)}, u32[]{:S(2)}, u32[]{:S(2)}) collective-permute-start(f32[136,128]{1,0:T(8,128)S(1)} %add_add_fusion.1), channel_id=1, source_target_pairs={{0,12},{1,19},{2,14},{3,17},{4,8},{5,23},{6,10},{7,21},{8,4},{9,27... | collective-permute-start | bytes 208904 | tf_op jit(solution)/shard_map/ppermute | solution.py:56
  35.3 5.2 %collective-permute-start.13 = (f32[136,128]{1,0:T(8,128)S(1)}, f32[136,128]{1,0:T(8,128)S(1)}, u32[]{:S(2)}, u32[]{:S(2)}) collective-permute-start(f32[136,128]{1,0:T(8,128)S(1)} %add_add_fusion.1), channel_id=1, source_target_pairs={{0,8},{1,17},{2,10},{3,19},{4,12},{5,21},{6,14},{7,23},{8,0},{9,25... | collective-permute-start | bytes 208904 | tf_op jit(solution)/shard_map/ppermute | solution.py:56
  35.3 5.2 %collective-permute-start.12 = (f32[136,128]{1,0:T(8,128)S(1)}, f32[136,128]{1,0:T(8,128)S(1)}, u32[]{:S(2)}, u32[]{:S(2)}) collective-permute-start(f32[136,128]{1,0:T(8,128)S(1)} %add_add_fusion.1), channel_id=1, source_target_pairs={{0,4},{1,3},{2,6},{3,1},{4,0},{5,7},{6,2},{7,5},{8,12},{9,11},{10,... | collective-permute-start | bytes 208904 | tf_op jit(solution)/shard_map/ppermute | solution.py:56
  40.5 1.3 %collective-permute-start.15 = (f32[136,128]{1,0:T(8,128)S(1)}, f32[136,128]{1,0:T(8,128)S(1)}, u32[]{:S(2)}, u32[]{:S(2)}) collective-permute-start(f32[136,128]{1,0:T(8,128)S(1)} %add_add_fusion.part_ref), channel_id=1, source_target_pairs={{0,1},{1,0},{2,3},{3,2},{4,5},{5,4},{6,7},{7,6},{8,9},{9,8},{10,11... | collective-permute-start | bytes 208904 | tf_op jit(solution)/shard_map/ppermute | solution.py:56

commit v4 on v3

--- a/solution.py
+++ b/solution.py
@@ -110,37 +110,45 @@
     for n, ref in enumerate(quarter_refs):
         peer, q = divmod(n, len(QUARTERS))
         base = days_local * (peer + 1) + ((pts_place % len(QUARTERS)) ^ QUARTERS[q]) * size
-        table_ref[pl.ds(pl.multiple_of(base, size), size), :] = ref[...]
+        table_ref[pl.ds(pl.multiple_of(base, size), size), :] = -ref[...]
     bins = bin_ref[:, pl.ds(at, width)]
     count = thr_ref.shape[0]
     entry = lax.broadcasted_iota(jnp.int32, (count, width), 0)
     level = jnp.sum(jnp.where(entry == bins, thr_ref[...], 0.0), axis=0, keepdims=True)
+    level = jnp.broadcast_to(level, (SUB, width)).T[:, :1]
     series = [days_ref[:, pl.ds(at, width)]] + [r[...] for r in recv_refs]
     proj = nn(filt_ref[place], series[0])
     for k in range(1, tm_count):
         proj = proj + nn(filt_ref[place ^ k], series[k])
+    proj = proj.T
     excess = [
-        jnp.maximum(series[k] - tn(filt_ref[place ^ k], proj) - level, 0.0)
+        jnp.maximum(series[k].T - nn(proj, filt_ref[place ^ k]) - level, 0.0)
         for k in range(tm_count)
     ]
-    sketch = tn(jnp.concatenate(excess, 0), table_ref[...])
+    sketch = nn(excess[0], table_ref[:days_local, :])
+    for k in range(1, tm_count):
+        sketch = sketch - nn(excess[k], table_ref[k * days_local:(k + 1) * days_local, :])
     sketch_ref[...] = sketch
     if not with_cross:
         return
     whole = jnp.concatenate([r[...] for r in earlier_refs] + [sketch], 0)
+    tile = whole.shape[1] // 2
     cross = tn(whole, whole)
+    top, below = cross[:tile, :tile], cross[tile:, :]
     for ref in acc_refs:
-        cross = cross + ref[...]
+        top = top + ref[:tile, :tile]
+        below = below + ref[tile:, :]
     if not last:
-        outs[0][...] = cross
+        outs[0][:tile, :tile] = top
+        outs[0][:tile, tile:] = jnp.zeros((tile, tile), jnp.float32)
+        outs[0][tile:, :] = below
         return
     kept_ref, sent_ref = outs
-    tile = cross.shape[0] // 2
     row = lax.broadcasted_iota(jnp.int32, (tile, tile), 0)
     col = lax.broadcasted_iota(jnp.int32, (tile, tile), 1)
-    second = cross[tile:, tile:]
-    ends = jnp.where(row >= col, cross[:tile, :tile], second)
-    side = cross[tile:, :tile]
+    second = below[:, tile:]
+    ends = jnp.where(row >= col, top, second)
+    side = below[:, :tile]
     diag = jnp.broadcast_to(
         jnp.sum(jnp.where(row == col, second, 0.0), axis=0, keepdims=True), (SUB, tile)
     )
@@ -170,10 +178,11 @@
     tile = count * SUB
     lane = lax.broadcasted_iota(jnp.int32, (SUB, tile), 1)
     row = lax.broadcasted_iota(jnp.int32, (SUB, tile), 0)
-    upper, inverse, pending = [], [], []
+    upper, inverse, pending, corners = [], [], [], []
     for i in range(count):
         first = SUB * i
         own = blocks[i]
+        corner = jnp.zeros((SUB, tile), jnp.float32)
         end = min(count, (i // group + 1) * group)
         if i % group == 0:
             ahead = [over_lanes(own, first + k, tile) for k in range(SUB)]
@@ -192,9 +201,10 @@
         for j in range(SUB):
             line = [over_rows(cols[k], j, tile) for k in range(j, SUB)]
             s = lax.rsqrt(line[0])
-            for k in range(j, SUB):
+            for k in range(j + 1, SUB):
                 e[j, k] = line[k - j] * s
             down = cols[j] * s
+            corner = jnp.where(lane == first + j, down, corner)
             for k in range(j + 1, SUB):
                 cols[k] = cols[k] - down * e[j, k]
             rows[j] = rows[j] * s
@@ -211,16 +221,12 @@
         for t in later:
             update = tree([later[t][j] * rows[j] for j in range(SUB)])
             blocks[t] = jnp.where(inside, 0.0, blocks[t]) - update
-        up = jnp.zeros((SUB, tile), jnp.float32)
-        full = up
-        for j in range(SUB):
-            line = jnp.where(lane >= first + SUB, rows[j], 0.0)
-            for k in range(j, SUB):
-                line = jnp.where(lane == first + k, e[j, k], line)
-            up = jnp.where(row == j, line, up)
+        full = rows[0]
+        for j in range(1, SUB):
             full = jnp.where(row == j, rows[j], full)
+        corners.append(corner)
         pending.append(jnp.where((lane >= first + SUB) & (lane < SUB * end), 0.0, full))
-        upper.append(up)
+        upper.append(jnp.where(lane >= first + SUB, full, 0.0))
         inverse.append(jnp.where(lane < first + SUB, full, 0.0))
         if i + 1 == end < count:
             done = jnp.concatenate(pending, 0)
@@ -231,7 +237,12 @@
             for t in range(end, count):
                 at = SUB * t - rest
                 blocks[t] = jnp.where(here, 0.0, blocks[t]) - update[at:at + SUB, :]
-    return jnp.concatenate(upper, 0), jnp.concatenate(inverse, 0)
+    across = lax.broadcasted_iota(jnp.int32, (tile, tile), 1)
+    along = lax.broadcasted_iota(jnp.int32, (tile, tile), 0)
+    corners = jnp.concatenate(corners, 0).T
+    inner = (across >= along) & (across // SUB == along // SUB)
+    upper = jnp.where(inner, corners, jnp.concatenate(upper, 0))
+    return upper, jnp.concatenate(inverse, 0)
 
 
 def back_kernel(points_total, chunks, part_ref, other_ref, *refs):

time: 49.3 us -> 48.9 us (level)
  Pallas kernels: 13 us -> 12.1 us
  waiting for transfers between devices: 13.2 us -> 13.8 us
    pallas_call x4, Pallas kernels: 5.73 us -> 4.88 us  [on_device(): pl.pallas_call(functools.partial(front_kernel, start, width, own_rows, tm...]
    ppermute x16, waiting for transfers between devices: 13.2 us -> 13.8 us  [swap(): lax.ppermute(value, AXES, [(i, i ^ (odd_bit if i % 2 else bit)) for i in...]
  transfers between devices with their start and end apart: 16 -> 16, of which waited for: 11 -> 11; matrix products, arithmetic and copies ran while one was open for 0% -> 0% of each run, Pallas kernels for 8% -> 7%
where the time goes in v4:
time: 48.9 us; the launch traced here: 48.6 us
  starting transfers between devices  17.6 us (36%)
  waiting for transfers between devices  13.8 us (28%)
  Pallas kernels  12.1 us (25%)
  local copies, waits for them, and re-layouts  4.34 us (9%)
  between operations  0.76 us (2%)
    ppermute x16, starting transfers between devices, swap(): lax.ppermute(value, AXES, [(i, i ^ (odd_bit if i % 2 else bit)) for i in...  17.6 us
    ppermute x16, waiting for transfers between devices, swap(): lax.ppermute(value, AXES, [(i, i ^ (odd_bit if i % 2 else bit)) for i in...  13.8 us
    pallas_call x1, Pallas kernels, on_device(): pl.pallas_call(functools.partial(back_kernel, points_total, len(sketches)...  7.08 us
    pallas_call x4, Pallas kernels, on_device(): pl.pallas_call(functools.partial(front_kernel, start, width, own_rows, tm...  4.88 us
    unnamed x12, local copies, waits for them, and re-layouts  3.4 us
  transfers between devices with their start and end apart: 16, of which 11 were waited for; matrix products, arithmetic and copies ran while one was open for 0% of the time, Pallas kernels for 7%

profile of v4, /device:TPU:0, one launch (start us, length us, event | category | flops | bytes accessed | tf_op | source)
XLA Modules:
  0.0 48.6 jit_solution(3535964596336189164)
XLA Ops:
  0.6 0.8 %constant_dynamic-slice_fusion = f32[64,256]{1,0:T(8,128)S(1)} fusion(f32[256,256]{1,0:T(8,128)} %test_ref.1, s32[]{:T(128)S(6)} %select_n.11), kind=kLoop, calls=%fused_computation.2 | loop fusion | bytes 131076 | tf_op jit(solution)/shard_map/dynamic_slice | solution.py:326
  1.5 3.0 %collective-permute-start.4 = (f32[64,256]{1,0:T(8,128)S(1)}, f32[64,256]{1,0:T(8,128)S(1)}, u32[]{:S(2)}, u32[]{:S(2)}) collective-permute-start(f32[64,256]{1,0:T(8,128)S(1)} %constant_dynamic-slice_fusion), channel_id=1, source_target_pairs={{0,16},{1,17},{2,18},{3,19},{4,20},{5,21},{6,22},{7,23},{8,24},{9,... | collective-permute-start | bytes 196616 | tf_op jit(solution)/shard_map/ppermute | solution.py:56
  4.5 0.0 copy-start
  4.5 1.2 %copy-done = f32[256,1024]{1,0:T(8,128)S(1)} copy-done((f32[256,1024]{1,0:T(8,128)S(1)}, f32[256,1024]{1,0:T(8,128)}, u32[]{:S(2)}) %copy-start) | copy-done | bytes 1048600
  5.7 0.1 cut.1
  5.8 0.9 %collective-permute-done.4.refs_6_ = f32[64,256]{1,0:T(8,128)S(1)} collective-permute-done((f32[64,256]{1,0:T(8,128)S(1)}, f32[64,256]{1,0:T(8,128)S(1)}, u32[]{:S(2)}, u32[]{:S(2)}) %collective-permute-start.4) | collective-permute-done | bytes 65568 | tf_op jit(solution)/shard_map/ppermute | solution.py:56
  6.7 2.0 %collective-permute-start.6 = (f32[64,256]{1,0:T(8,128)S(1)}, f32[64,256]{1,0:T(8,128)S(1)}, u32[]{:S(2)}, u32[]{:S(2)}) collective-permute-start(f32[64,256]{1,0:T(8,128)S(1)} %collective-permute-done.4.refs_6_), channel_id=1, source_target_pairs={{0,2},{1,3},{2,0},{3,1},{4,6},{5,7},{6,4},{7,5},{8,10},{9,11},{10,... | collective-permute-start | bytes 196616 | tf_op jit(solution)/shard_map/ppermute | solution.py:56
  8.7 1.5 %collective-permute-start.3 = (f32[256,128]{1,0:T(8,128)S(1)}, f32[256,128]{1,0:T(8,128)S(1)}, u32[]{:S(2)}, u32[]{:S(2)}) collective-permute-start(f32[256,128]{1,0:T(8,128)S(1)} %get-tuple-element.20), channel_id=1, source_target_pairs={{0,16},{1,17},{2,18},{3,19},{4,20},{5,21},{6,22},{7,23},{8,24},{9,... | collective-permute-start | bytes 393224 | tf_op jit(solution)/shard_map/ppermute | solution.py:56
  10.2 0.0 collective-permute-start.5
  10.3 0.5 %collective-permute-start.2 = (f32[256,128]{1,0:T(8,128)S(1)}, f32[256,128]{1,0:T(8,128)S(1)}, u32[]{:S(2)}, u32[]{:S(2)}) collective-permute-start(f32[256,128]{1,0:T(8,128)S(1)} %get-tuple-element.19), channel_id=1, source_target_pairs={{0,16},{1,17},{2,18},{3,19},{4,20},{5,21},{6,22},{7,23},{8,24},{9,... | collective-permute-start | bytes 393224 | tf_op jit(solution)/shard_map/ppermute | solution.py:56
  10.8 1.5 %collective-permute-start.1 = (f32[256,128]{1,0:T(8,128)S(1)}, f32[256,128]{1,0:T(8,128)S(1)}, u32[]{:S(2)}, u32[]{:S(2)}) collective-permute-start(f32[256,128]{1,0:T(8,128)S(1)} %get-tuple-element.18), channel_id=1, source_target_pairs={{0,16},{1,17},{2,18},{3,19},{4,20},{5,21},{6,22},{7,23},{8,24},{9,... | collective-permute-start | bytes 393224 | tf_op jit(solution)/shard_map/ppermute | solution.py:56
  12.3 0.0 collective-permute-done.6.refs_8_
  12.3 0.0 collective-permute-start.7
  12.3 0.0 collective-permute-done.5.refs_7_
  12.3 0.7 %collective-permute-start = (f32[256,128]{1,0:T(8,128)S(1)}, f32[256,128]{1,0:T(8,128)S(1)}, u32[]{:S(2)}, u32[]{:S(2)}) collective-permute-start(f32[256,128]{1,0:T(8,128)S(1)} %get-tuple-element.17), channel_id=1, source_target_pairs={{0,16},{1,17},{2,18},{3,19},{4,20},{5,21},{6,22},{7,23},{8,24},{9,... | collective-permute-start | bytes 393224 | tf_op jit(solution)/shard_map/ppermute | solution.py:56
  13.0 0.9 %copy-done.3 = f32[256,256]{1,0:T(8,128)S(1)} copy-done((f32[256,256]{1,0:T(8,128)S(1)}, f32[256,256]{1,0:T(8,128)}, u32[]{:S(2)}) %copy-start.3) | copy-done | bytes 262168
  14.0 0.0 copy-start.5
  14.0 0.6 %copy-done.5 = f32[64]{0:T(128)S(1)} copy-done((f32[64]{0:T(128)S(1)}, f32[64]{0:T(128)}, u32[]{:S(2)}) %copy-start.5) | copy-done | bytes 280
  14.7 0.1 copy.10.refs_1_
  14.8 0.0 collective-permute-done.3.refs_5_
  14.8 0.0 collective-permute-done.7.refs_9_
  14.8 0.0 copy-done.1
  14.8 0.0 copy-done.2
  14.8 0.6 %copy-done.4 = s32[1024]{0:T(1024)S(1)} copy-done((s32[1024]{0:T(1024)S(1)}, s32[1024]{0:T(1024)}, u32[]{:S(2)}) %copy-start.4) | copy-done | bytes 4120
  15.4 1.0 %shard_map.68.refs_10_.refs_0_ = f32[128,256]{1,0:T(8,128)S(1)} custom-call(f32[256,1024]{1,0:T(8,128)S(1)} %copy-done.1, f32[64,1]{1,0:T(8,128)S(1)} %copy.10.refs_1_, s32[1,1024]{1,0:T(1,128)S(1)} %bitcast.2, f32[2,24,256]{2,1,0:T(8,128)S(1)} %copy-done.2, f32[256,256]{1,0:T(8,128)S(1)} %hold.1.refs_4_, f32[256,128]{1,0:T(8,128)S(1)} %collective-permute-done.3.refs_5_, ...), custom_call_target="tpu_custom_call" | custom-call | flops 301989888 | bytes 786432 | tf_op jit(solution)/shard_map/pallas_call | solution.py:381
  16.4 0.5 %collective-permute-done.2.refs_5_ = f32[256,128]{1,0:T(8,128)S(1)} collective-permute-done((f32[256,128]{1,0:T(8,128)S(1)}, f32[256,128]{1,0:T(8,128)S(1)}, u32[]{:S(2)}, u32[]{:S(2)}) %collective-permute-start.2) | collective-permute-done | bytes 131104 | tf_op jit(solution)/shard_map/ppermute | solution.py:56
  16.9 1.4 %shard_map.69 = (f32[128,256]{1,0:T(8,128)S(1)}, f32[256,256]{1,0:T(8,128)S(1)}) custom-call(f32[256,1024]{1,0:T(8,128)S(1)} %copy-done.1, f32[64,1]{1,0:T(8,128)S(1)} %copy.10.refs_1_, s32[1,1024]{1,0:T(1,128)S(1)} %bitcast.3, f32[2,24,256]{2,1,0:T(8,128)S(1)} %copy-done.2, f32[256,256]{1,0:T(8,128)S(1)} %hold.1.refs_4_, ...), custom_call_target="tpu_custom_call" | custom-call | flops 301989888 | bytes 786432 | tf_op jit(solution)/shard_map/pallas_call | solution.py:381
  18.3 1.4 %collective-permute-done.1.refs_5_ = f32[256,128]{1,0:T(8,128)S(1)} collective-permute-done((f32[256,128]{1,0:T(8,128)S(1)}, f32[256,128]{1,0:T(8,128)S(1)}, u32[]{:S(2)}, u32[]{:S(2)}) %collective-permute-start.1) | collective-permute-done | bytes 131104 | tf_op jit(solution)/shard_map/ppermute | solution.py:56
  19.7 1.0 %shard_map.70.refs_10_.refs_2_ = f32[128,256]{1,0:T(8,128)S(1)} custom-call(f32[256,1024]{1,0:T(8,128)S(1)} %copy-done.1, f32[64,1]{1,0:T(8,128)S(1)} %copy.10.refs_1_, s32[1,1024]{1,0:T(1,128)S(1)} %bitcast.4, f32[2,24,256]{2,1,0:T(8,128)S(1)} %copy-done.2, f32[256,256]{1,0:T(8,128)S(1)} %hold.1.refs_4_, f32[256,128]{1,0:T(8,128)S(1)} %collective-permute-done.1.refs_5_, ...), custom_call_target="tpu_custom_call" | custom-call | flops 301989888 | bytes 786432 | tf_op jit(solution)/shard_map/pallas_call | solution.py:381
  20.7 1.4 %collective-permute-done.refs_5_ = f32[256,128]{1,0:T(8,128)S(1)} collective-permute-done((f32[256,128]{1,0:T(8,128)S(1)}, f32[256,128]{1,0:T(8,128)S(1)}, u32[]{:S(2)}, u32[]{:S(2)}) %collective-permute-start) | collective-permute-done | bytes 131104 | tf_op jit(solution)/shard_map/ppermute | solution.py:56
  22.1 1.4 %shard_map.71 = (f32[128,256]{1,0:T(8,128)S(1)}, f32[136,128]{1,0:T(8,128)S(1)}, f32[136,128]{1,0:T(8,128)S(1)}) custom-call(f32[256,1024]{1,0:T(8,128)S(1)} %copy-done.1, f32[64,1]{1,0:T(8,128)S(1)} %copy.10.refs_1_, s32[1,1024]{1,0:T(1,128)S(1)} %bitcast.5, f32[2,24,256]{2,1,0:T(8,128)S(1)} %copy-done.2, f32[256,256]{1,0:T(8,128)S(1)} %hold.1.refs_4_, ...), custom_call_target="tpu_custom_call" | custom-call | flops 301989888 | bytes 786432 | tf_op jit(solution)/shard_map/pallas_call | solution.py:381
  23.6 0.1 collective-permute-start.8
  23.6 1.2 %collective-permute-done.8 = f32[136,128]{1,0:T(8,128)S(1)} collective-permute-done((f32[136,128]{1,0:T(8,128)S(1)}, f32[136,128]{1,0:T(8,128)S(1)}, u32[]{:S(2)}, u32[]{:S(2)}) %collective-permute-start.8) | collective-permute-done | bytes 69664 | tf_op jit(solution)/shard_map/ppermute | solution.py:56
  24.9 1.4 %collective-permute-start.11 = (f32[136,128]{1,0:T(8,128)S(1)}, f32[136,128]{1,0:T(8,128)S(1)}, u32[]{:S(2)}, u32[]{:S(2)}) collective-permute-start(f32[136,128]{1,0:T(8,128)S(1)} %add.30), channel_id=1, source_target_pairs={{0,18},{1,13},{2,16},{3,15},{4,22},{5,9},{6,20},{7,11},{8,26},{9,5... | collective-permute-start | bytes 208904 | tf_op jit(solution)/shard_map/ppermute | solution.py:56
  26.3 0.3 collective-permute-start.10
  26.6 1.8 %collective-permute-start.9 = (f32[136,128]{1,0:T(8,128)S(1)}, f32[136,128]{1,0:T(8,128)S(1)}, u32[]{:S(2)}, u32[]{:S(2)}) collective-permute-start(f32[136,128]{1,0:T(8,128)S(1)} %add.30), channel_id=1, source_target_pairs={{0,2},{1,5},{2,0},{3,7},{4,6},{5,1},{6,4},{7,3},{8,10},{9,13},{10,... | collective-permute-start | bytes 208904 | tf_op jit(solution)/shard_map/ppermute | solution.py:56
  28.4 1.8 %collective-permute-done.11 = f32[136,128]{1,0:T(8,128)S(1)} collective-permute-done((f32[136,128]{1,0:T(8,128)S(1)}, f32[136,128]{1,0:T(8,128)S(1)}, u32[]{:S(2)}, u32[]{:S(2)}) %collective-permute-start.11) | collective-permute-done | bytes 69664 | tf_op jit(solution)/shard_map/ppermute | solution.py:56
  30.2 0.7 %collective-permute-done.10 = f32[136,128]{1,0:T(8,128)S(1)} collective-permute-done((f32[136,128]{1,0:T(8,128)S(1)}, f32[136,128]{1,0:T(8,128)S(1)}, u32[]{:S(2)}, u32[]{:S(2)}) %collective-permute-start.10) | collective-permute-done | bytes 69664 | tf_op jit(solution)/shard_map/ppermute | solution.py:56
  30.9 0.1 collective-permute-done.9
  31.0 4.0 %collective-permute-start.14 = (f32[136,128]{1,0:T(8,128)S(1)}, f32[136,128]{1,0:T(8,128)S(1)}, u32[]{:S(2)}, u32[]{:S(2)}) collective-permute-start(f32[136,128]{1,0:T(8,128)S(1)} %add_add_fusion.1), channel_id=1, source_target_pairs={{0,12},{1,19},{2,14},{3,17},{4,8},{5,23},{6,10},{7,21},{8,4},{9,27... | collective-permute-start | bytes 208904 | tf_op jit(solution)/shard_map/ppermute | solution.py:56
  35.0 0.0 collective-permute-start.13
  35.0 0.6 %collective-permute-start.12 = (f32[136,128]{1,0:T(8,128)S(1)}, f32[136,128]{1,0:T(8,128)S(1)}, u32[]{:S(2)}, u32[]{:S(2)}) collective-permute-start(f32[136,128]{1,0:T(8,128)S(1)} %add_add_fusion.1), channel_id=1, source_target_pairs={{0,4},{1,3},{2,6},{3,1},{4,0},{5,7},{6,2},{7,5},{8,12},{9,11},{10,... | collective-permute-start | bytes 208904 | tf_op jit(solution)/shard_map/ppermute | solution.py:56
  35.6 1.7 %collective-permute-done.14 = f32[136,128]{1,0:T(8,128)S(1)} collective-permute-done((f32[136,128]{1,0:T(8,128)S(1)}, f32[136,128]{1,0:T(8,128)S(1)}, u32[]{:S(2)}, u32[]{:S(2)}) %collective-permute-start.14) | collective-permute-done | bytes 69664 | tf_op jit(solution)/shard_map/ppermute | solution.py:56
  37.3 2.8 %collective-permute-done.13 = f32[136,128]{1,0:T(8,128)S(1)} collective-permute-done((f32[136,128]{1,0:T(8,128)S(1)}, f32[136,128]{1,0:T(8,128)S(1)}, u32[]{:S(2)}, u32[]{:S(2)}) %collective-permute-start.13) | collective-permute-done | bytes 69664 | tf_op jit(solution)/shard_map/ppermute | solution.py:56
  40.2 0.0 collective-permute-done.12
  40.2 0.1 collective-permute-start.15
  40.3 1.2 %collective-permute-done.15.other_ref = f32[136,128]{1,0:T(8,128)S(1)} collective-permute-done((f32[136,128]{1,0:T(8,128)S(1)}, f32[136,128]{1,0:T(8,128)S(1)}, u32[]{:S(2)}, u32[]{:S(2)}) %collective-permute-start.15) | collective-permute-done | bytes 69664 | tf_op jit(solution)/shard_map/ppermute | solution.py:56
  41.5 7.1 %back.1 = (f32[512,256]{1,0:T(8,128)}, f32[256,256]{1,0:T(8,128)}) custom-call(f32[136,128]{1,0:T(8,128)S(1)} %add_add_fusion.part_ref, f32[136,128]{1,0:T(8,128)S(1)} %collective-permute-done.15.other_ref, f32[128,256]{1,0:T(8,128)S(1)} %shard_map.68.refs_10_.refs_0_, f32[128,256]{1,0:T(8,128)S(1)} %get-tuple-element.29.refs_1_, ...), custom_call_target="tpu_custom_call" | custom-call | tf_op jit(solution)/shard_map/back/pallas_call | solution.py:427
  (8 shorter events, 0.1 us)
Async XLA Ops:
  1.5 5.2 %collective-permute-start.4 = (f32[64,256]{1,0:T(8,128)S(1)}, f32[64,256]{1,0:T(8,128)S(1)}, u32[]{:S(2)}, u32[]{:S(2)}) collective-permute-start(f32[64,256]{1,0:T(8,128)S(1)} %constant_dynamic-slice_fusion), channel_id=1, source_target_pairs={{0,16},{1,17},{2,18},{3,19},{4,20},{5,21},{6,22},{7,23},{8,24},{9,... | collective-permute-start | bytes 196616 | tf_op jit(solution)/shard_map/ppermute | solution.py:56
  4.5 1.2 %copy-start = (f32[256,1024]{1,0:T(8,128)S(1)}, f32[256,1024]{1,0:T(8,128)}, u32[]{:S(2)}) copy-start(f32[256,1024]{1,0:T(8,128)} %refs_0_.7) | copy-start | bytes 3145732
  5.7 9.1 %copy-start.1 = (f32[256,1024]{1,0:T(8,128)S(1)}, f32[256,1024]{1,0:T(8,128)}, u32[]{:S(2)}) copy-start(f32[256,1024]{1,0:T(8,128)} %refs_0_.7) | copy-start | bytes 3145732
  6.7 5.5 %collective-permute-start.6 = (f32[64,256]{1,0:T(8,128)S(1)}, f32[64,256]{1,0:T(8,128)S(1)}, u32[]{:S(2)}, u32[]{:S(2)}) collective-permute-start(f32[64,256]{1,0:T(8,128)S(1)} %collective-permute-done.4.refs_6_), channel_id=1, source_target_pairs={{0,2},{1,3},{2,0},{3,1},{4,6},{5,7},{6,4},{7,5},{8,10},{9,11},{10,... | collective-permute-start | bytes 196616 | tf_op jit(solution)/shard_map/ppermute | solution.py:56
  8.7 6.0 %collective-permute-start.3 = (f32[256,128]{1,0:T(8,128)S(1)}, f32[256,128]{1,0:T(8,128)S(1)}, u32[]{:S(2)}, u32[]{:S(2)}) collective-permute-start(f32[256,128]{1,0:T(8,128)S(1)} %get-tuple-element.20), channel_id=1, source_target_pairs={{0,16},{1,17},{2,18},{3,19},{4,20},{5,21},{6,22},{7,23},{8,24},{9,... | collective-permute-start | bytes 393224 | tf_op jit(solution)/shard_map/ppermute | solution.py:56
  10.2 2.0 %collective-permute-start.5 = (f32[64,256]{1,0:T(8,128)S(1)}, f32[64,256]{1,0:T(8,128)S(1)}, u32[]{:S(2)}, u32[]{:S(2)}) collective-permute-start(f32[64,256]{1,0:T(8,128)S(1)} %collective-permute-done.4.refs_6_), channel_id=1, source_target_pairs={{0,1},{1,0},{2,3},{3,2},{4,5},{5,4},{6,7},{7,6},{8,9},{9,8},{10,11... | collective-permute-start | bytes 196616 | tf_op jit(solution)/shard_map/ppermute | solution.py:56
  10.3 6.6 %collective-permute-start.2 = (f32[256,128]{1,0:T(8,128)S(1)}, f32[256,128]{1,0:T(8,128)S(1)}, u32[]{:S(2)}, u32[]{:S(2)}) collective-permute-start(f32[256,128]{1,0:T(8,128)S(1)} %get-tuple-element.19), channel_id=1, source_target_pairs={{0,16},{1,17},{2,18},{3,19},{4,20},{5,21},{6,22},{7,23},{8,24},{9,... | collective-permute-start | bytes 393224 | tf_op jit(solution)/shard_map/ppermute | solution.py:56
  10.8 8.9 %collective-permute-start.1 = (f32[256,128]{1,0:T(8,128)S(1)}, f32[256,128]{1,0:T(8,128)S(1)}, u32[]{:S(2)}, u32[]{:S(2)}) collective-permute-start(f32[256,128]{1,0:T(8,128)S(1)} %get-tuple-element.18), channel_id=1, source_target_pairs={{0,16},{1,17},{2,18},{3,19},{4,20},{5,21},{6,22},{7,23},{8,24},{9,... | collective-permute-start | bytes 393224 | tf_op jit(solution)/shard_map/ppermute | solution.py:56
  12.3 2.5 %collective-permute-start.7 = (f32[64,256]{1,0:T(8,128)S(1)}, f32[64,256]{1,0:T(8,128)S(1)}, u32[]{:S(2)}, u32[]{:S(2)}) collective-permute-start(f32[64,256]{1,0:T(8,128)S(1)} %collective-permute-done.6.refs_8_), channel_id=1, source_target_pairs={{0,1},{1,0},{2,3},{3,2},{4,5},{5,4},{6,7},{7,6},{8,9},{9,8},{10,11... | collective-permute-start | bytes 196616 | tf_op jit(solution)/shard_map/ppermute | solution.py:56
  12.3 9.8 %collective-permute-start = (f32[256,128]{1,0:T(8,128)S(1)}, f32[256,128]{1,0:T(8,128)S(1)}, u32[]{:S(2)}, u32[]{:S(2)}) collective-permute-start(f32[256,128]{1,0:T(8,128)S(1)} %get-tuple-element.17), channel_id=1, source_target_pairs={{0,16},{1,17},{2,18},{3,19},{4,20},{5,21},{6,22},{7,23},{8,24},{9,... | collective-permute-start | bytes 393224 | tf_op jit(solution)/shard_map/ppermute | solution.py:56
  13.0 0.9 %copy-start.3 = (f32[256,256]{1,0:T(8,128)S(1)}, f32[256,256]{1,0:T(8,128)}, u32[]{:S(2)}) copy-start(f32[256,256]{1,0:T(8,128)} %test_ref.1) | copy-start | bytes 786436
  14.0 0.8 %copy-start.2 = (f32[2,24,256]{2,1,0:T(8,128)S(1)}, f32[2,24,256]{2,1,0:T(8,128)}, u32[]{:S(2)}) copy-start(f32[2,24,256]{2,1,0:T(8,128)} %constant.24.clone.refs_3_) | copy-start | bytes 147460
  14.0 0.7 %copy-start.5 = (f32[64]{0:T(128)S(1)}, f32[64]{0:T(128)}, u32[]{:S(2)}) copy-start(f32[64]{0:T(128)} %param.6) | copy-start | bytes 772
  14.7 0.7 %copy-start.4 = (s32[1024]{0:T(1024)S(1)}, s32[1024]{0:T(1024)}, u32[]{:S(2)}) copy-start(s32[1024]{0:T(1024)} %param.7) | copy-start | bytes 12292
  23.6 1.3 %collective-permute-start.8 = (f32[136,128]{1,0:T(8,128)S(1)}, f32[136,128]{1,0:T(8,128)S(1)}, u32[]{:S(2)}, u32[]{:S(2)}) collective-permute-start(f32[136,128]{1,0:T(8,128)S(1)} %get-tuple-element.27), channel_id=1, source_target_pairs={{0,1},{1,0},{2,3},{3,2},{4,5},{5,4},{6,7},{7,6},{8,9},{9,8},{10,11... | collective-permute-start | bytes 208904 | tf_op jit(solution)/shard_map/ppermute | solution.py:56
  24.9 5.3 %collective-permute-start.11 = (f32[136,128]{1,0:T(8,128)S(1)}, f32[136,128]{1,0:T(8,128)S(1)}, u32[]{:S(2)}, u32[]{:S(2)}) collective-permute-start(f32[136,128]{1,0:T(8,128)S(1)} %add.30), channel_id=1, source_target_pairs={{0,18},{1,13},{2,16},{3,15},{4,22},{5,9},{6,20},{7,11},{8,26},{9,5... | collective-permute-start | bytes 208904 | tf_op jit(solution)/shard_map/ppermute | solution.py:56
  26.3 4.7 %collective-permute-start.10 = (f32[136,128]{1,0:T(8,128)S(1)}, f32[136,128]{1,0:T(8,128)S(1)}, u32[]{:S(2)}, u32[]{:S(2)}) collective-permute-start(f32[136,128]{1,0:T(8,128)S(1)} %add.30), channel_id=1, source_target_pairs={{0,16},{1,9},{2,18},{3,11},{4,20},{5,13},{6,22},{7,15},{8,24},{9,1... | collective-permute-start | bytes 208904 | tf_op jit(solution)/shard_map/ppermute | solution.py:56
  26.6 4.4 %collective-permute-start.9 = (f32[136,128]{1,0:T(8,128)S(1)}, f32[136,128]{1,0:T(8,128)S(1)}, u32[]{:S(2)}, u32[]{:S(2)}) collective-permute-start(f32[136,128]{1,0:T(8,128)S(1)} %add.30), channel_id=1, source_target_pairs={{0,2},{1,5},{2,0},{3,7},{4,6},{5,1},{6,4},{7,3},{8,10},{9,13},{10,... | collective-permute-start | bytes 208904 | tf_op jit(solution)/shard_map/ppermute | solution.py:56
  31.0 6.3 %collective-permute-start.14 = (f32[136,128]{1,0:T(8,128)S(1)}, f32[136,128]{1,0:T(8,128)S(1)}, u32[]{:S(2)}, u32[]{:S(2)}) collective-permute-start(f32[136,128]{1,0:T(8,128)S(1)} %add_add_fusion.1), channel_id=1, source_target_pairs={{0,12},{1,19},{2,14},{3,17},{4,8},{5,23},{6,10},{7,21},{8,4},{9,27... | collective-permute-start | bytes 208904 | tf_op jit(solution)/shard_map/ppermute | solution.py:56
  35.0 5.2 %collective-permute-start.13 = (f32[136,128]{1,0:T(8,128)S(1)}, f32[136,128]{1,0:T(8,128)S(1)}, u32[]{:S(2)}, u32[]{:S(2)}) collective-permute-start(f32[136,128]{1,0:T(8,128)S(1)} %add_add_fusion.1), channel_id=1, source_target_pairs={{0,8},{1,17},{2,10},{3,19},{4,12},{5,21},{6,14},{7,23},{8,0},{9,25... | collective-permute-start | bytes 208904 | tf_op jit(solution)/shard_map/ppermute | solution.py:56
  35.0 5.2 %collective-permute-start.12 = (f32[136,128]{1,0:T(8,128)S(1)}, f32[136,128]{1,0:T(8,128)S(1)}, u32[]{:S(2)}, u32[]{:S(2)}) collective-permute-start(f32[136,128]{1,0:T(8,128)S(1)} %add_add_fusion.1), channel_id=1, source_target_pairs={{0,4},{1,3},{2,6},{3,1},{4,0},{5,7},{6,2},{7,5},{8,12},{9,11},{10,... | collective-permute-start | bytes 208904 | tf_op jit(solution)/shard_map/ppermute | solution.py:56
  40.2 1.3 %collective-permute-start.15 = (f32[136,128]{1,0:T(8,128)S(1)}, f32[136,128]{1,0:T(8,128)S(1)}, u32[]{:S(2)}, u32[]{:S(2)}) collective-permute-start(f32[136,128]{1,0:T(8,128)S(1)} %add_add_fusion.part_ref), channel_id=1, source_target_pairs={{0,1},{1,0},{2,3},{3,2},{4,5},{5,4},{6,7},{7,6},{8,9},{9,8},{10,11... | collective-permute-start | bytes 208904 | tf_op jit(solution)/shard_map/ppermute | solution.py:56

commit v5 on v4

--- a/solution.py
+++ b/solution.py
@@ -172,7 +172,7 @@
     return terms[0]
 
 
-def panel(blocks, group):
+def panel(blocks, group, hooks):
     count = len(blocks)
     blocks = list(blocks)
     tile = count * SUB
@@ -237,6 +237,8 @@
             for t in range(end, count):
                 at = SUB * t - rest
                 blocks[t] = jnp.where(here, 0.0, blocks[t]) - update[at:at + SUB, :]
+        if i in hooks:
+            hooks[i](inverse)
     across = lax.broadcasted_iota(jnp.int32, (tile, tile), 1)
     along = lax.broadcasted_iota(jnp.int32, (tile, tile), 0)
     corners = jnp.concatenate(corners, 0).T
@@ -267,31 +269,40 @@
         copies.append(pltpu.make_async_copy(src, dst, sem.at[len(copies)]))
         copies[-1].start()
 
-    up, inv1 = panel(split(jnp.where(row >= col, ends, ends_t)), group)
-    factor_ref[:tile, :tile] = up
-    factor_ref[tile:, :tile] = jnp.zeros((tile, tile), jnp.float32)
-    right = nn(inv1, side_t)
-    right_t = nt(side, inv1)
-    factor_ref[:tile, tile:] = right
-    rest = jnp.where(row < col, ends, jnp.where(row == col, diag, ends_t)) - nn(right_t, right)
-    middle, at = [], 0
-    for ref in sketch_refs:
-        size = ref.shape[0]
-        left = nt(ref[:, :tile], inv1)
-        basis_ref[at:at + size, :tile] = left
-        middle.append(ref[:, tile:] - nn(left, right))
-        at += size
-    put(factor_ref.at[:tile, :], factor_out.at[:tile, :])
-    put(basis_ref.at[:, :tile], basis_out.at[:, :tile])
-    up, inv2 = panel(split(rest), group)
-    factor_ref[tile:, tile:] = up
+    right = []
+    rest = [jnp.where(row < col, ends, jnp.where(row == col, diag, ends_t))]
+
+    def reduce_rest(inverse):
+        inverse = jnp.concatenate(inverse[len(right) * group:(len(right) + 1) * group], 0)
+        right.append(nn(inverse, side_t))
+        rest.append(rest[-1] - nn(nt(side, inverse), right[-1]))
+
+    last = tile // SUB - 1
+    hooks = {min(last, end + 1): reduce_rest for end in range(group - 1, last, group)}
+    hooks[last] = reduce_rest
+    up, inv1 = panel(split(jnp.where(row >= col, ends, ends_t)), group, hooks)
+    right = jnp.concatenate(right, 0)
+    middle = []
+
+    def first_half(_):
+        factor_ref[:tile, :tile] = up
+        factor_ref[tile:, :tile] = jnp.zeros((tile, tile), jnp.float32)
+        factor_ref[:tile, tile:] = right
+        sketch = jnp.concatenate([ref[...] for ref in sketch_refs], 0)
+        left = nt(sketch[:, :tile], inv1)
+        basis_ref[:, :tile] = left
+        middle.append(sketch[:, tile:] - nn(left, right))
+        put(factor_ref.at[:tile, :], factor_out.at[:tile, :])
+        put(basis_ref.at[:, :tile], basis_out.at[:, :tile])
+
+    up2, inv2 = panel(split(rest[-1]), group, {min(last, 1): first_half})
+    middle = middle[0]
+    step = basis_ref.shape[0] // 2
+    for at in (0, step):
+        basis_ref[at:at + step, tile:] = nt(middle[at:at + step], inv2)
+        put(basis_ref.at[at:at + step, tile:], basis_out.at[at:at + step, tile:])
+    factor_ref[tile:, tile:] = up2
     put(factor_ref.at[tile:, :], factor_out.at[tile:, :])
-    at = 0
-    for value in middle:
-        size = value.shape[0]
-        basis_ref[at:at + size, tile:] = nt(value, inv2)
-        put(basis_ref.at[at:at + size, tile:], basis_out.at[at:at + size, tile:])
-        at += size
     for copy in copies:
         copy.wait()
 
@@ -435,7 +446,7 @@
         scratch_shapes=[
             pltpu.VMEM((own_rows, columns), f32),
             pltpu.VMEM((columns, columns), f32),
-            pltpu.SemaphoreType.DMA((3 + len(sketches),)),
+            pltpu.SemaphoreType.DMA((5,)),
         ],
         compiler_params=pltpu.CompilerParams(vmem_limit_bytes=16 << 20),
         name="back",

time: 48.9 us -> 48.4 us (0.990)
  Pallas kernels: 12.1 us -> 11.6 us
where the time goes in v5:
time: 48.4 us; the launch traced here: 48.1 us
  starting transfers between devices  17.6 us (36%)
  waiting for transfers between devices  13.8 us (29%)
  Pallas kernels  11.6 us (24%)
  local copies, waits for them, and re-layouts  4.34 us (9%)
  between operations  0.76 us (2%)
    ppermute x16, starting transfers between devices, swap(): lax.ppermute(value, AXES, [(i, i ^ (odd_bit if i % 2 else bit)) for i in...  17.6 us
    ppermute x16, waiting for transfers between devices, swap(): lax.ppermute(value, AXES, [(i, i ^ (odd_bit if i % 2 else bit)) for i in...  13.8 us
    pallas_call x1, Pallas kernels, on_device(): pl.pallas_call(functools.partial(back_kernel, points_total, len(sketches)...  6.61 us
    pallas_call x4, Pallas kernels, on_device(): pl.pallas_call(functools.partial(front_kernel, start, width, own_rows, tm...  4.88 us
    unnamed x12, local copies, waits for them, and re-layouts  3.4 us
  transfers between devices with their start and end apart: 16, of which 11 were waited for; matrix products, arithmetic and copies ran while one was open for 0% of the time, Pallas kernels for 7%

profile of v5, /device:TPU:0, one launch (start us, length us, event | category | flops | bytes accessed | tf_op | source)
XLA Modules:
  0.0 48.1 jit_solution(484812025035728354)
XLA Ops:
  0.6 0.8 %constant_dynamic-slice_fusion = f32[64,256]{1,0:T(8,128)S(1)} fusion(f32[256,256]{1,0:T(8,128)} %test_ref.1, s32[]{:T(128)S(6)} %select_n.11), kind=kLoop, calls=%fused_computation.2 | loop fusion | bytes 131076 | tf_op jit(solution)/shard_map/dynamic_slice | solution.py:337
  1.5 3.0 %collective-permute-start.4 = (f32[64,256]{1,0:T(8,128)S(1)}, f32[64,256]{1,0:T(8,128)S(1)}, u32[]{:S(2)}, u32[]{:S(2)}) collective-permute-start(f32[64,256]{1,0:T(8,128)S(1)} %constant_dynamic-slice_fusion), channel_id=1, source_target_pairs={{0,16},{1,17},{2,18},{3,19},{4,20},{5,21},{6,22},{7,23},{8,24},{9,... | collective-permute-start | bytes 196616 | tf_op jit(solution)/shard_map/ppermute | solution.py:56
  4.5 0.0 copy-start
  4.5 1.2 %copy-done = f32[256,1024]{1,0:T(8,128)S(1)} copy-done((f32[256,1024]{1,0:T(8,128)S(1)}, f32[256,1024]{1,0:T(8,128)}, u32[]{:S(2)}) %copy-start) | copy-done | bytes 1048600
  5.7 0.1 cut.1
  5.8 0.9 %collective-permute-done.4.refs_6_ = f32[64,256]{1,0:T(8,128)S(1)} collective-permute-done((f32[64,256]{1,0:T(8,128)S(1)}, f32[64,256]{1,0:T(8,128)S(1)}, u32[]{:S(2)}, u32[]{:S(2)}) %collective-permute-start.4) | collective-permute-done | bytes 65568 | tf_op jit(solution)/shard_map/ppermute | solution.py:56
  6.7 2.0 %collective-permute-start.6 = (f32[64,256]{1,0:T(8,128)S(1)}, f32[64,256]{1,0:T(8,128)S(1)}, u32[]{:S(2)}, u32[]{:S(2)}) collective-permute-start(f32[64,256]{1,0:T(8,128)S(1)} %collective-permute-done.4.refs_6_), channel_id=1, source_target_pairs={{0,2},{1,3},{2,0},{3,1},{4,6},{5,7},{6,4},{7,5},{8,10},{9,11},{10,... | collective-permute-start | bytes 196616 | tf_op jit(solution)/shard_map/ppermute | solution.py:56
  8.7 1.5 %collective-permute-start.3 = (f32[256,128]{1,0:T(8,128)S(1)}, f32[256,128]{1,0:T(8,128)S(1)}, u32[]{:S(2)}, u32[]{:S(2)}) collective-permute-start(f32[256,128]{1,0:T(8,128)S(1)} %get-tuple-element.20), channel_id=1, source_target_pairs={{0,16},{1,17},{2,18},{3,19},{4,20},{5,21},{6,22},{7,23},{8,24},{9,... | collective-permute-start | bytes 393224 | tf_op jit(solution)/shard_map/ppermute | solution.py:56
  10.2 0.0 collective-permute-start.5
  10.3 0.5 %collective-permute-start.2 = (f32[256,128]{1,0:T(8,128)S(1)}, f32[256,128]{1,0:T(8,128)S(1)}, u32[]{:S(2)}, u32[]{:S(2)}) collective-permute-start(f32[256,128]{1,0:T(8,128)S(1)} %get-tuple-element.19), channel_id=1, source_target_pairs={{0,16},{1,17},{2,18},{3,19},{4,20},{5,21},{6,22},{7,23},{8,24},{9,... | collective-permute-start | bytes 393224 | tf_op jit(solution)/shard_map/ppermute | solution.py:56
  10.8 1.5 %collective-permute-start.1 = (f32[256,128]{1,0:T(8,128)S(1)}, f32[256,128]{1,0:T(8,128)S(1)}, u32[]{:S(2)}, u32[]{:S(2)}) collective-permute-start(f32[256,128]{1,0:T(8,128)S(1)} %get-tuple-element.18), channel_id=1, source_target_pairs={{0,16},{1,17},{2,18},{3,19},{4,20},{5,21},{6,22},{7,23},{8,24},{9,... | collective-permute-start | bytes 393224 | tf_op jit(solution)/shard_map/ppermute | solution.py:56
  12.3 0.0 collective-permute-done.6.refs_8_
  12.3 0.0 collective-permute-start.7
  12.3 0.0 collective-permute-done.5.refs_7_
  12.3 0.7 %collective-permute-start = (f32[256,128]{1,0:T(8,128)S(1)}, f32[256,128]{1,0:T(8,128)S(1)}, u32[]{:S(2)}, u32[]{:S(2)}) collective-permute-start(f32[256,128]{1,0:T(8,128)S(1)} %get-tuple-element.17), channel_id=1, source_target_pairs={{0,16},{1,17},{2,18},{3,19},{4,20},{5,21},{6,22},{7,23},{8,24},{9,... | collective-permute-start | bytes 393224 | tf_op jit(solution)/shard_map/ppermute | solution.py:56
  13.0 0.9 %copy-done.3 = f32[256,256]{1,0:T(8,128)S(1)} copy-done((f32[256,256]{1,0:T(8,128)S(1)}, f32[256,256]{1,0:T(8,128)}, u32[]{:S(2)}) %copy-start.3) | copy-done | bytes 262168
  14.0 0.0 copy-start.5
  14.0 0.6 %copy-done.5 = f32[64]{0:T(128)S(1)} copy-done((f32[64]{0:T(128)S(1)}, f32[64]{0:T(128)}, u32[]{:S(2)}) %copy-start.5) | copy-done | bytes 280
  14.7 0.1 copy.10.refs_1_
  14.8 0.0 collective-permute-done.3.refs_5_
  14.8 0.0 collective-permute-done.7.refs_9_
  14.8 0.0 copy-done.1
  14.8 0.0 copy-done.2
  14.8 0.6 %copy-done.4 = s32[1024]{0:T(1024)S(1)} copy-done((s32[1024]{0:T(1024)S(1)}, s32[1024]{0:T(1024)}, u32[]{:S(2)}) %copy-start.4) | copy-done | bytes 4120
  15.4 1.0 %shard_map.68.refs_10_.refs_0_ = f32[128,256]{1,0:T(8,128)S(1)} custom-call(f32[256,1024]{1,0:T(8,128)S(1)} %copy-done.1, f32[64,1]{1,0:T(8,128)S(1)} %copy.10.refs_1_, s32[1,1024]{1,0:T(1,128)S(1)} %bitcast.2, f32[2,24,256]{2,1,0:T(8,128)S(1)} %copy-done.2, f32[256,256]{1,0:T(8,128)S(1)} %hold.1.refs_4_, f32[256,128]{1,0:T(8,128)S(1)} %collective-permute-done.3.refs_5_, ...), custom_call_target="tpu_custom_call" | custom-call | flops 301989888 | bytes 786432 | tf_op jit(solution)/shard_map/pallas_call | solution.py:392
  16.4 0.5 %collective-permute-done.2.refs_5_ = f32[256,128]{1,0:T(8,128)S(1)} collective-permute-done((f32[256,128]{1,0:T(8,128)S(1)}, f32[256,128]{1,0:T(8,128)S(1)}, u32[]{:S(2)}, u32[]{:S(2)}) %collective-permute-start.2) | collective-permute-done | bytes 131104 | tf_op jit(solution)/shard_map/ppermute | solution.py:56
  16.9 1.4 %shard_map.69 = (f32[128,256]{1,0:T(8,128)S(1)}, f32[256,256]{1,0:T(8,128)S(1)}) custom-call(f32[256,1024]{1,0:T(8,128)S(1)} %copy-done.1, f32[64,1]{1,0:T(8,128)S(1)} %copy.10.refs_1_, s32[1,1024]{1,0:T(1,128)S(1)} %bitcast.3, f32[2,24,256]{2,1,0:T(8,128)S(1)} %copy-done.2, f32[256,256]{1,0:T(8,128)S(1)} %hold.1.refs_4_, ...), custom_call_target="tpu_custom_call" | custom-call | flops 301989888 | bytes 786432 | tf_op jit(solution)/shard_map/pallas_call | solution.py:392
  18.3 1.4 %collective-permute-done.1.refs_5_ = f32[256,128]{1,0:T(8,128)S(1)} collective-permute-done((f32[256,128]{1,0:T(8,128)S(1)}, f32[256,128]{1,0:T(8,128)S(1)}, u32[]{:S(2)}, u32[]{:S(2)}) %collective-permute-start.1) | collective-permute-done | bytes 131104 | tf_op jit(solution)/shard_map/ppermute | solution.py:56
  19.7 1.0 %shard_map.70.refs_10_.refs_2_ = f32[128,256]{1,0:T(8,128)S(1)} custom-call(f32[256,1024]{1,0:T(8,128)S(1)} %copy-done.1, f32[64,1]{1,0:T(8,128)S(1)} %copy.10.refs_1_, s32[1,1024]{1,0:T(1,128)S(1)} %bitcast.4, f32[2,24,256]{2,1,0:T(8,128)S(1)} %copy-done.2, f32[256,256]{1,0:T(8,128)S(1)} %hold.1.refs_4_, f32[256,128]{1,0:T(8,128)S(1)} %collective-permute-done.1.refs_5_, ...), custom_call_target="tpu_custom_call" | custom-call | flops 301989888 | bytes 786432 | tf_op jit(solution)/shard_map/pallas_call | solution.py:392
  20.7 1.4 %collective-permute-done.refs_5_ = f32[256,128]{1,0:T(8,128)S(1)} collective-permute-done((f32[256,128]{1,0:T(8,128)S(1)}, f32[256,128]{1,0:T(8,128)S(1)}, u32[]{:S(2)}, u32[]{:S(2)}) %collective-permute-start) | collective-permute-done | bytes 131104 | tf_op jit(solution)/shard_map/ppermute | solution.py:56
  22.1 1.4 %shard_map.71 = (f32[128,256]{1,0:T(8,128)S(1)}, f32[136,128]{1,0:T(8,128)S(1)}, f32[136,128]{1,0:T(8,128)S(1)}) custom-call(f32[256,1024]{1,0:T(8,128)S(1)} %copy-done.1, f32[64,1]{1,0:T(8,128)S(1)} %copy.10.refs_1_, s32[1,1024]{1,0:T(1,128)S(1)} %bitcast.5, f32[2,24,256]{2,1,0:T(8,128)S(1)} %copy-done.2, f32[256,256]{1,0:T(8,128)S(1)} %hold.1.refs_4_, ...), custom_call_target="tpu_custom_call" | custom-call | flops 301989888 | bytes 786432 | tf_op jit(solution)/shard_map/pallas_call | solution.py:392
  23.6 0.1 collective-permute-start.8
  23.6 1.2 %collective-permute-done.8 = f32[136,128]{1,0:T(8,128)S(1)} collective-permute-done((f32[136,128]{1,0:T(8,128)S(1)}, f32[136,128]{1,0:T(8,128)S(1)}, u32[]{:S(2)}, u32[]{:S(2)}) %collective-permute-start.8) | collective-permute-done | bytes 69664 | tf_op jit(solution)/shard_map/ppermute | solution.py:56
  24.9 1.4 %collective-permute-start.11 = (f32[136,128]{1,0:T(8,128)S(1)}, f32[136,128]{1,0:T(8,128)S(1)}, u32[]{:S(2)}, u32[]{:S(2)}) collective-permute-start(f32[136,128]{1,0:T(8,128)S(1)} %add.30), channel_id=1, source_target_pairs={{0,18},{1,13},{2,16},{3,15},{4,22},{5,9},{6,20},{7,11},{8,26},{9,5... | collective-permute-start | bytes 208904 | tf_op jit(solution)/shard_map/ppermute | solution.py:56
  26.3 0.3 collective-permute-start.10
  26.6 1.8 %collective-permute-start.9 = (f32[136,128]{1,0:T(8,128)S(1)}, f32[136,128]{1,0:T(8,128)S(1)}, u32[]{:S(2)}, u32[]{:S(2)}) collective-permute-start(f32[136,128]{1,0:T(8,128)S(1)} %add.30), channel_id=1, source_target_pairs={{0,2},{1,5},{2,0},{3,7},{4,6},{5,1},{6,4},{7,3},{8,10},{9,13},{10,... | collective-permute-start | bytes 208904 | tf_op jit(solution)/shard_map/ppermute | solution.py:56
  28.4 1.8 %collective-permute-done.11 = f32[136,128]{1,0:T(8,128)S(1)} collective-permute-done((f32[136,128]{1,0:T(8,128)S(1)}, f32[136,128]{1,0:T(8,128)S(1)}, u32[]{:S(2)}, u32[]{:S(2)}) %collective-permute-start.11) | collective-permute-done | bytes 69664 | tf_op jit(solution)/shard_map/ppermute | solution.py:56
  30.2 0.7 %collective-permute-done.10 = f32[136,128]{1,0:T(8,128)S(1)} collective-permute-done((f32[136,128]{1,0:T(8,128)S(1)}, f32[136,128]{1,0:T(8,128)S(1)}, u32[]{:S(2)}, u32[]{:S(2)}) %collective-permute-start.10) | collective-permute-done | bytes 69664 | tf_op jit(solution)/shard_map/ppermute | solution.py:56
  30.9 0.1 collective-permute-done.9
  31.0 4.0 %collective-permute-start.14 = (f32[136,128]{1,0:T(8,128)S(1)}, f32[136,128]{1,0:T(8,128)S(1)}, u32[]{:S(2)}, u32[]{:S(2)}) collective-permute-start(f32[136,128]{1,0:T(8,128)S(1)} %add_add_fusion.1), channel_id=1, source_target_pairs={{0,12},{1,19},{2,14},{3,17},{4,8},{5,23},{6,10},{7,21},{8,4},{9,27... | collective-permute-start | bytes 208904 | tf_op jit(solution)/shard_map/ppermute | solution.py:56
  35.0 0.0 collective-permute-start.13
  35.0 0.6 %collective-permute-start.12 = (f32[136,128]{1,0:T(8,128)S(1)}, f32[136,128]{1,0:T(8,128)S(1)}, u32[]{:S(2)}, u32[]{:S(2)}) collective-permute-start(f32[136,128]{1,0:T(8,128)S(1)} %add_add_fusion.1), channel_id=1, source_target_pairs={{0,4},{1,3},{2,6},{3,1},{4,0},{5,7},{6,2},{7,5},{8,12},{9,11},{10,... | collective-permute-start | bytes 208904 | tf_op jit(solution)/shard_map/ppermute | solution.py:56
  35.6 1.7 %collective-permute-done.14 = f32[136,128]{1,0:T(8,128)S(1)} collective-permute-done((f32[136,128]{1,0:T(8,128)S(1)}, f32[136,128]{1,0:T(8,128)S(1)}, u32[]{:S(2)}, u32[]{:S(2)}) %collective-permute-start.14) | collective-permute-done | bytes 69664 | tf_op jit(solution)/shard_map/ppermute | solution.py:56
  37.3 2.8 %collective-permute-done.13 = f32[136,128]{1,0:T(8,128)S(1)} collective-permute-done((f32[136,128]{1,0:T(8,128)S(1)}, f32[136,128]{1,0:T(8,128)S(1)}, u32[]{:S(2)}, u32[]{:S(2)}) %collective-permute-start.13) | collective-permute-done | bytes 69664 | tf_op jit(solution)/shard_map/ppermute | solution.py:56
  40.2 0.0 collective-permute-done.12
  40.2 0.1 collective-permute-start.15
  40.3 1.2 %collective-permute-done.15.other_ref = f32[136,128]{1,0:T(8,128)S(1)} collective-permute-done((f32[136,128]{1,0:T(8,128)S(1)}, f32[136,128]{1,0:T(8,128)S(1)}, u32[]{:S(2)}, u32[]{:S(2)}) %collective-permute-start.15) | collective-permute-done | bytes 69664 | tf_op jit(solution)/shard_map/ppermute | solution.py:56
  41.5 6.6 %back.1 = (f32[512,256]{1,0:T(8,128)}, f32[256,256]{1,0:T(8,128)}) custom-call(f32[136,128]{1,0:T(8,128)S(1)} %add_add_fusion.part_ref, f32[136,128]{1,0:T(8,128)S(1)} %collective-permute-done.15.other_ref, f32[128,256]{1,0:T(8,128)S(1)} %shard_map.68.refs_10_.refs_0_, f32[128,256]{1,0:T(8,128)S(1)} %get-tuple-element.29.refs_1_, ...), custom_call_target="tpu_custom_call" | custom-call | tf_op jit(solution)/shard_map/back/pallas_call | solution.py:438
  (8 shorter events, 0.1 us)
Async XLA Ops:
  1.5 5.2 %collective-permute-start.4 = (f32[64,256]{1,0:T(8,128)S(1)}, f32[64,256]{1,0:T(8,128)S(1)}, u32[]{:S(2)}, u32[]{:S(2)}) collective-permute-start(f32[64,256]{1,0:T(8,128)S(1)} %constant_dynamic-slice_fusion), channel_id=1, source_target_pairs={{0,16},{1,17},{2,18},{3,19},{4,20},{5,21},{6,22},{7,23},{8,24},{9,... | collective-permute-start | bytes 196616 | tf_op jit(solution)/shard_map/ppermute | solution.py:56
  4.5 1.2 %copy-start = (f32[256,1024]{1,0:T(8,128)S(1)}, f32[256,1024]{1,0:T(8,128)}, u32[]{:S(2)}) copy-start(f32[256,1024]{1,0:T(8,128)} %refs_0_.7) | copy-start | bytes 3145732
  5.7 9.1 %copy-start.1 = (f32[256,1024]{1,0:T(8,128)S(1)}, f32[256,1024]{1,0:T(8,128)}, u32[]{:S(2)}) copy-start(f32[256,1024]{1,0:T(8,128)} %refs_0_.7) | copy-start | bytes 3145732
  6.7 5.5 %collective-permute-start.6 = (f32[64,256]{1,0:T(8,128)S(1)}, f32[64,256]{1,0:T(8,128)S(1)}, u32[]{:S(2)}, u32[]{:S(2)}) collective-permute-start(f32[64,256]{1,0:T(8,128)S(1)} %collective-permute-done.4.refs_6_), channel_id=1, source_target_pairs={{0,2},{1,3},{2,0},{3,1},{4,6},{5,7},{6,4},{7,5},{8,10},{9,11},{10,... | collective-permute-start | bytes 196616 | tf_op jit(solution)/shard_map/ppermute | solution.py:56
  8.7 6.0 %collective-permute-start.3 = (f32[256,128]{1,0:T(8,128)S(1)}, f32[256,128]{1,0:T(8,128)S(1)}, u32[]{:S(2)}, u32[]{:S(2)}) collective-permute-start(f32[256,128]{1,0:T(8,128)S(1)} %get-tuple-element.20), channel_id=1, source_target_pairs={{0,16},{1,17},{2,18},{3,19},{4,20},{5,21},{6,22},{7,23},{8,24},{9,... | collective-permute-start | bytes 393224 | tf_op jit(solution)/shard_map/ppermute | solution.py:56
  10.2 2.0 %collective-permute-start.5 = (f32[64,256]{1,0:T(8,128)S(1)}, f32[64,256]{1,0:T(8,128)S(1)}, u32[]{:S(2)}, u32[]{:S(2)}) collective-permute-start(f32[64,256]{1,0:T(8,128)S(1)} %collective-permute-done.4.refs_6_), channel_id=1, source_target_pairs={{0,1},{1,0},{2,3},{3,2},{4,5},{5,4},{6,7},{7,6},{8,9},{9,8},{10,11... | collective-permute-start | bytes 196616 | tf_op jit(solution)/shard_map/ppermute | solution.py:56
  10.3 6.6 %collective-permute-start.2 = (f32[256,128]{1,0:T(8,128)S(1)}, f32[256,128]{1,0:T(8,128)S(1)}, u32[]{:S(2)}, u32[]{:S(2)}) collective-permute-start(f32[256,128]{1,0:T(8,128)S(1)} %get-tuple-element.19), channel_id=1, source_target_pairs={{0,16},{1,17},{2,18},{3,19},{4,20},{5,21},{6,22},{7,23},{8,24},{9,... | collective-permute-start | bytes 393224 | tf_op jit(solution)/shard_map/ppermute | solution.py:56
  10.8 8.9 %collective-permute-start.1 = (f32[256,128]{1,0:T(8,128)S(1)}, f32[256,128]{1,0:T(8,128)S(1)}, u32[]{:S(2)}, u32[]{:S(2)}) collective-permute-start(f32[256,128]{1,0:T(8,128)S(1)} %get-tuple-element.18), channel_id=1, source_target_pairs={{0,16},{1,17},{2,18},{3,19},{4,20},{5,21},{6,22},{7,23},{8,24},{9,... | collective-permute-start | bytes 393224 | tf_op jit(solution)/shard_map/ppermute | solution.py:56
  12.3 2.5 %collective-permute-start.7 = (f32[64,256]{1,0:T(8,128)S(1)}, f32[64,256]{1,0:T(8,128)S(1)}, u32[]{:S(2)}, u32[]{:S(2)}) collective-permute-start(f32[64,256]{1,0:T(8,128)S(1)} %collective-permute-done.6.refs_8_), channel_id=1, source_target_pairs={{0,1},{1,0},{2,3},{3,2},{4,5},{5,4},{6,7},{7,6},{8,9},{9,8},{10,11... | collective-permute-start | bytes 196616 | tf_op jit(solution)/shard_map/ppermute | solution.py:56
  12.3 9.8 %collective-permute-start = (f32[256,128]{1,0:T(8,128)S(1)}, f32[256,128]{1,0:T(8,128)S(1)}, u32[]{:S(2)}, u32[]{:S(2)}) collective-permute-start(f32[256,128]{1,0:T(8,128)S(1)} %get-tuple-element.17), channel_id=1, source_target_pairs={{0,16},{1,17},{2,18},{3,19},{4,20},{5,21},{6,22},{7,23},{8,24},{9,... | collective-permute-start | bytes 393224 | tf_op jit(solution)/shard_map/ppermute | solution.py:56
  13.0 0.9 %copy-start.3 = (f32[256,256]{1,0:T(8,128)S(1)}, f32[256,256]{1,0:T(8,128)}, u32[]{:S(2)}) copy-start(f32[256,256]{1,0:T(8,128)} %test_ref.1) | copy-start | bytes 786436
  14.0 0.8 %copy-start.2 = (f32[2,24,256]{2,1,0:T(8,128)S(1)}, f32[2,24,256]{2,1,0:T(8,128)}, u32[]{:S(2)}) copy-start(f32[2,24,256]{2,1,0:T(8,128)} %constant.24.clone.refs_3_) | copy-start | bytes 147460
  14.0 0.7 %copy-start.5 = (f32[64]{0:T(128)S(1)}, f32[64]{0:T(128)}, u32[]{:S(2)}) copy-start(f32[64]{0:T(128)} %param.6) | copy-start | bytes 772
  14.7 0.7 %copy-start.4 = (s32[1024]{0:T(1024)S(1)}, s32[1024]{0:T(1024)}, u32[]{:S(2)}) copy-start(s32[1024]{0:T(1024)} %param.7) | copy-start | bytes 12292
  23.6 1.3 %collective-permute-start.8 = (f32[136,128]{1,0:T(8,128)S(1)}, f32[136,128]{1,0:T(8,128)S(1)}, u32[]{:S(2)}, u32[]{:S(2)}) collective-permute-start(f32[136,128]{1,0:T(8,128)S(1)} %get-tuple-element.27), channel_id=1, source_target_pairs={{0,1},{1,0},{2,3},{3,2},{4,5},{5,4},{6,7},{7,6},{8,9},{9,8},{10,11... | collective-permute-start | bytes 208904 | tf_op jit(solution)/shard_map/ppermute | solution.py:56
  24.9 5.3 %collective-permute-start.11 = (f32[136,128]{1,0:T(8,128)S(1)}, f32[136,128]{1,0:T(8,128)S(1)}, u32[]{:S(2)}, u32[]{:S(2)}) collective-permute-start(f32[136,128]{1,0:T(8,128)S(1)} %add.30), channel_id=1, source_target_pairs={{0,18},{1,13},{2,16},{3,15},{4,22},{5,9},{6,20},{7,11},{8,26},{9,5... | collective-permute-start | bytes 208904 | tf_op jit(solution)/shard_map/ppermute | solution.py:56
  26.3 4.7 %collective-permute-start.10 = (f32[136,128]{1,0:T(8,128)S(1)}, f32[136,128]{1,0:T(8,128)S(1)}, u32[]{:S(2)}, u32[]{:S(2)}) collective-permute-start(f32[136,128]{1,0:T(8,128)S(1)} %add.30), channel_id=1, source_target_pairs={{0,16},{1,9},{2,18},{3,11},{4,20},{5,13},{6,22},{7,15},{8,24},{9,1... | collective-permute-start | bytes 208904 | tf_op jit(solution)/shard_map/ppermute | solution.py:56
  26.6 4.4 %collective-permute-start.9 = (f32[136,128]{1,0:T(8,128)S(1)}, f32[136,128]{1,0:T(8,128)S(1)}, u32[]{:S(2)}, u32[]{:S(2)}) collective-permute-start(f32[136,128]{1,0:T(8,128)S(1)} %add.30), channel_id=1, source_target_pairs={{0,2},{1,5},{2,0},{3,7},{4,6},{5,1},{6,4},{7,3},{8,10},{9,13},{10,... | collective-permute-start | bytes 208904 | tf_op jit(solution)/shard_map/ppermute | solution.py:56
  31.0 6.3 %collective-permute-start.14 = (f32[136,128]{1,0:T(8,128)S(1)}, f32[136,128]{1,0:T(8,128)S(1)}, u32[]{:S(2)}, u32[]{:S(2)}) collective-permute-start(f32[136,128]{1,0:T(8,128)S(1)} %add_add_fusion.1), channel_id=1, source_target_pairs={{0,12},{1,19},{2,14},{3,17},{4,8},{5,23},{6,10},{7,21},{8,4},{9,27... | collective-permute-start | bytes 208904 | tf_op jit(solution)/shard_map/ppermute | solution.py:56
  35.0 5.2 %collective-permute-start.13 = (f32[136,128]{1,0:T(8,128)S(1)}, f32[136,128]{1,0:T(8,128)S(1)}, u32[]{:S(2)}, u32[]{:S(2)}) collective-permute-start(f32[136,128]{1,0:T(8,128)S(1)} %add_add_fusion.1), channel_id=1, source_target_pairs={{0,8},{1,17},{2,10},{3,19},{4,12},{5,21},{6,14},{7,23},{8,0},{9,25... | collective-permute-start | bytes 208904 | tf_op jit(solution)/shard_map/ppermute | solution.py:56
  35.0 5.2 %collective-permute-start.12 = (f32[136,128]{1,0:T(8,128)S(1)}, f32[136,128]{1,0:T(8,128)S(1)}, u32[]{:S(2)}, u32[]{:S(2)}) collective-permute-start(f32[136,128]{1,0:T(8,128)S(1)} %add_add_fusion.1), channel_id=1, source_target_pairs={{0,4},{1,3},{2,6},{3,1},{4,0},{5,7},{6,2},{7,5},{8,12},{9,11},{10,... | collective-permute-start | bytes 208904 | tf_op jit(solution)/shard_map/ppermute | solution.py:56
  40.2 1.3 %collective-permute-start.15 = (f32[136,128]{1,0:T(8,128)S(1)}, f32[136,128]{1,0:T(8,128)S(1)}, u32[]{:S(2)}, u32[]{:S(2)}) collective-permute-start(f32[136,128]{1,0:T(8,128)S(1)} %add_add_fusion.part_ref), channel_id=1, source_target_pairs={{0,1},{1,0},{2,3},{3,2},{4,5},{5,4},{6,7},{7,6},{8,9},{9,8},{10,11... | collective-permute-start | bytes 208904 | tf_op jit(solution)/shard_map/ppermute | solution.py:56

commit v6 on v5

--- a/solution.py
+++ b/solution.py
@@ -297,10 +297,8 @@
 
     up2, inv2 = panel(split(rest[-1]), group, {min(last, 1): first_half})
     middle = middle[0]
-    step = basis_ref.shape[0] // 2
-    for at in (0, step):
-        basis_ref[at:at + step, tile:] = nt(middle[at:at + step], inv2)
-        put(basis_ref.at[at:at + step, tile:], basis_out.at[at:at + step, tile:])
+    basis_ref[:, tile:] = nt(middle, inv2)
+    put(basis_ref.at[:, tile:], basis_out.at[:, tile:])
     factor_ref[tile:, tile:] = up2
     put(factor_ref.at[tile:, :], factor_out.at[tile:, :])
     for copy in copies:
@@ -446,7 +444,7 @@
         scratch_shapes=[
             pltpu.VMEM((own_rows, columns), f32),
             pltpu.VMEM((columns, columns), f32),
-            pltpu.SemaphoreType.DMA((5,)),
+            pltpu.SemaphoreType.DMA((4,)),
         ],
         compiler_params=pltpu.CompilerParams(vmem_limit_bytes=16 << 20),
         name="back",

time: 48.4 us -> 48.6 us (level)
  no operation moved by 1% of the time
where the time goes in v6:
time: 48.6 us; the launch traced here: 48.3 us
  starting transfers between devices  17.6 us (36%)
  waiting for transfers between devices  13.8 us (28%)
  Pallas kernels  11.8 us (24%)
  local copies, waits for them, and re-layouts  4.34 us (9%)
  between operations  0.76 us (2%)
    ppermute x16, starting transfers between devices, swap(): lax.ppermute(value, AXES, [(i, i ^ (odd_bit if i % 2 else bit)) for i in...  17.6 us
    ppermute x16, waiting for transfers between devices, swap(): lax.ppermute(value, AXES, [(i, i ^ (odd_bit if i % 2 else bit)) for i in...  13.8 us
    pallas_call x1, Pallas kernels, on_device(): pl.pallas_call(functools.partial(back_kernel, points_total, len(sketches)...  6.77 us
    pallas_call x4, Pallas kernels, on_device(): pl.pallas_call(functools.partial(front_kernel, start, width, own_rows, tm...  4.88 us
    unnamed x12, local copies, waits for them, and re-layouts  3.4 us
  transfers between devices with their start and end apart: 16, of which 11 were waited for; matrix products, arithmetic and copies ran while one was open for 0% of the time, Pallas kernels for 7%

profile of v6, /device:TPU:0, one launch (start us, length us, event | category | flops | bytes accessed | tf_op | source)
XLA Modules:
  0.0 48.3 jit_solution(14824267794043301373)
XLA Ops:
  0.6 0.8 %constant_dynamic-slice_fusion = f32[64,256]{1,0:T(8,128)S(1)} fusion(f32[256,256]{1,0:T(8,128)} %test_ref.1, s32[]{:T(128)S(6)} %select_n.11), kind=kLoop, calls=%fused_computation.2 | loop fusion | bytes 131076 | tf_op jit(solution)/shard_map/dynamic_slice | solution.py:335
  1.5 3.0 %collective-permute-start.4 = (f32[64,256]{1,0:T(8,128)S(1)}, f32[64,256]{1,0:T(8,128)S(1)}, u32[]{:S(2)}, u32[]{:S(2)}) collective-permute-start(f32[64,256]{1,0:T(8,128)S(1)} %constant_dynamic-slice_fusion), channel_id=1, source_target_pairs={{0,16},{1,17},{2,18},{3,19},{4,20},{5,21},{6,22},{7,23},{8,24},{9,... | collective-permute-start | bytes 196616 | tf_op jit(solution)/shard_map/ppermute | solution.py:56
  4.5 0.0 copy-start
  4.5 1.2 %copy-done = f32[256,1024]{1,0:T(8,128)S(1)} copy-done((f32[256,1024]{1,0:T(8,128)S(1)}, f32[256,1024]{1,0:T(8,128)}, u32[]{:S(2)}) %copy-start) | copy-done | bytes 1048600
  5.7 0.1 cut.1
  5.8 0.9 %collective-permute-done.4.refs_6_ = f32[64,256]{1,0:T(8,128)S(1)} collective-permute-done((f32[64,256]{1,0:T(8,128)S(1)}, f32[64,256]{1,0:T(8,128)S(1)}, u32[]{:S(2)}, u32[]{:S(2)}) %collective-permute-start.4) | collective-permute-done | bytes 65568 | tf_op jit(solution)/shard_map/ppermute | solution.py:56
  6.7 2.0 %collective-permute-start.6 = (f32[64,256]{1,0:T(8,128)S(1)}, f32[64,256]{1,0:T(8,128)S(1)}, u32[]{:S(2)}, u32[]{:S(2)}) collective-permute-start(f32[64,256]{1,0:T(8,128)S(1)} %collective-permute-done.4.refs_6_), channel_id=1, source_target_pairs={{0,2},{1,3},{2,0},{3,1},{4,6},{5,7},{6,4},{7,5},{8,10},{9,11},{10,... | collective-permute-start | bytes 196616 | tf_op jit(solution)/shard_map/ppermute | solution.py:56
  8.7 1.5 %collective-permute-start.3 = (f32[256,128]{1,0:T(8,128)S(1)}, f32[256,128]{1,0:T(8,128)S(1)}, u32[]{:S(2)}, u32[]{:S(2)}) collective-permute-start(f32[256,128]{1,0:T(8,128)S(1)} %get-tuple-element.20), channel_id=1, source_target_pairs={{0,16},{1,17},{2,18},{3,19},{4,20},{5,21},{6,22},{7,23},{8,24},{9,... | collective-permute-start | bytes 393224 | tf_op jit(solution)/shard_map/ppermute | solution.py:56
  10.2 0.0 collective-permute-start.5
  10.3 0.5 %collective-permute-start.2 = (f32[256,128]{1,0:T(8,128)S(1)}, f32[256,128]{1,0:T(8,128)S(1)}, u32[]{:S(2)}, u32[]{:S(2)}) collective-permute-start(f32[256,128]{1,0:T(8,128)S(1)} %get-tuple-element.19), channel_id=1, source_target_pairs={{0,16},{1,17},{2,18},{3,19},{4,20},{5,21},{6,22},{7,23},{8,24},{9,... | collective-permute-start | bytes 393224 | tf_op jit(solution)/shard_map/ppermute | solution.py:56
  10.8 1.5 %collective-permute-start.1 = (f32[256,128]{1,0:T(8,128)S(1)}, f32[256,128]{1,0:T(8,128)S(1)}, u32[]{:S(2)}, u32[]{:S(2)}) collective-permute-start(f32[256,128]{1,0:T(8,128)S(1)} %get-tuple-element.18), channel_id=1, source_target_pairs={{0,16},{1,17},{2,18},{3,19},{4,20},{5,21},{6,22},{7,23},{8,24},{9,... | collective-permute-start | bytes 393224 | tf_op jit(solution)/shard_map/ppermute | solution.py:56
  12.3 0.0 collective-permute-done.6.refs_8_
  12.3 0.0 collective-permute-start.7
  12.3 0.0 collective-permute-done.5.refs_7_
  12.3 0.7 %collective-permute-start = (f32[256,128]{1,0:T(8,128)S(1)}, f32[256,128]{1,0:T(8,128)S(1)}, u32[]{:S(2)}, u32[]{:S(2)}) collective-permute-start(f32[256,128]{1,0:T(8,128)S(1)} %get-tuple-element.17), channel_id=1, source_target_pairs={{0,16},{1,17},{2,18},{3,19},{4,20},{5,21},{6,22},{7,23},{8,24},{9,... | collective-permute-start | bytes 393224 | tf_op jit(solution)/shard_map/ppermute | solution.py:56
  13.0 0.9 %copy-done.3 = f32[256,256]{1,0:T(8,128)S(1)} copy-done((f32[256,256]{1,0:T(8,128)S(1)}, f32[256,256]{1,0:T(8,128)}, u32[]{:S(2)}) %copy-start.3) | copy-done | bytes 262168
  14.0 0.0 copy-start.5
  14.0 0.6 %copy-done.5 = f32[64]{0:T(128)S(1)} copy-done((f32[64]{0:T(128)S(1)}, f32[64]{0:T(128)}, u32[]{:S(2)}) %copy-start.5) | copy-done | bytes 280
  14.7 0.1 copy.10.refs_1_
  14.8 0.0 collective-permute-done.3.refs_5_
  14.8 0.0 collective-permute-done.7.refs_9_
  14.8 0.0 copy-done.1
  14.8 0.0 copy-done.2
  14.8 0.6 %copy-done.4 = s32[1024]{0:T(1024)S(1)} copy-done((s32[1024]{0:T(1024)S(1)}, s32[1024]{0:T(1024)}, u32[]{:S(2)}) %copy-start.4) | copy-done | bytes 4120
  15.4 1.0 %shard_map.68.refs_10_.refs_0_ = f32[128,256]{1,0:T(8,128)S(1)} custom-call(f32[256,1024]{1,0:T(8,128)S(1)} %copy-done.1, f32[64,1]{1,0:T(8,128)S(1)} %copy.10.refs_1_, s32[1,1024]{1,0:T(1,128)S(1)} %bitcast.2, f32[2,24,256]{2,1,0:T(8,128)S(1)} %copy-done.2, f32[256,256]{1,0:T(8,128)S(1)} %hold.1.refs_4_, f32[256,128]{1,0:T(8,128)S(1)} %collective-permute-done.3.refs_5_, ...), custom_call_target="tpu_custom_call" | custom-call | flops 301989888 | bytes 786432 | tf_op jit(solution)/shard_map/pallas_call | solution.py:390
  16.4 0.5 %collective-permute-done.2.refs_5_ = f32[256,128]{1,0:T(8,128)S(1)} collective-permute-done((f32[256,128]{1,0:T(8,128)S(1)}, f32[256,128]{1,0:T(8,128)S(1)}, u32[]{:S(2)}, u32[]{:S(2)}) %collective-permute-start.2) | collective-permute-done | bytes 131104 | tf_op jit(solution)/shard_map/ppermute | solution.py:56
  16.9 1.4 %shard_map.69 = (f32[128,256]{1,0:T(8,128)S(1)}, f32[256,256]{1,0:T(8,128)S(1)}) custom-call(f32[256,1024]{1,0:T(8,128)S(1)} %copy-done.1, f32[64,1]{1,0:T(8,128)S(1)} %copy.10.refs_1_, s32[1,1024]{1,0:T(1,128)S(1)} %bitcast.3, f32[2,24,256]{2,1,0:T(8,128)S(1)} %copy-done.2, f32[256,256]{1,0:T(8,128)S(1)} %hold.1.refs_4_, ...), custom_call_target="tpu_custom_call" | custom-call | flops 301989888 | bytes 786432 | tf_op jit(solution)/shard_map/pallas_call | solution.py:390
  18.3 1.4 %collective-permute-done.1.refs_5_ = f32[256,128]{1,0:T(8,128)S(1)} collective-permute-done((f32[256,128]{1,0:T(8,128)S(1)}, f32[256,128]{1,0:T(8,128)S(1)}, u32[]{:S(2)}, u32[]{:S(2)}) %collective-permute-start.1) | collective-permute-done | bytes 131104 | tf_op jit(solution)/shard_map/ppermute | solution.py:56
  19.7 1.0 %shard_map.70.refs_10_.refs_2_ = f32[128,256]{1,0:T(8,128)S(1)} custom-call(f32[256,1024]{1,0:T(8,128)S(1)} %copy-done.1, f32[64,1]{1,0:T(8,128)S(1)} %copy.10.refs_1_, s32[1,1024]{1,0:T(1,128)S(1)} %bitcast.4, f32[2,24,256]{2,1,0:T(8,128)S(1)} %copy-done.2, f32[256,256]{1,0:T(8,128)S(1)} %hold.1.refs_4_, f32[256,128]{1,0:T(8,128)S(1)} %collective-permute-done.1.refs_5_, ...), custom_call_target="tpu_custom_call" | custom-call | flops 301989888 | bytes 786432 | tf_op jit(solution)/shard_map/pallas_call | solution.py:390
  20.7 1.4 %collective-permute-done.refs_5_ = f32[256,128]{1,0:T(8,128)S(1)} collective-permute-done((f32[256,128]{1,0:T(8,128)S(1)}, f32[256,128]{1,0:T(8,128)S(1)}, u32[]{:S(2)}, u32[]{:S(2)}) %collective-permute-start) | collective-permute-done | bytes 131104 | tf_op jit(solution)/shard_map/ppermute | solution.py:56
  22.1 1.4 %shard_map.71 = (f32[128,256]{1,0:T(8,128)S(1)}, f32[136,128]{1,0:T(8,128)S(1)}, f32[136,128]{1,0:T(8,128)S(1)}) custom-call(f32[256,1024]{1,0:T(8,128)S(1)} %copy-done.1, f32[64,1]{1,0:T(8,128)S(1)} %copy.10.refs_1_, s32[1,1024]{1,0:T(1,128)S(1)} %bitcast.5, f32[2,24,256]{2,1,0:T(8,128)S(1)} %copy-done.2, f32[256,256]{1,0:T(8,128)S(1)} %hold.1.refs_4_, ...), custom_call_target="tpu_custom_call" | custom-call | flops 301989888 | bytes 786432 | tf_op jit(solution)/shard_map/pallas_call | solution.py:390
  23.6 0.1 collective-permute-start.8
  23.6 1.2 %collective-permute-done.8 = f32[136,128]{1,0:T(8,128)S(1)} collective-permute-done((f32[136,128]{1,0:T(8,128)S(1)}, f32[136,128]{1,0:T(8,128)S(1)}, u32[]{:S(2)}, u32[]{:S(2)}) %collective-permute-start.8) | collective-permute-done | bytes 69664 | tf_op jit(solution)/shard_map/ppermute | solution.py:56
  24.9 1.4 %collective-permute-start.11 = (f32[136,128]{1,0:T(8,128)S(1)}, f32[136,128]{1,0:T(8,128)S(1)}, u32[]{:S(2)}, u32[]{:S(2)}) collective-permute-start(f32[136,128]{1,0:T(8,128)S(1)} %add.30), channel_id=1, source_target_pairs={{0,18},{1,13},{2,16},{3,15},{4,22},{5,9},{6,20},{7,11},{8,26},{9,5... | collective-permute-start | bytes 208904 | tf_op jit(solution)/shard_map/ppermute | solution.py:56
  26.3 0.3 collective-permute-start.10
  26.6 1.8 %collective-permute-start.9 = (f32[136,128]{1,0:T(8,128)S(1)}, f32[136,128]{1,0:T(8,128)S(1)}, u32[]{:S(2)}, u32[]{:S(2)}) collective-permute-start(f32[136,128]{1,0:T(8,128)S(1)} %add.30), channel_id=1, source_target_pairs={{0,2},{1,5},{2,0},{3,7},{4,6},{5,1},{6,4},{7,3},{8,10},{9,13},{10,... | collective-permute-start | bytes 208904 | tf_op jit(solution)/shard_map/ppermute | solution.py:56
  28.4 1.8 %collective-permute-done.11 = f32[136,128]{1,0:T(8,128)S(1)} collective-permute-done((f32[136,128]{1,0:T(8,128)S(1)}, f32[136,128]{1,0:T(8,128)S(1)}, u32[]{:S(2)}, u32[]{:S(2)}) %collective-permute-start.11) | collective-permute-done | bytes 69664 | tf_op jit(solution)/shard_map/ppermute | solution.py:56
  30.2 0.7 %collective-permute-done.10 = f32[136,128]{1,0:T(8,128)S(1)} collective-permute-done((f32[136,128]{1,0:T(8,128)S(1)}, f32[136,128]{1,0:T(8,128)S(1)}, u32[]{:S(2)}, u32[]{:S(2)}) %collective-permute-start.10) | collective-permute-done | bytes 69664 | tf_op jit(solution)/shard_map/ppermute | solution.py:56
  30.9 0.1 collective-permute-done.9
  31.0 4.0 %collective-permute-start.14 = (f32[136,128]{1,0:T(8,128)S(1)}, f32[136,128]{1,0:T(8,128)S(1)}, u32[]{:S(2)}, u32[]{:S(2)}) collective-permute-start(f32[136,128]{1,0:T(8,128)S(1)} %add_add_fusion.1), channel_id=1, source_target_pairs={{0,12},{1,19},{2,14},{3,17},{4,8},{5,23},{6,10},{7,21},{8,4},{9,27... | collective-permute-start | bytes 208904 | tf_op jit(solution)/shard_map/ppermute | solution.py:56
  35.0 0.0 collective-permute-start.13
  35.0 0.6 %collective-permute-start.12 = (f32[136,128]{1,0:T(8,128)S(1)}, f32[136,128]{1,0:T(8,128)S(1)}, u32[]{:S(2)}, u32[]{:S(2)}) collective-permute-start(f32[136,128]{1,0:T(8,128)S(1)} %add_add_fusion.1), channel_id=1, source_target_pairs={{0,4},{1,3},{2,6},{3,1},{4,0},{5,7},{6,2},{7,5},{8,12},{9,11},{10,... | collective-permute-start | bytes 208904 | tf_op jit(solution)/shard_map/ppermute | solution.py:56
  35.6 1.7 %collective-permute-done.14 = f32[136,128]{1,0:T(8,128)S(1)} collective-permute-done((f32[136,128]{1,0:T(8,128)S(1)}, f32[136,128]{1,0:T(8,128)S(1)}, u32[]{:S(2)}, u32[]{:S(2)}) %collective-permute-start.14) | collective-permute-done | bytes 69664 | tf_op jit(solution)/shard_map/ppermute | solution.py:56
  37.3 2.8 %collective-permute-done.13 = f32[136,128]{1,0:T(8,128)S(1)} collective-permute-done((f32[136,128]{1,0:T(8,128)S(1)}, f32[136,128]{1,0:T(8,128)S(1)}, u32[]{:S(2)}, u32[]{:S(2)}) %collective-permute-start.13) | collective-permute-done | bytes 69664 | tf_op jit(solution)/shard_map/ppermute | solution.py:56
  40.2 0.0 collective-permute-done.12
  40.2 0.1 collective-permute-start.15
  40.3 1.2 %collective-permute-done.15.other_ref = f32[136,128]{1,0:T(8,128)S(1)} collective-permute-done((f32[136,128]{1,0:T(8,128)S(1)}, f32[136,128]{1,0:T(8,128)S(1)}, u32[]{:S(2)}, u32[]{:S(2)}) %collective-permute-start.15) | collective-permute-done | bytes 69664 | tf_op jit(solution)/shard_map/ppermute | solution.py:56
  41.5 6.8 %back.1 = (f32[512,256]{1,0:T(8,128)}, f32[256,256]{1,0:T(8,128)}) custom-call(f32[136,128]{1,0:T(8,128)S(1)} %add_add_fusion.part_ref, f32[136,128]{1,0:T(8,128)S(1)} %collective-permute-done.15.other_ref, f32[128,256]{1,0:T(8,128)S(1)} %shard_map.68.refs_10_.refs_0_, f32[128,256]{1,0:T(8,128)S(1)} %get-tuple-element.29.refs_1_, ...), custom_call_target="tpu_custom_call" | custom-call | tf_op jit(solution)/shard_map/back/pallas_call | solution.py:436
  (8 shorter events, 0.1 us)
Async XLA Ops:
  1.5 5.2 %collective-permute-start.4 = (f32[64,256]{1,0:T(8,128)S(1)}, f32[64,256]{1,0:T(8,128)S(1)}, u32[]{:S(2)}, u32[]{:S(2)}) collective-permute-start(f32[64,256]{1,0:T(8,128)S(1)} %constant_dynamic-slice_fusion), channel_id=1, source_target_pairs={{0,16},{1,17},{2,18},{3,19},{4,20},{5,21},{6,22},{7,23},{8,24},{9,... | collective-permute-start | bytes 196616 | tf_op jit(solution)/shard_map/ppermute | solution.py:56
  4.5 1.2 %copy-start = (f32[256,1024]{1,0:T(8,128)S(1)}, f32[256,1024]{1,0:T(8,128)}, u32[]{:S(2)}) copy-start(f32[256,1024]{1,0:T(8,128)} %refs_0_.7) | copy-start | bytes 3145732
  5.7 9.1 %copy-start.1 = (f32[256,1024]{1,0:T(8,128)S(1)}, f32[256,1024]{1,0:T(8,128)}, u32[]{:S(2)}) copy-start(f32[256,1024]{1,0:T(8,128)} %refs_0_.7) | copy-start | bytes 3145732
  6.7 5.5 %collective-permute-start.6 = (f32[64,256]{1,0:T(8,128)S(1)}, f32[64,256]{1,0:T(8,128)S(1)}, u32[]{:S(2)}, u32[]{:S(2)}) collective-permute-start(f32[64,256]{1,0:T(8,128)S(1)} %collective-permute-done.4.refs_6_), channel_id=1, source_target_pairs={{0,2},{1,3},{2,0},{3,1},{4,6},{5,7},{6,4},{7,5},{8,10},{9,11},{10,... | collective-permute-start | bytes 196616 | tf_op jit(solution)/shard_map/ppermute | solution.py:56
  8.7 6.0 %collective-permute-start.3 = (f32[256,128]{1,0:T(8,128)S(1)}, f32[256,128]{1,0:T(8,128)S(1)}, u32[]{:S(2)}, u32[]{:S(2)}) collective-permute-start(f32[256,128]{1,0:T(8,128)S(1)} %get-tuple-element.20), channel_id=1, source_target_pairs={{0,16},{1,17},{2,18},{3,19},{4,20},{5,21},{6,22},{7,23},{8,24},{9,... | collective-permute-start | bytes 393224 | tf_op jit(solution)/shard_map/ppermute | solution.py:56
  10.2 2.0 %collective-permute-start.5 = (f32[64,256]{1,0:T(8,128)S(1)}, f32[64,256]{1,0:T(8,128)S(1)}, u32[]{:S(2)}, u32[]{:S(2)}) collective-permute-start(f32[64,256]{1,0:T(8,128)S(1)} %collective-permute-done.4.refs_6_), channel_id=1, source_target_pairs={{0,1},{1,0},{2,3},{3,2},{4,5},{5,4},{6,7},{7,6},{8,9},{9,8},{10,11... | collective-permute-start | bytes 196616 | tf_op jit(solution)/shard_map/ppermute | solution.py:56
  10.3 6.6 %collective-permute-start.2 = (f32[256,128]{1,0:T(8,128)S(1)}, f32[256,128]{1,0:T(8,128)S(1)}, u32[]{:S(2)}, u32[]{:S(2)}) collective-permute-start(f32[256,128]{1,0:T(8,128)S(1)} %get-tuple-element.19), channel_id=1, source_target_pairs={{0,16},{1,17},{2,18},{3,19},{4,20},{5,21},{6,22},{7,23},{8,24},{9,... | collective-permute-start | bytes 393224 | tf_op jit(solution)/shard_map/ppermute | solution.py:56
  10.8 8.9 %collective-permute-start.1 = (f32[256,128]{1,0:T(8,128)S(1)}, f32[256,128]{1,0:T(8,128)S(1)}, u32[]{:S(2)}, u32[]{:S(2)}) collective-permute-start(f32[256,128]{1,0:T(8,128)S(1)} %get-tuple-element.18), channel_id=1, source_target_pairs={{0,16},{1,17},{2,18},{3,19},{4,20},{5,21},{6,22},{7,23},{8,24},{9,... | collective-permute-start | bytes 393224 | tf_op jit(solution)/shard_map/ppermute | solution.py:56
  12.3 2.5 %collective-permute-start.7 = (f32[64,256]{1,0:T(8,128)S(1)}, f32[64,256]{1,0:T(8,128)S(1)}, u32[]{:S(2)}, u32[]{:S(2)}) collective-permute-start(f32[64,256]{1,0:T(8,128)S(1)} %collective-permute-done.6.refs_8_), channel_id=1, source_target_pairs={{0,1},{1,0},{2,3},{3,2},{4,5},{5,4},{6,7},{7,6},{8,9},{9,8},{10,11... | collective-permute-start | bytes 196616 | tf_op jit(solution)/shard_map/ppermute | solution.py:56
  12.3 9.8 %collective-permute-start = (f32[256,128]{1,0:T(8,128)S(1)}, f32[256,128]{1,0:T(8,128)S(1)}, u32[]{:S(2)}, u32[]{:S(2)}) collective-permute-start(f32[256,128]{1,0:T(8,128)S(1)} %get-tuple-element.17), channel_id=1, source_target_pairs={{0,16},{1,17},{2,18},{3,19},{4,20},{5,21},{6,22},{7,23},{8,24},{9,... | collective-permute-start | bytes 393224 | tf_op jit(solution)/shard_map/ppermute | solution.py:56
  13.0 0.9 %copy-start.3 = (f32[256,256]{1,0:T(8,128)S(1)}, f32[256,256]{1,0:T(8,128)}, u32[]{:S(2)}) copy-start(f32[256,256]{1,0:T(8,128)} %test_ref.1) | copy-start | bytes 786436
  14.0 0.8 %copy-start.2 = (f32[2,24,256]{2,1,0:T(8,128)S(1)}, f32[2,24,256]{2,1,0:T(8,128)}, u32[]{:S(2)}) copy-start(f32[2,24,256]{2,1,0:T(8,128)} %constant.24.clone.refs_3_) | copy-start | bytes 147460
  14.0 0.7 %copy-start.5 = (f32[64]{0:T(128)S(1)}, f32[64]{0:T(128)}, u32[]{:S(2)}) copy-start(f32[64]{0:T(128)} %param.6) | copy-start | bytes 772
  14.7 0.7 %copy-start.4 = (s32[1024]{0:T(1024)S(1)}, s32[1024]{0:T(1024)}, u32[]{:S(2)}) copy-start(s32[1024]{0:T(1024)} %param.7) | copy-start | bytes 12292
  23.6 1.3 %collective-permute-start.8 = (f32[136,128]{1,0:T(8,128)S(1)}, f32[136,128]{1,0:T(8,128)S(1)}, u32[]{:S(2)}, u32[]{:S(2)}) collective-permute-start(f32[136,128]{1,0:T(8,128)S(1)} %get-tuple-element.27), channel_id=1, source_target_pairs={{0,1},{1,0},{2,3},{3,2},{4,5},{5,4},{6,7},{7,6},{8,9},{9,8},{10,11... | collective-permute-start | bytes 208904 | tf_op jit(solution)/shard_map/ppermute | solution.py:56
  24.9 5.3 %collective-permute-start.11 = (f32[136,128]{1,0:T(8,128)S(1)}, f32[136,128]{1,0:T(8,128)S(1)}, u32[]{:S(2)}, u32[]{:S(2)}) collective-permute-start(f32[136,128]{1,0:T(8,128)S(1)} %add.30), channel_id=1, source_target_pairs={{0,18},{1,13},{2,16},{3,15},{4,22},{5,9},{6,20},{7,11},{8,26},{9,5... | collective-permute-start | bytes 208904 | tf_op jit(solution)/shard_map/ppermute | solution.py:56
  26.3 4.7 %collective-permute-start.10 = (f32[136,128]{1,0:T(8,128)S(1)}, f32[136,128]{1,0:T(8,128)S(1)}, u32[]{:S(2)}, u32[]{:S(2)}) collective-permute-start(f32[136,128]{1,0:T(8,128)S(1)} %add.30), channel_id=1, source_target_pairs={{0,16},{1,9},{2,18},{3,11},{4,20},{5,13},{6,22},{7,15},{8,24},{9,1... | collective-permute-start | bytes 208904 | tf_op jit(solution)/shard_map/ppermute | solution.py:56
  26.6 4.4 %collective-permute-start.9 = (f32[136,128]{1,0:T(8,128)S(1)}, f32[136,128]{1,0:T(8,128)S(1)}, u32[]{:S(2)}, u32[]{:S(2)}) collective-permute-start(f32[136,128]{1,0:T(8,128)S(1)} %add.30), channel_id=1, source_target_pairs={{0,2},{1,5},{2,0},{3,7},{4,6},{5,1},{6,4},{7,3},{8,10},{9,13},{10,... | collective-permute-start | bytes 208904 | tf_op jit(solution)/shard_map/ppermute | solution.py:56
  31.0 6.3 %collective-permute-start.14 = (f32[136,128]{1,0:T(8,128)S(1)}, f32[136,128]{1,0:T(8,128)S(1)}, u32[]{:S(2)}, u32[]{:S(2)}) collective-permute-start(f32[136,128]{1,0:T(8,128)S(1)} %add_add_fusion.1), channel_id=1, source_target_pairs={{0,12},{1,19},{2,14},{3,17},{4,8},{5,23},{6,10},{7,21},{8,4},{9,27... | collective-permute-start | bytes 208904 | tf_op jit(solution)/shard_map/ppermute | solution.py:56
  35.0 5.2 %collective-permute-start.13 = (f32[136,128]{1,0:T(8,128)S(1)}, f32[136,128]{1,0:T(8,128)S(1)}, u32[]{:S(2)}, u32[]{:S(2)}) collective-permute-start(f32[136,128]{1,0:T(8,128)S(1)} %add_add_fusion.1), channel_id=1, source_target_pairs={{0,8},{1,17},{2,10},{3,19},{4,12},{5,21},{6,14},{7,23},{8,0},{9,25... | collective-permute-start | bytes 208904 | tf_op jit(solution)/shard_map/ppermute | solution.py:56
  35.0 5.2 %collective-permute-start.12 = (f32[136,128]{1,0:T(8,128)S(1)}, f32[136,128]{1,0:T(8,128)S(1)}, u32[]{:S(2)}, u32[]{:S(2)}) collective-permute-start(f32[136,128]{1,0:T(8,128)S(1)} %add_add_fusion.1), channel_id=1, source_target_pairs={{0,4},{1,3},{2,6},{3,1},{4,0},{5,7},{6,2},{7,5},{8,12},{9,11},{10,... | collective-permute-start | bytes 208904 | tf_op jit(solution)/shard_map/ppermute | solution.py:56
  40.2 1.3 %collective-permute-start.15 = (f32[136,128]{1,0:T(8,128)S(1)}, f32[136,128]{1,0:T(8,128)S(1)}, u32[]{:S(2)}, u32[]{:S(2)}) collective-permute-start(f32[136,128]{1,0:T(8,128)S(1)} %add_add_fusion.part_ref), channel_id=1, source_target_pairs={{0,1},{1,0},{2,3},{3,2},{4,5},{5,4},{6,7},{7,6},{8,9},{9,8},{10,11... | collective-permute-start | bytes 208904 | tf_op jit(solution)/shard_map/ppermute | solution.py:56
